TPU v7x, 32 devices: a whole 2x2x4 slice. The times are simulated.
32 devices in a mesh: dp: 4 (over z), seq: 8 (over y, x, core).
Axes of the slice: x: 2, y: 2, z: 4, core: 2. Of those that a mesh axis runs over, the one named last changes fastest.
Arguments:
- layer_input: bfloat16 [2, 4, 2048, 1152], P(None, 'dp', 'seq'), may hold values from -6 to 6
- out_cotangent: bfloat16 [2, 4, 2048, 1152], P(None, 'dp', 'seq'), may hold values from -6 to 6
- seq_lengths: int32 [2, 4, 2], P(None, 'dp'), may hold values from 0 to 2048, as said below
- inputnorm: bfloat16 [1152], P(('dp', 'seq')), may hold values from -0.5 to 0.5
- queryproj: bfloat16 [1152, 1024], P(('dp', 'seq')), may hold values from -0.1875 to 0.1875
- keyproj: bfloat16 [1152, 256], P(('dp', 'seq')), may hold values from -0.1875 to 0.1875
- valueproj: bfloat16 [1152, 256], P(('dp', 'seq')), may hold values from -0.1875 to 0.1875
- querynorm: bfloat16 [256], P(('dp', 'seq')), may hold values from 0.29882812 to 0.69921875
- keynorm: bfloat16 [256], P(('dp', 'seq')), may hold values from 0.29882812 to 0.69921875
- outproj: bfloat16 [1024, 1152], P(('dp', 'seq')), may hold values from -0.1875 to 0.1875
- attnnorm: bfloat16 [1152], P(('dp', 'seq')), may hold values from -0.5 to 0.5
- prefeednorm: bfloat16 [1152], P(('dp', 'seq')), may hold values from -0.5 to 0.5
- gateproj: bfloat16 [1152, 6912], P(('dp', 'seq')), may hold values from -0.1875 to 0.1875
- upproj: bfloat16 [1152, 6912], P(('dp', 'seq')), may hold values from -0.1875 to 0.1875
- downproj: bfloat16 [6912, 1152], P(('dp', 'seq')), may hold values from -0.078125 to 0.078125
- postfeednorm: bfloat16 [1152], P(('dp', 'seq')), may hold values from -0.5 to 0.5
Outputs:
- layer_output: float32 [2, 4, 2048, 1152], P(None, 'dp', 'seq')
- input_grad: float32 [2, 4, 2048, 1152], P(None, 'dp', 'seq')
- inputnorm_grad: float32 [1152], P(('dp', 'seq'))
- queryproj_grad: float32 [1152, 1024], P(('dp', 'seq'))
- keyproj_grad: float32 [1152, 256], P(('dp', 'seq'))
- valueproj_grad: float32 [1152, 256], P(('dp', 'seq'))
- querynorm_grad: float32 [256], P(('dp', 'seq'))
- keynorm_grad: float32 [256], P(('dp', 'seq'))
- outproj_grad: float32 [1024, 1152], P(('dp', 'seq'))
- attnnorm_grad: float32 [1152], P(('dp', 'seq'))
- prefeednorm_grad: float32 [1152], P(('dp', 'seq'))
- gateproj_grad: float32 [1152, 6912], P(('dp', 'seq'))
- upproj_grad: float32 [1152, 6912], P(('dp', 'seq'))
- downproj_grad: float32 [6912, 1152], P(('dp', 'seq'))
- postfeednorm_grad: float32 [1152], P(('dp', 'seq'))
Inputs may be any that keep to these rules, and one draw needn't show every extreme that they name: `seq_lengths`: in each row the nonzero lengths come first, are equal, and are 2048 divided by a power of two no larger than 2, so that they sum to 2048. For each index of dp, one micro-batch drawn from the seed holds a single sequence of 2048 tokens.
All inputs are finite; a program needn't handle non-finite values.
Results may differ from a plain program's by a relative error of at most 0.02.
Values may be sent and summed in bfloat16 or wider, within the bound.
No kernel may reach another device: no remote copies, remote signals or barrier semaphores. Data moves between devices by JAX's collectives and lax.ppermute only.
A program may use at most 576 MiB of HBM per device.

v0:
```python
import math

import jax
import jax.numpy as jnp
from jax import lax
from jax.sharding import PartitionSpec as P

HEADS = 4
HD = 256
FF = 6912
WINDOW = 512
QD = 1024


norm_eps = 1e-06


def from_behind(shard, axis, by):
    peers = lax.axis_size(axis)
    pairs = [(i, i + by) for i in range(peers) if 0 <= i + by < peers]
    return lax.ppermute(shard, axis, pairs)


def rms_scale(values, gain_vec):
    mean_square = jnp.mean(values * values, axis=-1, keepdims=True)
    return values * lax.rsqrt(mean_square + norm_eps) * (1.0 + gain_vec)


def rotate_half(values):
    middle = values.shape[-1] // 2
    return jnp.concatenate([-values[..., middle:], values[..., :middle]], axis=-1)


def rope_tables(relative):
    middle = HD // 2
    counter = jnp.arange(middle, dtype=jnp.float32)
    inverse = jnp.power(jnp.float32(10000.0), -2.0 * counter / HD)
    angles = relative.astype(jnp.float32)[:, None] * inverse[None, :]
    cosine = jnp.cos(angles)
    sine_table = jnp.sin(angles)
    return (jnp.concatenate([cosine, cosine], -1), jnp.concatenate([sine_table, sine_table], -1))


def prepare_heads(values, gain_vec, cosine, sine_table, factor):
    row_count = values.shape[0]
    head_view = values.reshape(row_count, -1, gain_vec.shape[0])
    normed = rms_scale(head_view, gain_vec)
    turned = normed * cosine[:, None, :] + rotate_half(normed) * sine_table[:, None, :]
    return (turned * factor).reshape(row_count, -1)


def gelu_gate(gate_raw, up_raw):
    return jax.nn.gelu(gate_raw, approximate=True) * up_raw


def locate(positions, starts):
    is_after = positions[:, None] >= starts[None, :]
    segment = jnp.sum(is_after.astype(jnp.int32), axis=1)
    first_pos = jnp.max(jnp.where(is_after, starts[None, :], 0), axis=1)
    return (segment, positions - first_pos)


def matmul_low(left_side, right_side):
    return jnp.dot(left_side, right_side, preferred_element_type=jnp.float32)


def token_product(left_cols, right_side):
    return lax.dot_general(
        left_cols, right_side, (((0,), (0,)), ((), ())), preferred_element_type=jnp.float32
    )


def wide_terms(kept):
    cols_in = kept[0]
    cols_ffn = kept[1]
    return jnp.concatenate(
        [
            token_product(cols_in, kept[4]),
            token_product(cols_in, kept[5]),
            token_product(cols_in, kept[6]),
            token_product(cols_ffn, kept[7]),
            token_product(cols_ffn, kept[8]),
        ],
        axis=1,
    )


def single_terms(left_side, right_side):
    return token_product(left_side, right_side)


def to_heads(values):
    row_count = values.shape[0]
    return values.reshape(row_count, HEADS, HD).transpose(1, 0, 2).reshape(HEADS * row_count, HD)


def from_heads(values):
    row_count = values.shape[0] // HEADS
    return values.reshape(HEADS, row_count, HD).transpose(1, 0, 2).reshape(row_count, HEADS * HD)


def shards(
    layer_input,
    out_cotangent,
    seq_lengths,
    inputnorm,
    queryproj,
    keyproj,
    valueproj,
    querynorm,
    keynorm,
    outproj,
    attnnorm,
    prefeednorm,
    gateproj,
    upproj,
    downproj,
    postfeednorm,
):
    token_rows = layer_input.shape[2]
    micro_count = layer_input.shape[0]
    reach_devs = WINDOW // token_rows
    base_pos = lax.axis_index("seq") * token_rows
    query_pos = base_pos + jnp.arange(token_rows, dtype=jnp.int32)
    keys_pos = (
        base_pos
        - reach_devs * token_rows
        + jnp.arange((reach_devs + 1) * token_rows, dtype=jnp.int32)
    )
    outputs_list = []
    input_grads = []
    gain_running = None
    kept_all = []
    for micro_idx in range(micro_count):
        gathered = (
            lax.all_gather(inputnorm, ("dp", "seq"), axis=0, tiled=True),
            lax.all_gather(queryproj, ("dp", "seq"), axis=0, tiled=True),
            lax.all_gather(keyproj, ("dp", "seq"), axis=0, tiled=True),
            lax.all_gather(valueproj, ("dp", "seq"), axis=0, tiled=True),
            lax.all_gather(querynorm, ("dp", "seq"), axis=0, tiled=True),
            lax.all_gather(keynorm, ("dp", "seq"), axis=0, tiled=True),
            lax.all_gather(outproj, ("dp", "seq"), axis=0, tiled=True),
            lax.all_gather(attnnorm, ("dp", "seq"), axis=0, tiled=True),
            lax.all_gather(prefeednorm, ("dp", "seq"), axis=0, tiled=True),
            lax.all_gather(gateproj, ("dp", "seq"), axis=0, tiled=True),
            lax.all_gather(upproj, ("dp", "seq"), axis=0, tiled=True),
            lax.all_gather(downproj, ("dp", "seq"), axis=0, tiled=True),
            lax.all_gather(postfeednorm, ("dp", "seq"), axis=0, tiled=True),
        )
        gain_input = gathered[0].astype(jnp.float32)
        gain_query = gathered[4].astype(jnp.float32)
        gain_keys = gathered[5].astype(jnp.float32)
        gain_attn = gathered[7].astype(jnp.float32)
        gain_prefeed = gathered[8].astype(jnp.float32)
        gain_postfeed = gathered[12].astype(jnp.float32)
        batch_input = layer_input[micro_idx, 0].astype(jnp.float32)
        batch_cot = out_cotangent[micro_idx, 0].astype(jnp.float32)
        lengths_row = seq_lengths[micro_idx, 0]
        starts = jnp.cumsum(lengths_row) - lengths_row
        query_seg, relative = locate(query_pos, starts)
        keys_seg, keys_rel = locate(keys_pos, starts)
        allowed = (keys_seg[None, :] == query_seg[:, None]) & (keys_pos[None, :] >= 0)
        allowed = (
            allowed
            & (keys_pos[None, :] <= query_pos[:, None])
            & (query_pos[:, None] - keys_pos[None, :] < WINDOW)
        )
        mask_rows = jnp.tile(allowed, (HEADS, 1))
        cosine, sine_table = rope_tables(relative)
        normed32, back_input = jax.vjp(rms_scale, batch_input, gain_input)
        normed_in = normed32.astype(jnp.bfloat16)
        query_raw = matmul_low(normed_in, gathered[1])
        keys_raw = matmul_low(normed_in, gathered[2])
        value_low = matmul_low(normed_in, gathered[3]).astype(jnp.bfloat16)
        query_prep, back_query = jax.vjp(
            lambda raw_in, gain_vec: prepare_heads(
                raw_in, gain_vec, cosine, sine_table, 1.0 / math.sqrt(HD)
            ),
            query_raw,
            gain_query,
        )
        keys_prep, back_keys = jax.vjp(
            lambda raw_in, gain_vec: prepare_heads(raw_in, gain_vec, cosine, sine_table, 1.0),
            keys_raw,
            gain_keys,
        )
        query_low = query_prep.astype(jnp.bfloat16)
        keys_low = keys_prep.astype(jnp.bfloat16)
        own_pair = jnp.concatenate([keys_low, value_low], axis=1)
        arrived = [from_behind(own_pair, "seq", distance) for distance in range(reach_devs, 0, -1)]
        pairs = jnp.concatenate(arrived + [own_pair], axis=0)
        keys_all = pairs[:, :HD]
        values_all = pairs[:, HD:]
        query_heads = to_heads(query_low)
        scores = matmul_low(query_heads, keys_all.T)
        masked = jnp.where(mask_rows, scores, -1e30)
        row_max = jnp.max(masked, axis=-1, keepdims=True)
        log_total = row_max + jnp.log(jnp.sum(jnp.exp(masked - row_max), axis=-1, keepdims=True))
        attn_probs = jnp.exp(masked - log_total).astype(jnp.bfloat16)
        attended = from_heads(matmul_low(attn_probs, values_all)).astype(jnp.bfloat16)
        attn_out = matmul_low(attended, gathered[6])
        post_attn, back_attn = jax.vjp(rms_scale, attn_out, gain_attn)
        hidden_one = batch_input + post_attn
        normed_ffn32, back_prefeed = jax.vjp(rms_scale, hidden_one, gain_prefeed)
        normed_ffn = normed_ffn32.astype(jnp.bfloat16)
        gate_raw = matmul_low(normed_ffn, gathered[9])
        up_raw = matmul_low(normed_ffn, gathered[10])
        activated32, back_gated = jax.vjp(gelu_gate, gate_raw, up_raw)
        activated = activated32.astype(jnp.bfloat16)
        ffn_out = matmul_low(activated, gathered[11])
        post_ffn, back_postfeed = jax.vjp(rms_scale, ffn_out, gain_postfeed)
        outputs_list.append(hidden_one + post_ffn)
        back_weights = (
            lax.all_gather(inputnorm, ("dp", "seq"), axis=0, tiled=True),
            lax.all_gather(queryproj, ("dp", "seq"), axis=0, tiled=True),
            lax.all_gather(keyproj, ("dp", "seq"), axis=0, tiled=True),
            lax.all_gather(valueproj, ("dp", "seq"), axis=0, tiled=True),
            lax.all_gather(querynorm, ("dp", "seq"), axis=0, tiled=True),
            lax.all_gather(keynorm, ("dp", "seq"), axis=0, tiled=True),
            lax.all_gather(outproj, ("dp", "seq"), axis=0, tiled=True),
            lax.all_gather(attnnorm, ("dp", "seq"), axis=0, tiled=True),
            lax.all_gather(prefeednorm, ("dp", "seq"), axis=0, tiled=True),
            lax.all_gather(gateproj, ("dp", "seq"), axis=0, tiled=True),
            lax.all_gather(upproj, ("dp", "seq"), axis=0, tiled=True),
            lax.all_gather(downproj, ("dp", "seq"), axis=0, tiled=True),
            lax.all_gather(postfeednorm, ("dp", "seq"), axis=0, tiled=True),
        )
        grad_ffn, grad_postfeed = back_postfeed(batch_cot)
        grad_ffn_low = grad_ffn.astype(jnp.bfloat16)
        grad_activ = matmul_low(grad_ffn_low, back_weights[11].T)
        grad_gate, grad_up = back_gated(grad_activ)
        gate_low = grad_gate.astype(jnp.bfloat16)
        up_low = grad_up.astype(jnp.bfloat16)
        grad_normed_ffn = matmul_low(gate_low, back_weights[9].T) + matmul_low(
            up_low, back_weights[10].T
        )
        grad_hidden_part, grad_prefeed = back_prefeed(grad_normed_ffn)
        grad_hidden = batch_cot + grad_hidden_part
        grad_attn_out, grad_attn = back_attn(grad_hidden)
        attn_low = grad_attn_out.astype(jnp.bfloat16)
        grad_attended = matmul_low(attn_low, back_weights[6].T).astype(jnp.bfloat16)
        grad_heads = to_heads(grad_attended)
        scores_again = matmul_low(query_heads, keys_all.T)
        masked_again = jnp.where(mask_rows, scores_again, -1e30)
        probs_again = jnp.exp(masked_again - log_total)
        grad_probs = matmul_low(grad_heads, values_all.T)
        inner_sum = jnp.sum(probs_again * grad_probs, axis=-1, keepdims=True)
        grad_scores = (probs_again * (grad_probs - inner_sum)).astype(jnp.bfloat16)
        grad_query_heads = matmul_low(grad_scores, keys_all)
        grad_keys_all = matmul_low(grad_scores.T, query_heads)
        grad_values_all = matmul_low(probs_again.astype(jnp.bfloat16).T, grad_heads)
        grad_pairs = jnp.concatenate([grad_keys_all, grad_values_all], axis=1)
        own_grad = grad_pairs[reach_devs * token_rows :]
        for distance in range(1, reach_devs + 1):
            offset = (reach_devs - distance) * token_rows
            own_grad = own_grad + from_behind(
                grad_pairs[offset : offset + token_rows].astype(jnp.bfloat16), "seq", -distance
            ).astype(jnp.float32)
        grad_keys_prep = own_grad[:, :HD]
        grad_value_low = own_grad[:, HD:].astype(jnp.bfloat16)
        grad_query_raw, grad_querynorm = back_query(from_heads(grad_query_heads))
        grad_keys_raw, grad_keynorm = back_keys(grad_keys_prep)
        query_grad_low = grad_query_raw.astype(jnp.bfloat16)
        keys_grad_low = grad_keys_raw.astype(jnp.bfloat16)
        grad_normed_in = (
            matmul_low(query_grad_low, back_weights[1].T)
            + matmul_low(keys_grad_low, back_weights[2].T)
            + matmul_low(grad_value_low, back_weights[3].T)
        )
        grad_input_part, grad_inputnorm = back_input(grad_normed_in)
        input_grads.append(grad_hidden + grad_input_part)
        gain_terms = (
            grad_inputnorm,
            grad_querynorm,
            grad_keynorm,
            grad_attn,
            grad_prefeed,
            grad_postfeed,
        )
        kept_now = (
            normed_in,
            normed_ffn,
            activated,
            attended,
            query_grad_low,
            keys_grad_low,
            grad_value_low,
            gate_low,
            up_low,
            grad_ffn_low,
            attn_low,
        )
        kept_all.append(kept_now)
        gain_running = (
            gain_terms if gain_running is None else jax.tree.map(jnp.add, gain_running, gain_terms)
        )
    joined = tuple(
        (jnp.concatenate([kept[index] for kept in kept_all], axis=0) for index in range(11))
    )
    gain_final = (
        lax.psum_scatter(gain_running[0], ("dp", "seq"), scatter_dimension=0, tiled=True),
        lax.psum_scatter(gain_running[1], ("dp", "seq"), scatter_dimension=0, tiled=True),
        lax.psum_scatter(gain_running[2], ("dp", "seq"), scatter_dimension=0, tiled=True),
        lax.psum_scatter(gain_running[3], ("dp", "seq"), scatter_dimension=0, tiled=True),
        lax.psum_scatter(gain_running[4], ("dp", "seq"), scatter_dimension=0, tiled=True),
        lax.psum_scatter(gain_running[5], ("dp", "seq"), scatter_dimension=0, tiled=True),
    )
    wide_final = lax.psum_scatter(
        wide_terms(joined), ("dp", "seq"), scatter_dimension=0, tiled=True
    )
    down_final = lax.psum_scatter(
        single_terms(joined[2], joined[9]), ("dp", "seq"), scatter_dimension=0, tiled=True
    )
    out_final = lax.psum_scatter(
        single_terms(joined[3], joined[10]), ("dp", "seq"), scatter_dimension=0, tiled=True
    )
    grad_queryproj = wide_final[:, :QD]
    grad_keyproj = wide_final[:, QD : QD + HD]
    grad_valueproj = wide_final[:, QD + HD : QD + 2 * HD]
    grad_gateproj = wide_final[:, QD + 2 * HD : QD + 2 * HD + FF]
    grad_upproj = wide_final[:, QD + 2 * HD + FF :]
    layer_out = jnp.stack(outputs_list)[:, None]
    input_out = jnp.stack(input_grads)[:, None]
    return (
        layer_out,
        input_out,
        gain_final[0],
        grad_queryproj,
        grad_keyproj,
        grad_valueproj,
        gain_final[1],
        gain_final[2],
        out_final,
        gain_final[3],
        gain_final[4],
        grad_gateproj,
        grad_upproj,
        down_final,
        gain_final[5],
    )


def solution(mesh):
    in_specs = (
        P(None, "dp", "seq", None),
        P(None, "dp", "seq", None),
        P(None, "dp", None),
        P(("dp", "seq")),
        P(("dp", "seq"), None),
        P(("dp", "seq"), None),
        P(("dp", "seq"), None),
        P(("dp", "seq")),
        P(("dp", "seq")),
        P(("dp", "seq"), None),
        P(("dp", "seq")),
        P(("dp", "seq")),
        P(("dp", "seq"), None),
        P(("dp", "seq"), None),
        P(("dp", "seq"), None),
        P(("dp", "seq")),
    )
    out_specs = (
        P(None, "dp", "seq", None),
        P(None, "dp", "seq", None),
        P(("dp", "seq")),
        P(("dp", "seq"), None),
        P(("dp", "seq"), None),
        P(("dp", "seq"), None),
        P(("dp", "seq")),
        P(("dp", "seq")),
        P(("dp", "seq"), None),
        P(("dp", "seq")),
        P(("dp", "seq")),
        P(("dp", "seq"), None),
        P(("dp", "seq"), None),
        P(("dp", "seq"), None),
        P(("dp", "seq")),
    )
    return jax.shard_map(shards, mesh=mesh, in_specs=in_specs, out_specs=out_specs, check_vma=False)
```

profile of v0, /device:TPU:0, one launch (start us, length us, event | category | flops | bytes accessed | tf_op | source)
XLA Modules:
  0.0 2151.1 jit_solution(13161520263586064756)
XLA Ops:
  11.7 45.7 %all-gather.1 = bf16[32,36,256]{2,1,0:T(8,128)(2,1)S(1)} all-gather(bf16[1,36,256]{2,1,0:T(8,128)(2,1)} %bitcast.323), channel_id=1, replica_groups=mesh['dp'=4,'seq'=8] {'dp','seq'}, dimensions={0}, use_global_device_ids=true | all-gather | bytes 608256 | tf_op jit(solution)/shard_map/all_gather | solution.py:138
  57.5 38.8 %all-gather.2 = bf16[32,36,256]{2,1,0:T(8,128)(2,1)S(1)} all-gather(bf16[1,36,256]{2,1,0:T(8,128)(2,1)S(1)} %bitcast.324), channel_id=1, replica_groups=mesh['dp'=4,'seq'=8] {'dp','seq'}, dimensions={0}, use_global_device_ids=true | all-gather | bytes 608256 | tf_op jit(solution)/shard_map/all_gather | solution.py:139
  97.9 38.2 %all-reduce.23 = (bf16[1152]{0:T(1024)(128)(2,1)S(1)}, bf16[256]{0:T(256)(128)(2,1)S(1)}, bf16[256]{0:T(256)(128)(2,1)S(1)}, bf16[1152]{0:T(1024)(128)(2,1)S(1)}...) all-reduce(bf16[1152]{0:T(1024)(128)(2,1)S(1)} %dynamic-update-slic, ...), channel_id=1, replica_groups=mesh['dp'=4,'seq'=8] {'dp','seq'}, use_global_device_ids=true, to_apply=%add.8 | all-reduce | flops 5120 | bytes 20480
  193.7 60.2 %all-gather.17.cloned.1.call-done = bf16[32,36,6912]{2,1,0:T(8,128)(2,1)} async-done(((bf16[1,36,6912]{2,1,0:T(8,128)(2,1)}), bf16[32,36,6912]{2,1,0:T(8,128)(2,1)}) %all-gather.17.cloned.1.call-update) | async-done | bytes 15925264 | tf_op jit(solution)/shard_map/all_gather | solution.py:145
  253.9 18.5 reshape.772
  272.4 101.8 %all-gather.19.cloned.1.call-done = bf16[32,36,6912]{2,1,0:T(8,128)(2,1)} async-done(((bf16[1,36,6912]{2,1,0:T(8,128)(2,1)}), bf16[32,36,6912]{2,1,0:T(8,128)(2,1)}) %all-gather.19.cloned.1.call-update) | async-done | bytes 15925264 | tf_op jit(solution)/shard_map/all_gather | solution.py:146
  374.1 18.4 reshape.774
  392.6 12.5 fusion.190
  405.1 12.6 fusion.191
  428.4 57.7 %all-gather.13.cloned.1.call-done = bf16[6912,1152]{1,0:T(8,128)(2,1)} async-done(((bf16[216,1152]{1,0:T(8,128)(2,1)}), bf16[6912,1152]{1,0:T(8,128)(2,1)}) %all-gather.13.cloned.1.call-update) | async-done | bytes 15925264 | tf_op jit(solution)/shard_map/all_gather | solution.py:147
  486.1 11.2 multiply_reduce_fusion.10
  497.4 15.3 multiply_convert_fusion.3
  523.4 16.5 multiply_convert_fusion.1
  539.9 12.4 fusion.192
  552.3 16.0 multiply_convert_fusion
  578.7 12.4 convolution_add_fusion.4
  591.1 13.9 multiply_reduce_fusion.3
  662.7 17.0 convolution_dynamic-update-slice_fusion.1
  679.7 15.8 convolution_dynamic-update-slice_fusion
  702.3 18.9 fusion.20
  735.5 42.1 %all-reduce.22 = (f32[1152]{0:T(1024)}, f32[256]{0:T(256)}, f32[256]{0:T(256)}, f32[1152]{0:T(1024)}, f32[1152]{0:T(1024)}, /*index=5*/f32[1152]{0:T(1024)}) all-reduce(f32[1152]{0:T(1024)} %add.380, f32[256]{0:T(256)} %add.381, f32[256]{0:T(256)} %add.382, f32[1152]{0:T(1024)} %add.383, ...), channel_id=2, replica_groups=mesh['dp'=4,'seq'=8] {'dp','seq'}, use_global_device_ids=true, to_apply=%region_40.41.clone | all-reduce | flops 5120 | bytes 40960
  790.3 921.1 %all-reduce.26.cloned.1.call-done = f32[1152,15360]{1,0:T(8,128)} async-done(((f32[1152,15360]{1,0:T(8,128)}), f32[1152,15360]{1,0:T(8,128)}) %all-reduce.26.cloned.1.call-update) | async-done | bytes 70778896
  1718.4 105.9 %reduce-scatter.5.cloned.1.call-done = f32[32,1152]{1,0:T(8,128)} async-done(((f32[1024,1152]{1,0:T(8,128)}), f32[32,1152]{1,0:T(8,128)}) %reduce-scatter.5.cloned.1.call-update) | async-done | bytes 147472 | tf_op jit(solution)/shard_map/reduce_scatter | solution.py:314
  1824.2 319.8 %reduce-scatter.7.cloned.1.call-done = f32[216,1152]{1,0:T(8,128)} async-done(((f32[6912,1152]{1,0:T(8,128)}), f32[216,1152]{1,0:T(8,128)}) %reduce-scatter.7.cloned.1.call-update) | async-done | bytes 995344
  (528 shorter events, 192.0 us)
Async XLA Ops:
  7.2 158.5 %all-gather.15.cloned.1.call-start = ((), (), s32[]{:S(2)}) async-start(), calls=%async_computation.5 | async-start | bytes 2703360 | tf_op jit(solution)/shard_map/all_gather | solution.py:137
  7.9 179.8 %all-gather.11.cloned.1.call-start = ((), (), s32[]{:S(2)}) async-start(), calls=%async_computation.2 | async-start | bytes 2433024 | tf_op jit(solution)/shard_map/all_gather | solution.py:142
  8.7 245.2 %all-gather.17.cloned.1.call-start = ((), (), s32[]{:S(2)}) async-start(), calls=%async_computation.6 | async-start | bytes 18247680 | tf_op jit(solution)/shard_map/all_gather | solution.py:145
  9.4 364.7 %all-gather.19.cloned.1.call-start = ((), (), s32[]{:S(2)}) async-start(), calls=%async_computation.7 | async-start | bytes 18247680 | tf_op jit(solution)/shard_map/all_gather | solution.py:146
  9.5 87.5 %copy-start.149 = (bf16[36]{0:T(256)(128)(2,1)S(1)}, bf16[36]{0:T(256)(128)(2,1)}, u32[]{:S(2)}) copy-start(bf16[36]{0:T(256)(128)(2,1)} %param.27) | copy-start | bytes 220
  9.5 87.7 %copy-start.150 = (bf16[36]{0:T(256)(128)(2,1)S(1)}, bf16[36]{0:T(256)(128)(2,1)}, u32[]{:S(2)}) copy-start(bf16[36]{0:T(256)(128)(2,1)} %param.26) | copy-start | bytes 220
  9.5 87.9 %copy-start.151 = (bf16[36]{0:T(256)(128)(2,1)S(1)}, bf16[36]{0:T(256)(128)(2,1)}, u32[]{:S(2)}) copy-start(bf16[36]{0:T(256)(128)(2,1)} %param.19) | copy-start | bytes 220
  9.5 88.2 %copy-start.152 = (bf16[36]{0:T(256)(128)(2,1)S(1)}, bf16[36]{0:T(256)(128)(2,1)}, u32[]{:S(2)}) copy-start(bf16[36]{0:T(256)(128)(2,1)} %param.31) | copy-start | bytes 220
  9.5 126.6 %copy-start.144 = (s32[2,1,2]{2,1,0:T(1,128)S(1)}, s32[2,1,2]{2,1,0:T(1,128)}, u32[]{:S(2)}) copy-start(s32[2,1,2]{2,1,0:T(1,128)} %param.18) | copy-start | bytes 52
  9.5 126.7 %copy-start.10 = (bf16[2,1,256,1152]{3,2,1,0:T(8,128)(2,1)S(1)}, bf16[2,1,256,1152]{3,2,1,0:T(8,128)(2,1)}, u32[]{:S(2)}) copy-start(bf16[2,1,256,1152]{3,2,1,0:T(8,128)(2,1)} %param.16) | copy-start | bytes 3538948
  10.0 476.1 %all-gather.13.cloned.1.call-start = ((), (), s32[]{:S(2)}) async-start(), calls=%async_computation.3 | async-start | bytes 16422912 | tf_op jit(solution)/shard_map/all_gather | solution.py:147
  10.6 1700.8 %all-reduce.26.cloned.1.call-start = ((), (), s32[]{:S(2)}) async-start(), calls=%async_computation.8 | async-start | bytes 141557760
  142.2 20.5 collective-permute-start.3
  143.5 19.2 collective-permute-start.2
  149.8 13.8 collective-permute-start.1
  153.7 9.9 collective-permute-start
  193.7 224.0 %copy-start.42 = (bf16[256,1152]{1,0:T(8,128)(2,1)}, bf16[256,1152]{1,0:T(8,128)(2,1)S(1)}, u32[]{:S(2)}) copy-start(bf16[256,1152]{1,0:T(8,128)(2,1)S(1)} %get-tuple-element.195) | copy-start | bytes 1769476
  193.7 303.6 %copy-start.40 = (bf16[256,1152]{1,0:T(8,128)(2,1)}, bf16[256,1152]{1,0:T(8,128)(2,1)S(1)}, u32[]{:S(2)}) copy-start(bf16[256,1152]{1,0:T(8,128)(2,1)S(1)} %get-tuple-element.194) | copy-start | bytes 1769476
  626.6 9.5 collective-permute-start.6
  627.9 12.8 collective-permute-start.7
  633.3 8.6 collective-permute-start.4
  634.6 14.4 collective-permute-start.5
  695.5 1128.7 %reduce-scatter.5.cloned.1.call-start = ((), (), s32[]{:S(2)}) async-start(), calls=%async_computation.4 | async-start | bytes 4866048 | tf_op jit(solution)/shard_map/reduce_scatter | solution.py:314
  700.7 1443.3 %reduce-scatter.7.cloned.1.call-start = ((), (), s32[]{:S(2)}) async-start(), calls=%async_computation.9 | async-start | bytes 32845824
  (153 other events, 1324.7 us)
Sparse Core Ops, SparseCore 0:
  10.9 61.8 all-gather.14
  75.7 56.3 all-gather.10
  135.0 118.9 all-gather.16
  256.7 117.4 all-gather.18
  376.9 109.1 all-gather.12
  695.6 1015.6 all-reduce.25
  1717.4 106.7 reduce-scatter.4
  1832.4 311.6 reduce-scatter.6
where the time goes:
time: 2160 us; the launch traced here: 2150 us
  waiting for transfers between devices  1580 us (73%)
  matrix products  241 us (11%)
  blocking collectives  165 us (8%)
  local copies, waits for them, and re-layouts  87.5 us (4%)
  other arithmetic  41.9 us (2%)
    unnamed x10, waiting for transfers between devices  1240 us
    dot_general x40, matrix products, matmul_low(): return jnp.dot(left_side, right_side, preferred_element_type=jnp.float32)  178 us
    reduce_scatter x1, waiting for transfers between devices, shards(): lax.psum_scatter(single_terms(joined[3], joined[10]), ('dp', 'seq'), scat...  106 us
    all_gather x1, waiting for transfers between devices, shards(): lax.all_gather(upproj, ('dp', 'seq'), axis=0, tiled=True)  102 us
    unnamed x2, blocking collectives  80.2 us
    unnamed x347, local copies, waits for them, and re-layouts  70 us
    dot_general x7, matrix products, token_product(): lax.dot_general(left_cols, right_side, (((0,), (0,)), ((), ())), preferre...  62.2 us
    all_gather x1, waiting for transfers between devices, shards(): lax.all_gather(gateproj, ('dp', 'seq'), axis=0, tiled=True)  60.2 us
  transfers between devices with their start and end apart: 16, of which 8 were waited for; matrix products, arithmetic and copies ran while one was open for 8% of the time, Pallas kernels for 0%

commit v1 on v0

v1 whole, which is shorter than its diff:
```python
import math

import jax
import jax.numpy as jnp
from jax import lax
from jax.sharding import PartitionSpec as P

HEADS = 4
HD = 256
WINDOW = 512
EPS = 1e-06
LANES = 128

BF = jnp.bfloat16
F32 = jnp.float32
BOTH = ("dp", "seq")


def dot(left, right, dims=((1,), (0,))):
    return lax.dot_general(left, right, (dims, ((), ())), preferred_element_type=F32)


NT = ((1,), (1,))
TN = ((0,), (0,))


def rms(values, gain):
    scale = lax.rsqrt(jnp.mean(values * values, axis=-1, keepdims=True) + EPS)
    return values * scale * (1.0 + gain), scale


def rms_back(grad, values, scale, gain):
    normed = values * scale
    inner = grad * (1.0 + gain)
    back = scale * (inner - normed * jnp.mean(inner * normed, axis=-1, keepdims=True))
    return back, grad * normed


def rotate(values):
    middle = values.shape[-1] // 2
    return jnp.concatenate([-values[..., middle:], values[..., :middle]], axis=-1)


def rotate_back(values):
    middle = values.shape[-1] // 2
    return jnp.concatenate([values[..., middle:], -values[..., :middle]], axis=-1)


def xor_permute(value, bit, size):
    return lax.ppermute(value, "seq", [(i, i ^ bit) for i in range(size)])


def from_behind(value, by, size):
    pairs = [(i, i + by) for i in range(size) if 0 <= i + by < size]
    return lax.ppermute(value, "seq", pairs)


def gather_tokens(own, size):
    if size != 8:
        return lax.all_gather(own, "seq", axis=0, tiled=True)
    near = [xor_permute(own, bit, size) for bit in (2, 4, 6)]
    mine = jnp.concatenate([own] + near, axis=0)
    other = xor_permute(mine, 1, size)
    return jnp.concatenate([mine, other], axis=0)


def scatter_tokens(parts, size):
    if size != 8:
        return lax.psum_scatter(parts.astype(BF), "seq", scatter_dimension=0, tiled=True).astype(F32)
    half = parts.shape[0] // 2
    rows = half // 4
    got = xor_permute(parts[half:].astype(BF), 1, size)
    mine = parts[:half] + got.astype(F32)
    total = mine[:rows]
    for index, bit in enumerate((2, 4, 6), 1):
        block = mine[index * rows : (index + 1) * rows].astype(BF)
        total = total + xor_permute(block, bit, size).astype(F32)
    return total


def shards(
    dp,
    seq,
    layer_input,
    out_cotangent,
    seq_lengths,
    inputnorm,
    queryproj,
    keyproj,
    valueproj,
    querynorm,
    keynorm,
    outproj,
    attnnorm,
    prefeednorm,
    gateproj,
    upproj,
    downproj,
    postfeednorm,
):
    micro, _, rows, width = layer_input.shape
    devices = dp * seq
    wrows = width // devices
    qd = queryproj.shape[1]
    ff = gateproj.shape[1]
    chunk = ff // devices
    own_ff = dp * chunk
    pad_ff = -(-own_ff // LANES) * LANES
    reach = WINDOW // rows
    keys_rows = (reach + 1) * rows

    short = querynorm.shape[0]
    gains = jnp.stack(
        [
            inputnorm,
            attnnorm,
            prefeednorm,
            postfeednorm,
            jnp.pad(querynorm, (0, wrows - short)),
            jnp.pad(keynorm, (0, wrows - short)),
        ],
        axis=1,
    )
    packed = jnp.concatenate(
        [queryproj, keyproj, valueproj, jnp.pad(gains, ((0, 0), (0, LANES - 6)))], axis=1
    )
    gathered = lax.all_gather(packed, BOTH, axis=0, tiled=True)
    w_in = gathered[:, : qd + 2 * HD]
    gain_rows = gathered[:, qd + 2 * HD :].astype(F32).T
    g_in, g_attn, g_pre, g_post = (gain_rows[i] for i in range(4))
    g_query = gain_rows[4].reshape(devices, wrows)[:, :short].reshape(HD)
    g_keys = gain_rows[5].reshape(devices, wrows)[:, :short].reshape(HD)
    w_out = lax.all_gather(outproj, BOTH, axis=0, tiled=True)

    def by_owner(shard):
        cut = shard.reshape(wrows, dp, seq, chunk).transpose(2, 0, 1, 3).reshape(seq, wrows, own_ff)
        return jnp.pad(cut, ((0, 0), (0, 0), (0, pad_ff - own_ff)))

    gate_up = jnp.concatenate([by_owner(gateproj), by_owner(upproj)], axis=2)
    gate_up = lax.all_to_all(gate_up, "seq", 0, 0)
    w_gu = lax.all_gather(gate_up.reshape(seq * wrows, 2 * pad_ff), "dp", axis=0, tiled=True)
    w_gate = w_gu[:, :pad_ff]
    w_up = w_gu[:, pad_ff:]
    w_down = lax.all_gather(downproj, "dp", axis=0, tiled=True)
    w_down = jnp.pad(w_down, ((0, pad_ff - own_ff), (0, 0)))

    base = lax.axis_index("seq") * rows
    query_pos = base + jnp.arange(rows, dtype=jnp.int32)
    keys_pos = base - reach * rows + jnp.arange(keys_rows, dtype=jnp.int32)
    counter = jnp.arange(HD // 2, dtype=F32)
    inverse = jnp.power(F32(10000.0), -2.0 * counter / HD)

    def heads_forward(raw, gain, cosine, sine, factor):
        view = raw.reshape(raw.shape[0], -1, HD)
        normed, scale = rms(view, gain)
        turned = normed * cosine[:, None, :] + rotate(normed) * sine[:, None, :]
        return (turned * factor).reshape(raw.shape).astype(BF), scale

    def heads_backward(grad, raw, scale, gain, cosine, sine, factor):
        view = raw.reshape(raw.shape[0], -1, HD)
        grad = grad.reshape(view.shape) * factor
        grad = grad * cosine[:, None, :] + rotate_back(grad * sine[:, None, :])
        back, terms = rms_back(grad, view, scale, gain)
        return back.reshape(raw.shape).astype(BF), jnp.sum(terms, axis=(0, 1))

    def to_heads(values):
        return values.reshape(rows, HEADS, HD).transpose(1, 0, 2).reshape(HEADS * rows, HD)

    def from_heads(values):
        return values.reshape(HEADS, rows, HD).transpose(1, 0, 2).reshape(rows, HEADS * HD)

    states = []
    for index in range(micro):
        length = seq_lengths[index, 0, 0]
        relative = query_pos & (length - 1)
        same = (keys_pos & -length)[None, :] == (query_pos & -length)[:, None]
        behind = query_pos[:, None] - keys_pos[None, :]
        allowed = same & (behind >= 0) & (behind < WINDOW)
        mask = jnp.tile(allowed, (HEADS, 1))
        angles = relative.astype(F32)[:, None] * inverse[None, :]
        cosine = jnp.concatenate([jnp.cos(angles)] * 2, -1)
        sine = jnp.concatenate([jnp.sin(angles)] * 2, -1)
        value_in = layer_input[index, 0].astype(F32)
        normed32, scale_in = rms(value_in, g_in)
        normed_in = normed32.astype(BF)
        raw = dot(normed_in, w_in)
        raw_q = raw[:, :qd]
        raw_k = raw[:, qd : qd + HD]
        value_low = raw[:, qd + HD :].astype(BF)
        query_low, scale_q = heads_forward(raw_q, g_query, cosine, sine, 1.0 / math.sqrt(HD))
        keys_low, scale_k = heads_forward(raw_k, g_keys, cosine, sine, 1.0)
        pair = jnp.concatenate([keys_low, value_low], axis=1)
        arrived = [from_behind(pair, by, seq) for by in range(reach, 0, -1)]
        pairs = jnp.concatenate(arrived + [pair], axis=0)
        keys_all = pairs[:, :HD]
        values_all = pairs[:, HD:]
        query_heads = to_heads(query_low)
        scores = jnp.where(mask, dot(query_heads, keys_all, NT), -1e30)
        top = jnp.max(scores, axis=-1, keepdims=True)
        lse = top + jnp.log(jnp.sum(jnp.exp(scores - top), axis=-1, keepdims=True))
        probs = jnp.exp(scores - lse).astype(BF)
        attended = from_heads(dot(probs, values_all)).astype(BF)
        attn_out = dot(attended, w_out)
        post_attn, scale_attn = rms(attn_out, g_attn)
        hidden = value_in + post_attn
        normed_ffn, scale_pre = rms(hidden, g_pre)
        states.append(
            dict(
                mask=mask, cosine=cosine, sine=sine, value_in=value_in, scale_in=scale_in, normed_in=normed_in,
                raw_q=raw_q, raw_k=raw_k, scale_q=scale_q, scale_k=scale_k, keys_all=keys_all, values_all=values_all,
                query_heads=query_heads, lse=lse, attended=attended, attn_out=attn_out, scale_attn=scale_attn,
                hidden=hidden, scale_pre=scale_pre, normed_ffn=normed_ffn.astype(BF),
            )
        )

    outputs = []
    for index in range(micro):
        s = states[index]
        s["tokens"] = gather_tokens(s["normed_ffn"], seq)
        s["gate"] = dot(s["tokens"], w_gate)
        s["up"] = dot(s["tokens"], w_up)
        s["act"] = (jax.nn.gelu(s["gate"], approximate=True) * s["up"]).astype(BF)
        ffn_out = scatter_tokens(dot(s["act"], w_down), seq)
        post, scale_post = rms(ffn_out, g_post)
        outputs.append(s["hidden"] + post)
        s["dy"] = out_cotangent[index, 0].astype(F32)
        d_ffn, s["t_post"] = rms_back(s["dy"], ffn_out, scale_post, g_post)
        s["d_ffn"] = d_ffn.astype(BF)

    in_grads = []
    for index in range(micro):
        s = states[index]
        s["d_tokens"] = gather_tokens(s["d_ffn"], seq)
        d_act = dot(s["d_tokens"], w_down, NT)
        _, back = jax.vjp(lambda a, b: jax.nn.gelu(a, approximate=True) * b, s["gate"], s["up"])
        d_gate, d_up = back(d_act)
        s["d_gate"] = d_gate.astype(BF)
        s["d_up"] = d_up.astype(BF)
        d_normed = scatter_tokens(dot(s["d_gate"], w_gate, NT) + dot(s["d_up"], w_up, NT), seq)
        d_hidden, s["t_pre"] = rms_back(d_normed, s["hidden"], s["scale_pre"], g_pre)
        d_hidden = s["dy"] + d_hidden
        d_attn, s["t_attn"] = rms_back(d_hidden, s["attn_out"], s["scale_attn"], g_attn)
        s["d_attn"] = d_attn.astype(BF)
        d_heads = to_heads(dot(s["d_attn"], w_out, NT).astype(BF))
        scores = jnp.where(s["mask"], dot(s["query_heads"], s["keys_all"], NT), -1e30)
        probs = jnp.exp(scores - s["lse"])
        d_probs = dot(d_heads, s["values_all"], NT)
        inner = jnp.sum(probs * d_probs, axis=-1, keepdims=True)
        d_scores = (probs * (d_probs - inner)).astype(BF)
        d_query = from_heads(dot(d_scores, s["keys_all"]))
        d_pairs = jnp.concatenate(
            [dot(d_scores, s["query_heads"], TN), dot(probs.astype(BF), d_heads, TN)], axis=1
        )
        own = d_pairs[reach * rows :]
        for by in range(1, reach + 1):
            start = (reach - by) * rows
            own = own + from_behind(d_pairs[start : start + rows].astype(BF), -by, seq).astype(F32)
        d_raw_q, s["t_query"] = heads_backward(
            d_query, s["raw_q"], s["scale_q"], g_query, s["cosine"], s["sine"], 1.0 / math.sqrt(HD)
        )
        d_raw_k, s["t_keys"] = heads_backward(
            own[:, :HD], s["raw_k"], s["scale_k"], g_keys, s["cosine"], s["sine"], 1.0
        )
        s["d_raw"] = jnp.concatenate([d_raw_q, d_raw_k, own[:, HD:].astype(BF)], axis=1)
        d_normed_in = dot(s["d_raw"], w_in, NT)
        d_in, s["t_in"] = rms_back(d_normed_in, s["value_in"], s["scale_in"], g_in)
        in_grads.append(d_hidden + d_in)

    def over_micro(left, right):
        return dot(
            jnp.concatenate([s[left] for s in states], axis=0),
            jnp.concatenate([s[right] for s in states], axis=0),
            TN,
        )

    down_terms = over_micro("act", "d_tokens")[:own_ff].astype(BF)
    down_grad = lax.psum_scatter(down_terms, "dp", scatter_dimension=0, tiled=True).astype(F32)

    gu_terms = jnp.concatenate([over_micro("tokens", "d_gate"), over_micro("tokens", "d_up")], axis=1).astype(BF)
    gu_sum = lax.psum_scatter(gu_terms, "dp", scatter_dimension=0, tiled=True)
    gu_sum = lax.all_to_all(gu_sum.reshape(seq, wrows, 2 * pad_ff), "seq", 0, 0)

    def to_columns(part):
        cut = part[:, :, :own_ff].reshape(seq, wrows, dp, chunk).transpose(1, 2, 0, 3)
        return cut.reshape(wrows, ff).astype(F32)

    gate_grad = to_columns(gu_sum[:, :, :pad_ff])
    up_grad = to_columns(gu_sum[:, :, pad_ff:])

    out_grad = lax.psum_scatter(
        over_micro("attended", "d_attn").astype(BF), BOTH, scatter_dimension=0, tiled=True
    ).astype(F32)

    def summed(name):
        return sum(jnp.sum(s[name], axis=0) for s in states)

    def spread(vector):
        return jnp.pad(vector.reshape(devices, short), ((0, 0), (0, wrows - short))).reshape(width)

    gain_terms = jnp.stack(
        [summed("t_in"), summed("t_attn"), summed("t_pre"), summed("t_post")]
        + [spread(sum(s[name] for s in states)) for name in ("t_query", "t_keys")],
        axis=0,
    )
    gain_cols = jnp.pad(gain_terms, ((0, LANES - 6), (0, 0))).T
    in_terms = jnp.concatenate([over_micro("normed_in", "d_raw"), gain_cols], axis=1).astype(BF)
    in_sum = lax.psum_scatter(in_terms.reshape(devices, wrows, -1), BOTH, scatter_dimension=0, tiled=True)
    in_sum = in_sum.reshape(wrows, -1).astype(F32)
    gain_sum = in_sum[:, qd + 2 * HD :]

    return (
        jnp.stack(outputs)[:, None],
        jnp.stack(in_grads)[:, None],
        gain_sum[:, 0],
        in_sum[:, :qd],
        in_sum[:, qd : qd + HD],
        in_sum[:, qd + HD : qd + 2 * HD],
        gain_sum[:short, 4],
        gain_sum[:short, 5],
        out_grad,
        gain_sum[:, 1],
        gain_sum[:, 2],
        gate_grad,
        up_grad,
        down_grad,
        gain_sum[:, 3],
    )


def solution(mesh):
    dp, seq = mesh.shape["dp"], mesh.shape["seq"]
    acts = P(None, "dp", "seq", None)
    vector = P(BOTH)
    matrix = P(BOTH, None)

    def run(*args):
        return shards(dp, seq, *args)

    return jax.shard_map(
        run,
        mesh=mesh,
        in_specs=(acts, acts, P(None, "dp", None), vector)
        + (matrix,) * 3
        + (vector,) * 2
        + (matrix, vector, vector)
        + (matrix,) * 3
        + (vector,),
        out_specs=(acts, acts, vector) + (matrix,) * 3 + (vector,) * 2 + (matrix, vector, vector) + (matrix,) * 3 + (vector,),
        check_vma=False,
    )
```

time: 2160 us -> 924 us (0.43)
  waiting for transfers between devices: 1580 us -> 444 us
  blocking collectives: 165 us -> 0 us
  matrix products: 241 us -> 190 us
  other arithmetic: 41.9 us -> 88.4 us
  starting transfers between devices: 19.3 us -> 64.2 us
    unnamed x10, waiting for transfers between devices: 1240 us -> 141 us
    ppermute x8 -> x40, waiting for transfers between devices: 10.9 us -> 151 us  [the longest x32 151 us: xor_permute(): return lax.ppermute(value, 'seq', [(i, i ^ bit) for i in range(size)])]
    all_gather x5 -> x4, waiting for transfers between devices: 220 us -> 88.4 us  [the longest x1 34.8 us: shards(): gathered = lax.all_gather(packed, BOTH, axis=0, tiled=True)]
    all_gather x2 -> x0, blocking collectives: 84.5 us -> none  [the longest x1 45.7 us: shards(): lax.all_gather(keyproj, ('dp', 'seq'), axis=0, tiled=True)]
    unnamed x2 -> x0, blocking collectives: 80.2 us -> none
    dot_general x47 -> x37, matrix products: 241 us -> 190 us  [dot(): lax.dot_general(left, right, (dims, ((), ())), preferred_element_type=F32)]
    reduce_scatter x1 -> x2, waiting for transfers between devices: 106 us -> 56.6 us  [the longest x1 56.6 us: shards(): lax.psum_scatter(over_micro('attended', 'd_attn').astype(BF), BOTH, scatt...]
    ppermute x8 -> x40, starting transfers between devices: 18.8 us -> 48.5 us  [the longest x32 31.4 us: xor_permute(): return lax.ppermute(value, 'seq', [(i, i ^ bit) for i in range(size)])]
  transfers between devices with their start and end apart: 16 -> 50, of which waited for: 8 -> 24; matrix products, arithmetic and copies ran while one was open for 8% -> 33% of each run, Pallas kernels for 0% -> 0%
where the time goes in v1:
time: 924 us; the launch traced here: 915 us
  waiting for transfers between devices  444 us (48%)
  matrix products  190 us (21%)
  local copies, waits for them, and re-layouts  109 us (12%)
  other arithmetic  88.4 us (10%)
  starting transfers between devices  64.2 us (7%)
  between operations  19.8 us (2%)
    dot_general x37, matrix products, dot(): lax.dot_general(left, right, (dims, ((), ())), preferred_element_type=F32)  190 us
    ppermute x32, waiting for transfers between devices, xor_permute(): return lax.ppermute(value, 'seq', [(i, i ^ bit) for i in range(size)])  151 us
    unnamed x10, waiting for transfers between devices  141 us
    reduce_scatter x1, waiting for transfers between devices, shards(): lax.psum_scatter(over_micro('attended', 'd_attn').astype(BF), BOTH, scatt...  56.6 us
    unnamed x315, local copies, waits for them, and re-layouts  46.2 us
    all_gather x1, waiting for transfers between devices, shards(): gathered = lax.all_gather(packed, BOTH, axis=0, tiled=True)  34.8 us
    ppermute x32, starting transfers between devices, xor_permute(): return lax.ppermute(value, 'seq', [(i, i ^ bit) for i in range(size)])  31.4 us
    all_gather x1, waiting for transfers between devices, shards(): lax.all_gather(gate_up.reshape(seq * wrows, 2 * pad_ff), 'dp', axis=0, ti...  29.2 us
  transfers between devices with their start and end apart: 50, of which 24 were waited for; matrix products, arithmetic and copies ran while one was open for 33% of the time, Pallas kernels for 0%

profile of v1, /device:TPU:0, one launch (start us, length us, event | category | flops | bytes accessed | tf_op | source)
XLA Modules:
  0.0 915.1 jit_solution(13301531978783576837)
XLA Ops:
  41.7 34.8 %all-gather.12.cloned.1.call-done = bf16[32,36,1664]{2,1,0:T(8,128)(2,1)} async-done(((bf16[1,36,1664]{2,1,0:T(8,128)(2,1)}), bf16[32,36,1664]{2,1,0:T(8,128)(2,1)}) %all-gather.12.cloned.1.call-update) | async-done | bytes 3833872 | tf_op jit(solution)/shard_map/all_gather | solution.py:127
  146.2 12.7 %collective-permute-done.2 = bf16[256,1152]{1,0:T(8,128)(2,1)S(1)} collective-permute-done((bf16[256,1152]{1,0:T(8,128)(2,1)S(1)}, bf16[256,1152]{1,0:T(8,128)(2,1)S(1)}, u32[]{:S(2)}, u32[]{:S(2)}) %collective-permute-start.2) | collective-permute-done | bytes 589856 | tf_op jit(solution)/shard_map/ppermute | solution.py:50
  158.9 13.1 %collective-permute-done.3 = bf16[256,1152]{1,0:T(8,128)(2,1)S(1)} collective-permute-done((bf16[256,1152]{1,0:T(8,128)(2,1)S(1)}, bf16[256,1152]{1,0:T(8,128)(2,1)S(1)}, u32[]{:S(2)}, u32[]{:S(2)}) %collective-permute-start.3) | collective-permute-done | bytes 589856 | tf_op jit(solution)/shard_map/ppermute | solution.py:50
  187.5 29.2 %all-gather.8.cloned.1.call-done = bf16[1152,1792]{1,0:T(8,128)(2,1)} async-done(((bf16[288,1792]{1,0:T(8,128)(2,1)}), bf16[1152,1792]{1,0:T(8,128)(2,1)}) %all-gather.8.cloned.1.call-update) | async-done | bytes 4128784 | tf_op jit(solution)/shard_map/all_gather | solution.py:141
  239.7 21.0 %all-gather.10.cloned.1.call-done = bf16[864,1152]{1,0:T(8,128)(2,1)} async-done(((bf16[216,1152]{1,0:T(8,128)(2,1)}), bf16[864,1152]{1,0:T(8,128)(2,1)}) %all-gather.10.cloned.1.call-update) | async-done | bytes 1990672 | tf_op jit(solution)/shard_map/all_gather | solution.py:144
  285.5 10.9 %multiply_convert_fusion.2 = (bf16[2048,896]{1,0:T(8,128)(2,1)}, f32[2048,896]{1,0:T(8,128)}) fusion(f32[2048,896]{1,0:T(8,128)} %fusion.87, bf16[2048,1152]{1,0:T(8,128)(2,1)S(1)} %get-tuple-element.201, bf16[1152,1792]{1,0:T(8,128)(2,1)S(1)} %copy-done.129), kind=kOutput, calls=%fused_computation.35 | convolution fusion | flops 4246208512 | bytes 25133056 | tf_op jit(solution)/shard_map/dot_general | solution.py:20
  328.0 11.2 %collective-permute-done.8 = bf16[256,1152]{1,0:T(8,128)(2,1)S(1)} collective-permute-done((bf16[256,1152]{1,0:T(8,128)(2,1)S(1)}, bf16[256,1152]{1,0:T(8,128)(2,1)S(1)}, u32[]{:S(2)}, u32[]{:S(2)}) %collective-permute-start.8) | collective-permute-done | bytes 589856 | tf_op jit(solution)/shard_map/ppermute | solution.py:50
  339.6 12.2 %collective-permute-done.19 = bf16[256,1152]{1,0:T(8,128)(2,1)S(1)} collective-permute-done((bf16[256,1152]{1,0:T(8,128)(2,1)S(1)}, bf16[256,1152]{1,0:T(8,128)(2,1)S(1)}, u32[]{:S(2)}, u32[]{:S(2)}) %collective-permute-start.19) | collective-permute-done | bytes 589856 | tf_op jit(solution)/shard_map/ppermute | solution.py:50
  351.9 11.6 %collective-permute-done.18 = bf16[256,1152]{1,0:T(8,128)(2,1)S(1)} collective-permute-done((bf16[256,1152]{1,0:T(8,128)(2,1)S(1)}, bf16[256,1152]{1,0:T(8,128)(2,1)S(1)}, u32[]{:S(2)}, u32[]{:S(2)}) %collective-permute-start.18) | collective-permute-done | bytes 589856 | tf_op jit(solution)/shard_map/ppermute | solution.py:50
  370.7 12.7 %collective-permute-done.20 = bf16[256,1152]{1,0:T(8,128)(2,1)S(1)} collective-permute-done((bf16[256,1152]{1,0:T(8,128)(2,1)S(1)}, bf16[256,1152]{1,0:T(8,128)(2,1)S(1)}, u32[]{:S(2)}, u32[]{:S(2)}) %collective-permute-start.20) | collective-permute-done | bytes 589856 | tf_op jit(solution)/shard_map/ppermute | solution.py:50
  383.4 12.8 %collective-permute-done.21 = bf16[256,1152]{1,0:T(8,128)(2,1)S(1)} collective-permute-done((bf16[256,1152]{1,0:T(8,128)(2,1)S(1)}, bf16[256,1152]{1,0:T(8,128)(2,1)S(1)}, u32[]{:S(2)}, u32[]{:S(2)}) %collective-permute-start.21) | collective-permute-done | bytes 589856 | tf_op jit(solution)/shard_map/ppermute | solution.py:50
  410.0 12.7 %collective-permute-done.30 = bf16[256,1152]{1,0:T(8,128)(2,1)S(1)} collective-permute-done((bf16[256,1152]{1,0:T(8,128)(2,1)S(1)}, bf16[256,1152]{1,0:T(8,128)(2,1)S(1)}, u32[]{:S(2)}, u32[]{:S(2)}) %collective-permute-start.30) | collective-permute-done | bytes 589856 | tf_op jit(solution)/shard_map/ppermute | solution.py:50
  422.7 12.1 %collective-permute-done.31 = bf16[256,1152]{1,0:T(8,128)(2,1)S(1)} collective-permute-done((bf16[256,1152]{1,0:T(8,128)(2,1)S(1)}, bf16[256,1152]{1,0:T(8,128)(2,1)S(1)}, u32[]{:S(2)}, u32[]{:S(2)}) %collective-permute-start.31) | collective-permute-done | bytes 589856 | tf_op jit(solution)/shard_map/ppermute | solution.py:50
  435.3 14.4 %multiply_convert_fusion.1 = (bf16[2048,896]{1,0:T(8,128)(2,1)}, bf16[2048,896]{1,0:T(8,128)(2,1)}) fusion(f32[2048,896]{1,0:T(8,128)} %copy-done.133, f32[2048,896]{1,0:T(8,128)} %get-tuple-element.318, bf16[2048,1152]{1,0:T(8,128)(2,1)S(1)} %get-tuple-element.205, bf16[864,1152]{1,0:T(8,128)(2,1)S(1)} %copy-done.132), kind=kOutput, calls=%fused_computation.34 | convolution fusion | flops 4271898624 | bytes 28729344 | tf_op jit(solution)/shard_map/dot_general | solution.py:20
  449.7 9.5 %fusion.85 = f32[2048,1152]{1,0:T(8,128)} fusion(bf16[2048,896]{1,0:T(8,128)(2,1)} %get-tuple-element.195, bf16[1152,1792]{1,0:T(8,128)(2,1)S(1)} %copy-done.130), kind=kOutput, calls=%fused_computation.142 | convolution fusion | flops 4227858432 | bytes 15171584 | tf_op jit(solution)/shard_map/dot_general | solution.py:20
  463.8 14.4 %multiply_convert_fusion = (bf16[2048,896]{1,0:T(8,128)(2,1)}, bf16[2048,896]{1,0:T(8,128)(2,1)}) fusion(f32[2048,896]{1,0:T(8,128)} %fusion.87, f32[2048,896]{1,0:T(8,128)} %get-tuple-element.320, bf16[2048,1152]{1,0:T(8,128)(2,1)S(1)} %get-tuple-element.199, bf16[864,1152]{1,0:T(8,128)(2,1)S(1)} %copy-done.132), kind=kOutput, calls=%fused_computation.33 | convolution fusion | flops 4271898624 | bytes 28729344 | tf_op jit(solution)/shard_map/dot_general | solution.py:20
  478.2 15.0 %fusion.29 = bf16[1152,896]{0,1:T(8,128)(2,1)S(1)} fusion(bf16[4096,1152]{1,0:T(8,128)(2,1)} %get-tuple-element.200, bf16[2048,896]{1,0:T(8,128)(2,1)} %get-tuple-element.197, bf16[2048,896]{1,0:T(8,128)(2,1)} %get-tuple-element.195), kind=kOutput, calls=%fused_computation.52 | convolution fusion | flops 8471429120 | bytes 18841600 | tf_op jit(solution)/shard_map/dot_general | solution.py:20
  493.2 13.3 %fusion.26 = bf16[1152,896]{0,1:T(8,128)(2,1)S(1)} fusion(bf16[4096,1152]{1,0:T(8,128)(2,1)S(1)} %bitcast.280, bf16[2048,896]{1,0:T(8,128)(2,1)} %get-tuple-element.196, bf16[2048,896]{1,0:T(8,128)(2,1)} %get-tuple-element.194), kind=kOutput, calls=%fused_computation.51 | convolution fusion | flops 8471429120 | bytes 18841600 | tf_op jit(solution)/shard_map/dot_general | solution.py:20
  515.3 9.9 %convolution_add_fusion.1 = f32[2048,1152]{1,0:T(8,128)S(1)} fusion(f32[2048,1152]{1,0:T(8,128)} %fusion.85, bf16[2048,896]{1,0:T(8,128)(2,1)} %get-tuple-element.194, bf16[1152,1792]{1,0:T(8,128)(2,1)} %all-gather.8.cloned.1.call-done), kind=kOutput, calls=%fused_computation.5 | convolution fusion | flops 4230217728 | bytes 24608768 | tf_op jit(solution)/shard_map/dot_general | solution.py:20
  569.8 13.7 %fusion.22 = bf16[896,1152]{1,0:T(8,128)(2,1)S(1)} fusion(bf16[4096,1152]{1,0:T(8,128)(2,1)} %get-tuple-element.198, bf16[2048,896]{1,0:T(8,128)(2,1)S(1)} %copy-done.135, bf16[2048,896]{1,0:T(8,128)(2,1)S(1)} %copy-done.134), kind=kOutput, calls=%fused_computation.29 | convolution fusion | flops 8470396928 | bytes 18841600 | tf_op jit(solution)/shard_map/dot_general | solution.py:20
  593.8 12.0 %collective-permute-done.36 = bf16[256,1152]{1,0:T(8,128)(2,1)S(1)} collective-permute-done((bf16[256,1152]{1,0:T(8,128)(2,1)}, bf16[256,1152]{1,0:T(8,128)(2,1)S(1)}, u32[]{:S(2)}, u32[]{:S(2)}) %collective-permute-start.36) | collective-permute-done | bytes 589856 | tf_op jit(solution)/shard_map/ppermute | solution.py:50
  682.9 9.8 %all-to-all-start.1 = ((bf16[8,36,1792]{2,1,0:T(8,128)(2,1)}), bf16[8,36,1792]{2,1,0:T(8,128)(2,1)}, u32[]{:S(2)}, u32[]{:S(2)}) async-start(bf16[8,36,1792]{2,1,0:T(8,128)(2,1)} %reshape.633), calls=%async_computation.2 | async-start | bytes 2293760 | tf_op jit(solution)/shard_map/all_to_all | solution.py:281
  698.6 56.6 %reduce-scatter.12.cloned.1.call-done = bf16[32,1152]{1,0:T(8,128)(2,1)} async-done(((bf16[1024,1152]{1,0:T(8,128)(2,1)}), bf16[32,1152]{1,0:T(8,128)(2,1)}) %reduce-scatter.12.cloned.1.call-update) | async-done | bytes 73744 | tf_op jit(solution)/shard_map/reduce_scatter | solution.py:290
  764.3 140.1 %reduce-scatter.16.cloned.1.call-done = bf16[1,36,1664]{2,1,0:T(8,128)(2,1)} async-done(((bf16[32,36,1664]{2,1,0:T(8,128)(2,1)}), bf16[1,36,1664]{2,1,0:T(8,128)(2,1)}) %reduce-scatter.16.cloned.1.call-update) | async-done | bytes 119824
  (632 shorter events, 379.6 us)
Async XLA Ops:
  7.2 69.3 %all-gather.12.cloned.1.call-start = ((), (), s32[]{:S(2)}) async-start(), calls=%async_computation.10 | async-start | bytes 4392960 | tf_op jit(solution)/shard_map/all_gather | solution.py:127
  10.4 126.1 %all-gather.6.cloned.1.call-start = ((), (), s32[]{:S(2)}) async-start(), calls=%async_computation.6 | async-start | bytes 2433024 | tf_op jit(solution)/shard_map/all_gather | solution.py:133
  23.7 193.0 %all-gather.8.cloned.1.call-start = ((), (), s32[]{:S(2)}) async-start(), calls=%async_computation.7 | async-start | bytes 5160960 | tf_op jit(solution)/shard_map/all_gather | solution.py:141
  41.3 219.3 %all-gather.10.cloned.1.call-start = ((), (), s32[]{:S(2)}) async-start(), calls=%async_computation.8 | async-start | bytes 2488320 | tf_op jit(solution)/shard_map/all_gather | solution.py:144
  144.2 27.8 %collective-permute-start.3 = (bf16[256,1152]{1,0:T(8,128)(2,1)S(1)}, bf16[256,1152]{1,0:T(8,128)(2,1)S(1)}, u32[]{:S(2)}, u32[]{:S(2)}) collective-permute-start(bf16[256,1152]{1,0:T(8,128)(2,1)S(1)} %get-tuple-element.169), channel_id=1, source_target_pairs={{0,4},{1,5},{2,6},{3,7},{4,0},{5,1},{6,2},{7,3},{8,12},{9,13},{10,... | collective-permute-start | bytes 1769480 | tf_op jit(solution)/shard_map/ppermute | solution.py:50
  174.5 506.3 %reduce-scatter.14.cloned.1.call-start = ((), (), s32[]{:S(2)}) async-start(), calls=%async_computation.11 | async-start | bytes 5160960 | tf_op jit(solution)/shard_map/reduce_scatter | solution.py:280
  184.0 40.7 %collective-permute-start.12 = (bf16[256,1152]{1,0:T(8,128)(2,1)S(1)}, bf16[256,1152]{1,0:T(8,128)(2,1)}, u32[]{:S(2)}, u32[]{:S(2)}) collective-permute-start(bf16[256,1152]{1,0:T(8,128)(2,1)S(1)} %get-tuple-element.167), channel_id=1, source_target_pairs={{0,2},{1,3},{2,0},{3,1},{4,6},{5,7},{6,4},{7,5},{8,10},{9,11},{10,... | collective-permute-start | bytes 1769480 | tf_op jit(solution)/shard_map/ppermute | solution.py:50
  185.2 39.6 %collective-permute-start.13 = (bf16[256,1152]{1,0:T(8,128)(2,1)S(1)}, bf16[256,1152]{1,0:T(8,128)(2,1)}, u32[]{:S(2)}, u32[]{:S(2)}) collective-permute-start(bf16[256,1152]{1,0:T(8,128)(2,1)S(1)} %get-tuple-element.167), channel_id=1, source_target_pairs={{0,4},{1,5},{2,6},{3,7},{4,0},{5,1},{6,2},{7,3},{8,12},{9,13},{10,... | collective-permute-start | bytes 1769480 | tf_op jit(solution)/shard_map/ppermute | solution.py:50
  186.1 38.7 %collective-permute-start.14 = (bf16[256,1152]{1,0:T(8,128)(2,1)S(1)}, bf16[256,1152]{1,0:T(8,128)(2,1)S(1)}, u32[]{:S(2)}, u32[]{:S(2)}) collective-permute-start(bf16[256,1152]{1,0:T(8,128)(2,1)S(1)} %get-tuple-element.167), channel_id=1, source_target_pairs={{0,6},{1,7},{2,4},{3,5},{4,2},{5,3},{6,0},{7,1},{8,14},{9,15},{10,... | collective-permute-start | bytes 1769480 | tf_op jit(solution)/shard_map/ppermute | solution.py:50
  228.7 45.4 %collective-permute-start.15 = (bf16[1024,1152]{1,0:T(8,128)(2,1)}, bf16[1024,1152]{1,0:T(8,128)(2,1)}, u32[]{:S(2)}, u32[]{:S(2)}) collective-permute-start(bf16[1024,1152]{1,0:T(8,128)(2,1)} %pad_maximum_fusion.3), channel_id=1, source_target_pairs={{0,1},{1,0},{2,3},{3,2},{4,5},{5,4},{6,7},{7,6},{8,9},{9,8},{10,11... | collective-permute-start | bytes 7077896 | tf_op jit(solution)/shard_map/ppermute | solution.py:50
  269.2 37.6 %collective-permute-start.6 = (bf16[1024,1152]{1,0:T(8,128)(2,1)S(1)}, bf16[1024,1152]{1,0:T(8,128)(2,1)}, u32[]{:S(2)}, u32[]{:S(2)}) collective-permute-start(bf16[1024,1152]{1,0:T(8,128)(2,1)S(1)} %slice.671), channel_id=1, source_target_pairs={{0,1},{1,0},{2,3},{3,2},{4,5},{5,4},{6,7},{7,6},{8,9},{9,8},{10,11... | collective-permute-start | bytes 7077896 | tf_op jit(solution)/shard_map/ppermute | solution.py:50
  315.4 36.5 %collective-permute-start.19 = (bf16[256,1152]{1,0:T(8,128)(2,1)S(1)}, bf16[256,1152]{1,0:T(8,128)(2,1)S(1)}, u32[]{:S(2)}, u32[]{:S(2)}) collective-permute-start(bf16[256,1152]{1,0:T(8,128)(2,1)S(1)} %get-tuple-element.216), channel_id=1, source_target_pairs={{0,6},{1,7},{2,4},{3,5},{4,2},{5,3},{6,0},{7,1},{8,14},{9,15},{10,... | collective-permute-start | bytes 1769480 | tf_op jit(solution)/shard_map/ppermute | solution.py:50
  317.8 45.6 %collective-permute-start.18 = (bf16[256,1152]{1,0:T(8,128)(2,1)S(1)}, bf16[256,1152]{1,0:T(8,128)(2,1)S(1)}, u32[]{:S(2)}, u32[]{:S(2)}) collective-permute-start(bf16[256,1152]{1,0:T(8,128)(2,1)S(1)} %get-tuple-element.217), channel_id=1, source_target_pairs={{0,4},{1,5},{2,6},{3,7},{4,0},{5,1},{6,2},{7,3},{8,12},{9,13},{10,... | collective-permute-start | bytes 1769480 | tf_op jit(solution)/shard_map/ppermute | solution.py:50
  326.5 37.0 %collective-permute-start.17 = (bf16[256,1152]{1,0:T(8,128)(2,1)S(1)}, bf16[256,1152]{1,0:T(8,128)(2,1)S(1)}, u32[]{:S(2)}, u32[]{:S(2)}) collective-permute-start(bf16[256,1152]{1,0:T(8,128)(2,1)S(1)} %get-tuple-element.215), channel_id=1, source_target_pairs={{0,2},{1,3},{2,0},{3,1},{4,6},{5,7},{6,4},{7,5},{8,10},{9,11},{10,... | collective-permute-start | bytes 1769480 | tf_op jit(solution)/shard_map/ppermute | solution.py:50
  407.1 27.7 %collective-permute-start.31 = (bf16[256,1152]{1,0:T(8,128)(2,1)S(1)}, bf16[256,1152]{1,0:T(8,128)(2,1)S(1)}, u32[]{:S(2)}, u32[]{:S(2)}) collective-permute-start(bf16[256,1152]{1,0:T(8,128)(2,1)S(1)} %get-tuple-element.163), channel_id=1, source_target_pairs={{0,4},{1,5},{2,6},{3,7},{4,0},{5,1},{6,2},{7,3},{8,12},{9,13},{10,... | collective-permute-start | bytes 1769480 | tf_op jit(solution)/shard_map/ppermute | solution.py:50
  515.3 181.3 %reduce-scatter.18.cloned.1.call-start = ((), (), s32[]{:S(2)}) async-start(), calls=%async_computation.13 | async-start | bytes 2488320
  552.4 32.9 %collective-permute-start.26 = (bf16[256,1152]{1,0:T(8,128)(2,1)}, bf16[256,1152]{1,0:T(8,128)(2,1)}, u32[]{:S(2)}, u32[]{:S(2)}) collective-permute-start(bf16[256,1152]{1,0:T(8,128)(2,1)} %get-tuple-element.204), channel_id=1, source_target_pairs={{0,4},{1,5},{2,6},{3,7},{4,0},{5,1},{6,2},{7,3},{8,12},{9,13},{10,... | collective-permute-start | bytes 1769480 | tf_op jit(solution)/shard_map/ppermute | solution.py:50
  554.2 31.1 %collective-permute-start.25 = (bf16[256,1152]{1,0:T(8,128)(2,1)}, bf16[256,1152]{1,0:T(8,128)(2,1)}, u32[]{:S(2)}, u32[]{:S(2)}) collective-permute-start(bf16[256,1152]{1,0:T(8,128)(2,1)} %get-tuple-element.202), channel_id=1, source_target_pairs={{0,2},{1,3},{2,0},{3,1},{4,6},{5,7},{6,4},{7,5},{8,10},{9,11},{10,... | collective-permute-start | bytes 1769480 | tf_op jit(solution)/shard_map/ppermute | solution.py:50
  559.2 34.6 %collective-permute-start.37 = (bf16[256,1152]{1,0:T(8,128)(2,1)}, bf16[256,1152]{1,0:T(8,128)(2,1)S(1)}, u32[]{:S(2)}, u32[]{:S(2)}) collective-permute-start(bf16[256,1152]{1,0:T(8,128)(2,1)} %get-tuple-element.208), channel_id=1, source_target_pairs={{0,6},{1,7},{2,4},{3,5},{4,2},{5,3},{6,0},{7,1},{8,14},{9,15},{10,... | collective-permute-start | bytes 1769480 | tf_op jit(solution)/shard_map/ppermute | solution.py:50
  560.2 45.6 %collective-permute-start.36 = (bf16[256,1152]{1,0:T(8,128)(2,1)}, bf16[256,1152]{1,0:T(8,128)(2,1)S(1)}, u32[]{:S(2)}, u32[]{:S(2)}) collective-permute-start(bf16[256,1152]{1,0:T(8,128)(2,1)} %get-tuple-element.209), channel_id=1, source_target_pairs={{0,4},{1,5},{2,6},{3,7},{4,0},{5,1},{6,2},{7,3},{8,12},{9,13},{10,... | collective-permute-start | bytes 1769480 | tf_op jit(solution)/shard_map/ppermute | solution.py:50
  568.5 37.4 %collective-permute-start.35 = (bf16[256,1152]{1,0:T(8,128)(2,1)}, bf16[256,1152]{1,0:T(8,128)(2,1)}, u32[]{:S(2)}, u32[]{:S(2)}) collective-permute-start(bf16[256,1152]{1,0:T(8,128)(2,1)} %get-tuple-element.207), channel_id=1, source_target_pairs={{0,2},{1,3},{2,0},{3,1},{4,6},{5,7},{6,4},{7,5},{8,10},{9,11},{10,... | collective-permute-start | bytes 1769480 | tf_op jit(solution)/shard_map/ppermute | solution.py:50
  585.2 170.0 %reduce-scatter.12.cloned.1.call-start = ((), (), s32[]{:S(2)}) async-start(), calls=%async_computation.9 | async-start | bytes 2433024 | tf_op jit(solution)/shard_map/reduce_scatter | solution.py:290
  647.1 257.2 %reduce-scatter.16.cloned.1.call-start = ((), (), s32[]{:S(2)}) async-start(), calls=%async_computation.12 | async-start | bytes 4392960
  682.9 73.9 %all-to-all-start.1 = ((bf16[8,36,1792]{2,1,0:T(8,128)(2,1)}), bf16[8,36,1792]{2,1,0:T(8,128)(2,1)}, u32[]{:S(2)}, u32[]{:S(2)}) async-start(bf16[8,36,1792]{2,1,0:T(8,128)(2,1)} %reshape.633), calls=%async_computation.2 | async-start | bytes 2293760 | tf_op jit(solution)/shard_map/all_to_all | solution.py:281
  (168 other events, 2272.1 us)
Sparse Core Ops, SparseCore 0:
  11.5 64.9 all-gather.11
  79.4 57.0 all-gather.5
  138.1 78.5 all-gather.7
  218.1 42.4 all-gather.9
  515.4 73.8 reduce-scatter.13
  591.5 42.2 reduce-scatter.17
  647.2 107.9 reduce-scatter.11
  757.5 146.7 reduce-scatter.15

commit v2 on v1

v2 whole, which is shorter than its diff:
```python
import functools
import math

import jax
import jax.numpy as jnp
from jax import lax
from jax.experimental import pallas as pl
from jax.experimental.pallas import tpu as pltpu
from jax.sharding import PartitionSpec as P

HEADS = 4
HD = 256
HALF = HD // 2
WINDOW = 512
EPS = 1e-06
LANES = 128
FACTOR = 1.0 / math.sqrt(HD)
GELU_C = math.sqrt(2.0 / math.pi)
NEG = -1e30

BF = jnp.bfloat16
F32 = jnp.float32
BOTH = ("dp", "seq")
NN = ((1,), (0,))
NT = ((1,), (1,))
TN = ((0,), (0,))


def dot(left, right, dims=NN):
    return lax.dot_general(left, right, (dims, ((), ())), preferred_element_type=F32)


def shape(dims, dtype):
    return jax.ShapeDtypeStruct(dims, dtype)


def whole(array):
    return pl.BlockSpec(array.shape, lambda *_: (0,) * array.ndim)


def call(body, grid, inputs, outs, scratch=(), aliases=None, name=None):
    return pl.pallas_call(
        body,
        **({} if grid is None else {"grid": grid}),
        in_specs=[spec for _, spec in inputs],
        out_specs=[spec for _, spec in outs],
        out_shape=[made for made, _ in outs],
        scratch_shapes=list(scratch),
        input_output_aliases=aliases or {},
        compiler_params=pltpu.CompilerParams(vmem_limit_bytes=58 * 2**20),
        cost_estimate=pl.CostEstimate(flops=0, bytes_accessed=1, transcendentals=0),
        name=name,
    )(*[array for array, _ in inputs])


def scale_of(values):
    return lax.rsqrt(jnp.mean(values * values, axis=-1, keepdims=True) + EPS)


def rms(values, gain):
    return values * scale_of(values) * (1.0 + gain)


def rms_back(grad, values, gain):
    scale = scale_of(values)
    normed = values * scale
    inner = grad * (1.0 + gain)
    back = scale * (inner - normed * jnp.mean(inner * normed, axis=-1, keepdims=True))
    return back, jnp.sum(grad * normed, axis=0, keepdims=True)


def turn(values, cosine, sine):
    first, second = values[:, :HALF], values[:, HALF:]
    return jnp.concatenate([first * cosine - second * sine, second * cosine + first * sine], axis=1)


def turn_back(grad, cosine, sine):
    first, second = grad[:, :HALF], grad[:, HALF:]
    return jnp.concatenate([first * cosine + second * sine, second * cosine - first * sine], axis=1)


def gelu_parts(value):
    inner = GELU_C * (value + 0.044715 * value * value * value)
    tanh = jnp.tanh(inner)
    gelu = 0.5 * value * (1.0 + tanh)
    slope = 0.5 * (1.0 + tanh) + 0.5 * value * (1.0 - tanh * tanh) * GELU_C * (1.0 + 3 * 0.044715 * value * value)
    return gelu, slope


def spots(short, wrows, width):
    row = lax.broadcasted_iota(jnp.int32, (width, HD), 0)
    entry = lax.broadcasted_iota(jnp.int32, (width, HD), 1)
    bits = short.bit_length() - 1
    return (row == (entry >> bits) * wrows + (entry & (short - 1))).astype(F32).astype(BF)


def project_kernel(
    short, wrows, x_ref, w_ref, packed_ref, cos_ref, sin_ref, normed_ref, raw_ref, q_ref, pair_ref, gains_ref
):
    qd = q_ref.shape[-1]
    width = x_ref.shape[-1]
    gains_ref[...] = jnp.transpose(packed_ref[...].astype(F32))[:8]
    heads = dot(packed_ref[...], spots(short, wrows, width), TN)
    gains_ref[4:6, :HD] = heads[4:6]
    g_q, g_k = heads[4:5], heads[5:6]
    normed = rms(x_ref[0, 0].astype(F32), gains_ref[0:1]).astype(BF)
    normed_ref[0] = normed
    raw = dot(normed, w_ref[...])
    raw_ref[0] = raw[:, : qd + HD]
    cosine, sine = cos_ref[0], sin_ref[0]
    for head in range(qd // HD):
        at = slice(head * HD, (head + 1) * HD)
        q_ref[0, :, at] = (turn(rms(raw[:, at], g_q), cosine, sine) * FACTOR).astype(BF)
    keys = turn(rms(raw[:, qd : qd + HD], g_k), cosine, sine)
    pair_ref[0, :, :HD] = keys.astype(BF)
    pair_ref[0, :, HD:] = raw[:, qd + HD :].astype(BF)


def masks_of(rows, reach, place):
    length, base = place[0], place[1]
    query = lax.broadcasted_iota(jnp.int32, (rows, rows), 0)
    keys = lax.broadcasted_iota(jnp.int32, (rows, rows), 1)
    first = base & -length
    masks = []
    for by in range(reach + 1):
        behind = query - keys + by * rows
        valid = jnp.where(base - by * rows >= first, WINDOW, -1)
        masks.append((behind >= 0) & (behind < valid))
    return masks


def probs_of(query, pairs, masks):
    scores = [jnp.where(m, dot(query, p[:, :HD], NT), NEG) for p, m in zip(pairs, masks)]
    top = functools.reduce(jnp.maximum, [jnp.max(s, axis=-1, keepdims=True) for s in scores])
    raised = [jnp.exp(s - top) for s in scores]
    total = functools.reduce(jnp.add, [jnp.sum(e, axis=-1, keepdims=True) for e in raised])
    return [e * (1.0 / total) for e in raised]


def attend_kernel(reach, place, x_ref, q_ref, *rest):
    pairs_refs, (w_out, gains, att_ref, out_ref, hidden_ref, nf_ref) = rest[: reach + 1], rest[reach + 1 :]
    pairs = [p[...].reshape(p.shape[-2:]) for p in pairs_refs]
    masks = masks_of(pairs[0].shape[0], reach, place)
    qd = q_ref.shape[-1]
    for head in range(qd // HD):
        at = slice(head * HD, (head + 1) * HD)
        probs = probs_of(q_ref[0, :, at], pairs, masks)
        mixed = sum(dot(p.astype(BF), v[:, HD:]) for p, v in zip(probs, pairs))
        att_ref[:, at] = mixed.astype(BF)
    out = dot(att_ref[...], w_out[...])
    out_ref[...] = out
    hidden = x_ref[0, 0].astype(F32) + rms(out, gains[1:2])
    hidden_ref[...] = hidden
    nf_ref[...] = rms(hidden, gains[2:3]).astype(BF)


def gelu_gate(gate, up):
    return 0.5 * gate * (1.0 + jnp.tanh(GELU_C * (gate + 0.044715 * gate * gate * gate))) * up


def ffn_rows(tokens, w_gu, w_down, store):
    total = None
    for half, (gu, down) in enumerate(zip(w_gu, w_down)):
        pad = down.shape[0]
        both = dot(tokens, gu[...])
        gate, up = both[:, :pad], both[:, pad:]
        act = gelu_gate(gate, up).astype(BF)
        store(half, gate.astype(BF), up.astype(BF), act)
        part = dot(act, down[...])
        total = part if total is None else total + part
    return total.astype(BF)


def ffn_back_rows(tokens, kept, w_gu, w_down, store):
    total = None
    for half, (gu, down) in enumerate(zip(w_gu, w_down)):
        gate, up = kept(half)
        d_act = dot(tokens, down[...], NT)
        gelu, slope = gelu_parts(gate.astype(F32))
        d_gate = (d_act * up.astype(F32) * slope).astype(BF)
        d_up = (d_act * gelu).astype(BF)
        store(half, d_gate, d_up)
        pad = down.shape[0]
        part = dot(d_gate, gu[:, :pad], NT) + dot(d_up, gu[:, pad:], NT)
        total = part if total is None else total + part
    return total.astype(BF)


def ffn_grid_kernel(halves, t_ref, *refs):
    w_gu, w_down, refs = refs[:halves], refs[halves : 2 * halves], refs[2 * halves :]

    def store(half, *values):
        for kind, value in enumerate(values):
            refs[kind * halves + half][...] = value

    refs[-1][...] = ffn_rows(t_ref[...], w_gu, w_down, store)


def ffn_back_grid_kernel(halves, t_ref, *refs):
    gates, ups, w_gu, w_down = (refs[i * halves : (i + 1) * halves] for i in range(4))
    refs = refs[4 * halves :]

    def store(half, *values):
        for kind, value in enumerate(values):
            refs[kind * halves + half][...] = value

    kept = lambda half: (gates[half][...], ups[half][...])
    refs[-1][...] = ffn_back_rows(t_ref[...], kept, w_gu, w_down, store)


class Leaving:
    def __init__(self, sems):
        self.sems, self.copies = sems, []

    def send(self, source, target):
        copy = pltpu.make_async_copy(source, target, self.sems.at[len(self.copies)])
        copy.start()
        self.copies.append(copy)

    def wait(self):
        for copy in self.copies:
            copy.wait()


def ffn_kernel(count, halves, *refs):
    tokens, refs = refs[:count], refs[count:]
    w_gu, w_down, refs = refs[:halves], refs[halves : 2 * halves], refs[2 * halves :]
    t_out, outs, parts = refs[0], refs[1 : 1 + 3 * halves], refs[1 + 3 * halves : 1 + 3 * halves + count]
    buffers, sems = refs[1 + 3 * halves + count : -1], refs[-1]
    leaving = Leaving(sems)
    rows = tokens[0].shape[0]
    for index in range(count):
        at = pl.ds(index * rows, rows)
        leaving.send(tokens[index], t_out.at[at])

        def store(half, *values):
            for kind, value in enumerate(values):
                slot = kind * halves + half
                buffers[slot][at] = value
                leaving.send(buffers[slot].at[at], outs[slot].at[at])

        parts[index][...] = ffn_rows(tokens[index][...], w_gu, w_down, store)
    leaving.wait()


def ffn_back_kernel(count, halves, *refs):
    tokens, refs = refs[:count], refs[count:]
    gates, ups, w_gu, w_down = (refs[i * halves : (i + 1) * halves] for i in range(4))
    t_out, refs = refs[4 * halves], refs[4 * halves + 1 :]
    outs, parts = refs[: 2 * halves], refs[2 * halves : 2 * halves + count]
    kept_in, buffers, sems, in_sems = refs[2 * halves + count : -2 - 2 * halves], refs[-2 - 2 * halves : -2], refs[-2], refs[-1]
    leaving = Leaving(sems)
    rows = tokens[0].shape[0]
    arriving = {}
    for index in range(count):
        at = pl.ds(index * rows, rows)
        for half in range(halves):
            for kind, source in enumerate((gates[half], ups[half])):
                slot = kind * halves + half
                copy = pltpu.make_async_copy(source.at[at], kept_in[slot].at[at], in_sems.at[index * 2 * halves + slot])
                copy.start()
                arriving[index, slot] = copy
    for index in range(count):
        at = pl.ds(index * rows, rows)
        leaving.send(tokens[index], t_out.at[at])

        def kept(half):
            for slot in (half, halves + half):
                arriving[index, slot].wait()
            return kept_in[half][at], kept_in[halves + half][at]

        def store(half, *values):
            for kind, value in enumerate(values):
                slot = kind * halves + half
                buffers[slot][at] = value
                leaving.send(buffers[slot].at[at], outs[slot].at[at])

        parts[index][...] = ffn_back_rows(tokens[index][...], kept, w_gu, w_down, store)
    leaving.wait()


def untangle_kernel(dp, seq, place, *refs):
    lines, (in_ref, out_ref) = refs[:-2], refs[-2:]
    columns = in_ref.shape[1]
    in_rows, out_rows = in_ref.shape[0] // (dp * seq), out_ref.shape[0] // (dp * seq)

    def body(me):
        for index, ref in enumerate(lines):
            at = me ^ (index % 4 * 2) ^ (index // 4)
            for d in range(dp):
                start, to = d * in_rows, d * seq + at
                in_ref[to * in_rows : (to + 1) * in_rows] = ref[start : start + in_rows, :columns]
                out_ref[to * out_rows : (to + 1) * out_rows] = ref[start : start + out_rows, columns:]

    on_value(place[0], seq, body)


def pad_kernel(in_ref, out_ref):
    rows = in_ref.shape[0]
    out_ref[:rows] = in_ref[...]
    out_ref[rows:] = jnp.zeros((out_ref.shape[0] - rows, out_ref.shape[1]), out_ref.dtype)


def join_kernel(*refs):
    pieces, out, sems = refs[:-2], refs[-2], refs[-1]
    rows = pieces[0].shape[0]
    copies = []
    for index, piece in enumerate(pieces):
        copies.append(pltpu.make_async_copy(piece, out.at[pl.ds(index * rows, rows)], sems.at[index]))
        copies[-1].start()
    for copy in copies:
        copy.wait()


def owner_kernel(dp, gate_ref, up_ref, out_ref):
    seq, rows, columns = out_ref.shape
    pad = columns // 2
    chunk = gate_ref.shape[1] // (dp * seq)
    zeros = [] if pad == dp * chunk else [jnp.zeros((rows, pad - dp * chunk), BF)]
    for to in range(seq):
        for half, ref in enumerate((gate_ref, up_ref)):
            cuts = [ref[:, (d * seq + to) * chunk : (d * seq + to + 1) * chunk] for d in range(dp)]
            out_ref[to, :, half * pad : (half + 1) * pad] = jnp.concatenate(cuts + zeros, axis=1)


def columns_kernel(dp, in_ref, out_ref):
    seq = in_ref.shape[0]
    chunk = out_ref.shape[1] // (dp * seq)
    for d in range(dp):
        for at in range(seq):
            start = (d * seq + at) * chunk
            out_ref[:, start : start + chunk] = in_ref[at, :, d * chunk : (d + 1) * chunk].astype(F32)


def add_up(refs):
    total = refs[0][...].astype(F32)
    for ref in refs[1:]:
        total = total + ref[...].astype(F32)
    return total


def middle_kernel(count, chained, *refs):
    parts, (dy_ref, hidden_ref, gains), (out_ref, d_ref, t_ref) = refs[:count], refs[count : count + 3], refs[-3:]
    g_post = gains[3:4]
    ffn_out = add_up(parts)
    out_ref[0, 0] = hidden_ref[...] + rms(ffn_out, g_post)
    back, terms = rms_back(dy_ref[0, 0].astype(F32), ffn_out, g_post)
    d_ref[...] = back.astype(BF)
    t_ref[...] = terms


def attend_back_kernel(reach, count, place, *refs):
    parts, refs = refs[:count], refs[count:]
    dy_ref, hidden_ref, out_ref, q_ref, raw_ref, cos_ref, sin_ref, w_out, gains = refs[:9]
    pairs_refs, refs = refs[9 : 10 + reach], refs[10 + reach :]
    g_attn, g_pre, g_q = gains[1:2], gains[2:3], gains[4:5, :HD]
    dh_ref, da_ref, dq_ref, t_pre, t_attn, t_q = refs[:6]
    back_refs, own_ref, sums = refs[6 : 6 + reach], refs[6 + reach], refs[7 + reach :]
    d_hidden, terms = rms_back(add_up(parts), hidden_ref[...], g_pre)
    t_pre[...] = terms
    d_hidden = d_hidden + dy_ref[0, 0].astype(F32)
    dh_ref[...] = d_hidden
    d_attn, terms = rms_back(d_hidden, out_ref[...], g_attn)
    t_attn[...] = terms
    d_attn = d_attn.astype(BF)
    da_ref[...] = d_attn
    d_heads = dot(d_attn, w_out[...], NT).astype(BF)
    pairs = [p[...].reshape(p.shape[-2:]) for p in pairs_refs]
    masks = masks_of(pairs[0].shape[0], reach, place)
    into = (own_ref,) + tuple(sums)
    total_q = None
    for head in range(q_ref.shape[-1] // HD):
        at = slice(head * HD, (head + 1) * HD)
        query, d_head = q_ref[0, :, at], d_heads[:, at]
        probs = probs_of(query, pairs, masks)
        d_probs = [dot(d_head, p[:, HD:], NT) for p in pairs]
        inner = sum(jnp.sum(p * d, axis=-1, keepdims=True) for p, d in zip(probs, d_probs))
        d_scores = [(p * (d - inner)).astype(BF) for p, d in zip(probs, d_probs)]
        d_query = sum(dot(d, p[:, :HD]) for d, p in zip(d_scores, pairs))
        for ref, d, p in zip(into, d_scores, probs):
            d_keys = dot(d, query, TN)
            d_value = dot(p.astype(BF), d_head, TN)
            if head == 0:
                ref[:, :HD] = d_keys
                ref[:, HD:] = d_value
            else:
                ref[:, :HD] += d_keys
                ref[:, HD:] += d_value
        d_turned = turn_back(d_query * FACTOR, cos_ref[0], sin_ref[0])
        back, terms = rms_back(d_turned, raw_ref[0, :, at], g_q)
        dq_ref[:, at] = back.astype(BF)
        total_q = terms if total_q is None else total_q + terms
    t_q[...] = total_q
    for ref, value in zip(back_refs, sums):
        ref[...] = value[...].astype(BF)


def project_back_kernel(count, chained, *refs):
    parts, refs = refs[:count], refs[count:]
    raw_ref, dq_ref, cos_ref, sin_ref, w_ref, x_ref, dh_ref, gains = refs[:8]
    g_in, g_k = gains[0:1], gains[5:6, :HD]
    in_ref, d_ref, t_in, t_k = refs[-4:]
    qd = dq_ref.shape[-1]
    own = add_up(parts)
    d_turned = turn_back(own[:, :HD], cos_ref[0], sin_ref[0])
    back, terms = rms_back(d_turned, raw_ref[0], g_k)
    t_k[...] = terms
    d_ref[:, :qd] = dq_ref[...]
    d_ref[:, qd : qd + HD] = back.astype(BF)
    d_ref[:, qd + HD :] = own[:, HD:].astype(BF)
    d_normed = dot(d_ref[...], w_ref[...], NT)
    back, terms = rms_back(d_normed, x_ref[0, 0].astype(F32), g_in)
    t_in[...] = terms
    in_ref[0, 0] = dh_ref[...] + back


def weights_kernel(short, wrows, micro, core, *refs):
    normed, d_raw, terms = refs[0], refs[1 : 1 + micro], refs[1 + micro : 1 + 7 * micro]
    mine, other, total = refs[1 + 7 * micro :]
    width = normed.shape[-1]
    ind = d_raw[0].shape[-1]
    weights = None
    for index in range(micro):
        term = dot(normed[index], d_raw[index][...], TN)
        weights = term if weights is None else weights + term
    total[:, :ind] = weights
    sums = []
    for kind in range(6):
        value = terms[kind * micro][...]
        for index in range(1, micro):
            value = value + terms[kind * micro + index][...]
        sums.append(value)
    place = spots(short, wrows, width)
    heads = [dot(jnp.broadcast_to(s, (8, HD)).astype(BF), place, NT)[:1] for s in sums[4:]]
    rows = jnp.concatenate(sums[:4] + heads + [jnp.zeros((LANES - 6, width), F32)], axis=0)
    total[:, ind:] = jnp.transpose(rows)
    odd = core[0] == 1
    for index in range(mine.shape[0] // wrows):
        at = slice(index * wrows, (index + 1) * wrows)
        first = total[2 * index * wrows : (2 * index + 1) * wrows]
        second = total[(2 * index + 1) * wrows : (2 * index + 2) * wrows]
        mine[at] = jnp.where(odd, second, first).astype(BF)
        other[at] = jnp.where(odd, first, second).astype(BF)


def on_value(scalar, count, body):
    for value in range(count):

        @pl.when(scalar == value)
        def _(value=value):
            body(value)


def line_kernel(place, *refs):
    blocks, out = refs[:-1], refs[-1]
    count, rows = len(blocks), blocks[0].shape[1]

    def body(d):
        for by, ref in enumerate(blocks):
            at = (d - by) % count
            out[at * rows : (at + 1) * rows] = ref[0]

    on_value(place[0], count, body)


def terms_kernel(count, kinds, has_got, *refs):
    lefts, rights, refs = refs[:count], refs[count : count + count * kinds], refs[count + count * kinds :]
    gots, outs = refs[: kinds if has_got else 0], refs[-kinds:]
    for kind in range(kinds):
        total = None
        for left, right in zip(lefts, rights[kind * count :]):
            term = dot(left[...], right[...], TN)
            total = term if total is None else total + term
        total = total[: outs[kind].shape[0]]
        if has_got:
            total = total + gots[kind][...].astype(F32)
        outs[kind][...] = total.astype(BF)


def fold_chips_kernel(dp, place, mine, got, line, *sends):
    chips = len(sends) + 1
    rows = line.shape[0] // dp

    def body(chip):
        for index in range(dp):
            for bit in range(chips):
                start = (index * chips + (chip ^ bit)) * rows
                value = mine[start : start + rows].astype(F32) + got[start : start + rows].astype(F32)
                at = slice(index * rows, (index + 1) * rows)
                if bit:
                    sends[bit - 1][at] = value.astype(BF)
                else:
                    line[at] = value

    on_value(place[0], chips, body)


def fold_line_kernel(dp, count, place, *refs):
    parts, (own, *sends) = refs[:count], refs[count:]
    rows = own.shape[0]

    def body(d):
        for by in range(dp):
            start = (d + by) % dp * rows
            value = parts[0][start : start + rows]
            for part in parts[1:]:
                value = value + part[start : start + rows].astype(F32)
            if by:
                sends[by - 1][...] = value.astype(BF)
            else:
                own[...] = value

    on_value(place[0], dp, body)


def finish_kernel(count, *refs):
    parts, outs = refs[:count], refs[count:]
    total = add_up(parts)
    start = 0
    for out in outs[:-1]:
        out[...] = total[:, start : start + out.shape[1]]
        start += out.shape[1]
    outs[-1][...] = jnp.transpose(total[:, start:])[:8]


def after(value, *others):
    return lax.optimization_barrier((value,) + others)[0]


def xor_permute(value, bit, size):
    return lax.ppermute(value, "seq", [(i, i ^ bit) for i in range(size)])


def from_behind(value, by, size):
    pairs = [(i, i + by) for i in range(size) if 0 <= i + by < size]
    return lax.ppermute(value, "seq", pairs)


def near_blocks(own, size):
    return [xor_permute(own, bit, size) for bit in (2, 4, 6)]


class Order:
    def __init__(self):
        self.last = None

    def behind(self, value):
        return value if self.last is None else after(value, self.last)

    def step(self, value):
        self.last = value
        return value


def around(value, by, dp):
    return lax.ppermute(value, "dp", [(i, (i + by) % dp) for i in range(dp)])


def along(value, by, dp):
    return lax.ppermute(value, "dp", [(i, i + by) for i in range(dp) if 0 <= i + by < dp])


def add_up_arrays(parts):
    return functools.reduce(lambda a, b: a + b.astype(F32), parts[1:], parts[0])


VMEM = pl.BlockSpec(memory_space=pltpu.VMEM)
SMEM = pl.BlockSpec(memory_space=pltpu.SMEM)


def plain(array):
    return (array, VMEM)


def fold_chips(mine, got, dp, seq, order):
    dims = (mine.shape[0] * 2 // seq, mine.shape[1])
    chip = order.behind((lax.axis_index("seq") >> 1).reshape(1))
    line, *sends = call(
        functools.partial(fold_chips_kernel, dp),
        None,
        [(chip, SMEM), plain(mine), plain(got)],
        [(shape(dims, F32), VMEM)] + [(shape(dims, BF), VMEM)] * 3,
        name="fold_chips",
    )
    order.step(sends)
    return [line] + [xor_permute(send, bit, seq) for send, bit in zip(sends, (2, 4, 6))]


def fold_line(parts, dp, order):
    dims = (parts[0].shape[0] // dp, parts[0].shape[1])
    place = order.behind(lax.axis_index("dp").reshape(1))
    own, *sends = call(
        functools.partial(fold_line_kernel, dp, len(parts)),
        None,
        [(place, SMEM)] + [plain(part) for part in parts],
        [(shape(dims, F32), VMEM)] + [(shape(dims, BF), VMEM)] * (dp - 1),
        name="fold_line",
    )
    order.step(sends)
    return [own] + [around(send, by, dp) for by, send in enumerate(sends, 1)]


def shards(
    dp,
    seq,
    layer_input,
    out_cotangent,
    seq_lengths,
    inputnorm,
    queryproj,
    keyproj,
    valueproj,
    querynorm,
    keynorm,
    outproj,
    attnnorm,
    prefeednorm,
    gateproj,
    upproj,
    downproj,
    postfeednorm,
):
    micro, _, rows, width = layer_input.shape
    devices = dp * seq
    wrows = width // devices
    qd = queryproj.shape[1]
    ind = qd + 2 * HD
    ff = gateproj.shape[1]
    chunk = ff // devices
    own_ff = dp * chunk
    pad = -(-own_ff // LANES) * LANES
    reach = WINDOW // rows
    split = seq == 8 and dp == 4

    base = lax.axis_index("seq") * rows
    positions = base + jnp.arange(rows, dtype=jnp.int32)
    inverse = jnp.power(F32(10000.0), -2.0 * jnp.arange(HALF, dtype=F32) / HD)
    lengths = seq_lengths[:, 0, 0]
    relative = positions[None, :] & (lengths[:, None] - 1)
    angles = relative.astype(F32)[:, :, None] * inverse
    cosine, sine = jnp.cos(angles), jnp.sin(angles)

    order = Order()
    short = querynorm.shape[0]
    fill = (0, wrows - short)
    gains = [inputnorm, attnnorm, prefeednorm, postfeednorm, jnp.pad(querynorm, fill), jnp.pad(keynorm, fill)]
    gains = jnp.pad(jnp.stack(gains, axis=1), ((0, 0), (0, LANES - len(gains))))
    packed = jnp.concatenate([queryproj, keyproj, valueproj, gains], axis=1)
    along_dp = lax.axis_index("dp").reshape(1)
    if split:
        orows = outproj.shape[0]
        both = jnp.concatenate([packed, jnp.pad(outproj, ((0, wrows - orows), (0, 0)))], axis=1)
        both = order.step(lax.optimization_barrier(both[None]))
        line = [around(both, by, dp) for by in range(1, dp)]

    [gate_up] = call(
        functools.partial(owner_kernel, dp),
        None,
        [plain(gateproj), plain(upproj)],
        [(shape((seq, wrows, 2 * pad), BF), VMEM)],
        name="owner",
    )
    w_down = lax.all_gather(downproj, "dp", axis=0, tiled=True)
    if split:
        gate_up, cosine, sine, line[0] = order.step(order.behind((gate_up, cosine, sine, line[0])))
    gate_up = lax.all_to_all(gate_up, "seq", 0, 0).reshape(seq * wrows, 2 * pad)
    if split:
        [line] = call(
            line_kernel,
            None,
            [(along_dp, SMEM)] + [plain(block) for block in [both] + order.behind(line)],
            [(shape((dp * wrows, both.shape[2]), BF), VMEM)],
            name="line",
        )
        lines = [line] + near_blocks(order.step(line), seq)
        lines = order.step(order.behind(lines))
        others = [xor_permute(line, 1, seq) for line in lines]
        others, w_down = order.step(order.behind((others, w_down)))
        w_in, w_out = call(
            functools.partial(untangle_kernel, dp, seq),
            None,
            [(lax.axis_index("seq").reshape(1), SMEM)] + [plain(line) for line in lines + others],
            [(shape((width, ind + LANES), BF), VMEM), (shape((qd, width), BF), VMEM)],
            name="untangle",
        )
    else:
        w_in = lax.all_gather(packed[None], BOTH, axis=0, tiled=True).reshape(width, -1)
        w_out = lax.all_gather(outproj, BOTH, axis=0, tiled=True)
    w_gu = [lax.all_gather(gate_up, "dp", axis=0, tiled=True)]
    [w_down] = call(
        pad_kernel, None, [plain(order.behind(w_down))], [(shape((pad, width), BF), VMEM)], name="pad"
    )
    w_down = [order.step(w_down)]
    if split:
        w_down = order.step(order.behind(w_down + [xor_permute(w_down[0], 1, seq)]))

    def of_micro(array, index):
        dims = array.shape[1:]
        return (array, pl.BlockSpec((1,) + dims, lambda *_: (index,) + (0,) * len(dims)))

    def full(array):
        return (array, whole(array))

    def new(dims, dtype):
        return (shape(dims, dtype), pl.BlockSpec(dims, lambda *_: (0,) * len(dims)))

    smem = pl.BlockSpec(memory_space=pltpu.SMEM)
    each = lambda *dims: pl.BlockSpec((1,) + dims, lambda i: (i,) + (0,) * len(dims))
    w_in_spec = pl.BlockSpec((width, ind), lambda *_: (0, 0))

    cosine = order.behind(cosine)
    gains_spec = pl.BlockSpec((width, LANES), lambda *_: (0, ind // LANES))
    normed_in, raw, query, pair, gains = call(
        functools.partial(project_kernel, short, wrows),
        (micro,),
        [(layer_input, each(1, rows, width)), (w_in, w_in_spec), (w_in, gains_spec)]
        + [(cosine, each(rows, HALF)), (sine, each(rows, HALF))],
        [
            (shape((micro, rows, width), BF), each(rows, width)),
            (shape((micro, rows, qd + HD), F32), each(rows, qd + HD)),
            (shape((micro, rows, qd), BF), each(rows, qd)),
            (shape((micro, rows, 2 * HD), BF), each(rows, 2 * HD)),
            new((8, width), F32),
        ],
        name="project",
    )

    order.step(pair)
    behind = [from_behind(pair, by, seq) for by in range(1, reach + 1)]
    states = []
    for index in range(micro):
        place = order.behind(jnp.stack([lengths[index], base]))
        pairs = [of_micro(p, index) for p in [pair] + behind]
        attended, attn_out, hidden, normed_ffn = call(
            functools.partial(attend_kernel, reach),
            (1,),
            [(place, smem), of_micro(layer_input, index), of_micro(query, index)]
            + pairs
            + [full(w_out), full(gains)],
            [new((rows, qd), BF), new((rows, width), F32), new((rows, width), F32), new((rows, width), BF)],
            name="attend",
        )
        order.step(normed_ffn)
        s = dict(place=place, pairs=pairs, attended=attended, attn_out=attn_out, hidden=hidden)
        s["sent"] = near_blocks(normed_ffn, seq) if split else None
        s["nf"] = normed_ffn
        states.append(s)

    if split:
        states[0]["sent"] = order.step(order.behind(states[0]["sent"]))
        w_gu.append(xor_permute(order.step(order.behind(w_gu[0])), 1, seq))
    halves = len(w_gu)

    def blocks(array):
        return (array, pl.BlockSpec((rows, array.shape[1]), lambda i: (i, 0)))

    def made(count, columns):
        return (shape((count, columns), BF), pl.BlockSpec((rows, columns), lambda i: (i, 0)))

    def fixed(array):
        return (array, pl.BlockSpec(array.shape, lambda *_: (0,) * array.ndim, pipeline_mode=pl.Buffered(1)))

    def block(index_of, columns):
        return pl.BlockSpec((rows, columns), index_of)

    any_spec = pl.BlockSpec(memory_space=pl.ANY)

    def ffn(pieces):
        if not split:
            count = pieces[0].shape[0] // rows
            results = call(
                functools.partial(ffn_grid_kernel, halves),
                (count,),
                [blocks(pieces[0])] + [fixed(w) for w in w_gu] + [fixed(w) for w in w_down],
                [made(count * rows, pad)] * 3 + [made(count * rows, width)],
                name="ffn",
            )
            return pieces[0], results[:1], results[1:2], results[2:3], results[3:]
        count = len(pieces)
        results = call(
            functools.partial(ffn_kernel, count, halves),
            None,
            [plain(array) for array in pieces + list(w_gu) + list(w_down)],
            [(shape((count * rows, width), BF), any_spec)]
            + [(shape((count * rows, pad), BF), any_spec)] * (3 * halves)
            + [(shape((rows, width), BF), VMEM)] * count,
            scratch=[pltpu.VMEM((count * rows, pad), BF)] * (3 * halves)
            + [pltpu.SemaphoreType.DMA((count * (1 + 3 * halves),))],
            name="ffn",
        )
        kinds = [results[1 + i * halves : 1 + (i + 1) * halves] for i in range(3)]
        return results[0], *kinds, results[1 + 3 * halves :]

    def ffn_backward(pieces, gate, up):
        if not split:
            count = pieces[0].shape[0] // rows
            results = call(
                functools.partial(ffn_back_grid_kernel, halves),
                (count,),
                [blocks(pieces[0]), *map(blocks, gate), *map(blocks, up)]
                + [fixed(w) for w in w_gu]
                + [fixed(w) for w in w_down],
                [made(count * rows, pad)] * 2 + [made(count * rows, width)],
                name="ffn_back",
            )
            return pieces[0], results[:1], results[1:2], results[2:]
        count = len(pieces)
        results = call(
            functools.partial(ffn_back_kernel, count, halves),
            None,
            [plain(piece) for piece in pieces]
            + [(array, any_spec) for array in [*gate, *up]]
            + [plain(array) for array in list(w_gu) + list(w_down)],
            [(shape((count * rows, width), BF), any_spec)]
            + [(shape((count * rows, pad), BF), any_spec)] * (2 * halves)
            + [(shape((rows, width), BF), VMEM)] * count,
            scratch=[pltpu.VMEM((count * rows, pad), BF)] * (4 * halves)
            + [pltpu.SemaphoreType.DMA((count * (1 + 2 * halves),)), pltpu.SemaphoreType.DMA((count * 2 * halves,))],
            name="ffn_back",
        )
        return results[0], results[1 : 1 + halves], results[1 + halves : 1 + 2 * halves], results[1 + 2 * halves :]

    def pieces_of(own, near):
        if not split:
            return [lax.all_gather(order.behind(own), "seq", axis=0, tiled=True)]
        return [order.behind(own)] + list(near)

    def scatter(parts):
        if not split:
            return [lax.psum_scatter(parts[0], "seq", scatter_dimension=0, tiled=True)]
        return [parts[0]] + [xor_permute(part, bit, seq) for part, bit in zip(parts[1:], (2, 4, 6))]

    for s in states:
        pieces = pieces_of(s["nf"], s["sent"])
        s["tokens"], s["gate"], s["up"], s["act"], parts = ffn(pieces)
        order.step(parts)
        s["terms"] = scatter(parts)

    layer_out = None
    result = shape((micro, 1, rows, width), F32)
    for index, s in enumerate(states):
        parts = s["terms"]
        chain = [] if layer_out is None else [(layer_out, pl.BlockSpec(memory_space=pl.ANY))]
        layer_out, s["d_ffn"], s["t_post"] = call(
            functools.partial(middle_kernel, len(parts), bool(chain)),
            (1,),
            [full(p) for p in parts]
            + [of_micro(out_cotangent, index), full(s["hidden"]), full(order.behind(gains))]
            + chain,
            [(result, of_micro(result, index)[1]), new((rows, width), BF), new((1, width), F32)],
            aliases={len(parts) + 3: 0} if chain else None,
            name="middle",
        )
        order.step(s["d_ffn"])
        s["sent"] = near_blocks(s["d_ffn"], seq) if split else None

    def join(pieces):
        [joined] = call(
            join_kernel,
            None,
            [(piece, any_spec) for piece in pieces],
            [(shape((len(pieces) * rows, width), BF), any_spec)],
            scratch=[pltpu.SemaphoreType.DMA((len(pieces),))],
            name="join",
        )
        return joined

    def over_tokens(left, rights, half, gots=(), high_out=None):
        of = lambda s, name: s[name] if name in ("tokens", "d_tokens") else s[name][half]
        lefts = order.behind([of(s, left) for s in states])
        others = [of(s, right) for right in rights for s in states]
        count, high, wide = lefts[0].shape[0], lefts[0].shape[1], others[0].shape[1]
        by_rows = high % 384 == 0
        moving = lambda columns: pl.BlockSpec((count, columns), lambda i: (0, i))
        staying = lambda columns: pl.BlockSpec((count, columns), lambda i: (0, 0), pipeline_mode=pl.Buffered(1))
        if by_rows:
            steps, left_spec, right_spec = high // 384, moving(384), staying(wide)
            out_spec = pl.BlockSpec((384, wide), lambda i: (i, 0))
        else:
            steps, left_spec, right_spec = wide // 384, staying(high), moving(384)
            out_spec = pl.BlockSpec((high_out or high, 384), lambda i: (0, i))
        results = call(
            functools.partial(terms_kernel, micro, len(rights), bool(gots)),
            (steps,),
            [(a, left_spec) for a in lefts] + [(b, right_spec) for b in others] + [(got, out_spec) for got in gots],
            [(shape((high_out or high, wide), BF), out_spec)] * len(rights),
            name="terms",
        )
        return order.step(results)

    def weight_terms(left, rights, high_out=None, meanwhile=None):
        if not split:
            if meanwhile is not None:
                meanwhile()
            yield from over_tokens(left, rights, 0, (), high_out)
            return
        others = over_tokens(left, rights, 1, (), high_out)
        if meanwhile is not None:
            meanwhile()
            others = order.behind(others)
        gots = [xor_permute(other, 1, seq) for other in others]
        if meanwhile is not None:
            attend_back(micro - 1)
        for right, got in zip(rights, gots):
            yield over_tokens(left, [right], 0, [got], high_out)[0]

    def ffn_back(s):
        pieces = pieces_of(s["d_ffn"], s["sent"])
        tokens, s["d_gate"], s["d_up"], parts = ffn_backward(pieces, s["gate"], s["up"])
        s.setdefault("d_tokens", tokens)
        order.step(parts)
        s["terms"] = scatter(parts)

    for s in states[:-1]:
        ffn_back(s)
    late = states[-1]
    if split:
        late["sent"] = order.step(order.behind(late["sent"]))
        late["d_tokens"] = order.step(join([late["d_ffn"]] + list(late["sent"])))
        down_terms = next(weight_terms("act", ["d_tokens"], own_ff))
        ffn_back(late)
    else:
        ffn_back(late)
        down_terms = next(weight_terms("act", ["d_tokens"], own_ff))
    down_grad = lax.psum_scatter(down_terms, "dp", scatter_dimension=0, tiled=True)
    for s in states[:-1]:
        s["terms"] = order.step(order.behind(s["terms"]))

    def attend_back(index):
        s = states[index]
        parts = s["terms"]
        backs = call(
            functools.partial(attend_back_kernel, reach, len(parts)),
            (1,),
            [(order.behind(s["place"]), smem)]
            + [full(p) for p in parts]
            + [of_micro(out_cotangent, index), full(s["hidden"]), full(s["attn_out"]), of_micro(query, index)]
            + [of_micro(raw, index), of_micro(cosine, index), of_micro(sine, index)]
            + [full(w_out), full(gains)]
            + s["pairs"],
            [new((rows, width), F32), new((rows, width), BF), new((rows, qd), BF)]
            + [new((1, width), F32), new((1, width), F32), new((1, HD), F32)]
            + [new((rows, 2 * HD), BF)] * reach
            + [new((rows, 2 * HD), F32)],
            scratch=[pltpu.VMEM((rows, 2 * HD), F32)] * reach,
            name="attend_back",
        )
        s["d_hidden"], s["d_attn"], s["d_raw_q"], s["t_pre"], s["t_attn"], s["t_query"] = backs[:6]
        order.step(s["d_attn"])
        sent, own = backs[6 : 6 + reach], backs[-1]
        s["d_pairs"] = [own] + [from_behind(value, -by, seq) for by, value in enumerate(sent, 1)]

    def project_back(index, input_grad):
        s = states[index]
        terms = s["d_pairs"]
        chain = [] if input_grad is None else [(input_grad, pl.BlockSpec(memory_space=pl.ANY))]
        keys_spec = pl.BlockSpec((1, rows, HD), lambda *_: (index, 0, qd // HD))
        input_grad, s["d_raw"], s["t_in"], s["t_keys"] = call(
            functools.partial(project_back_kernel, len(terms), bool(chain)),
            (1,),
            [full(t) for t in terms]
            + [(raw, keys_spec), full(s["d_raw_q"]), of_micro(cosine, index), of_micro(sine, index), (w_in, w_in_spec)]
            + [of_micro(layer_input, index), full(s["d_hidden"]), full(order.behind(gains))]
            + chain,
            [(result, of_micro(result, index)[1]), new((rows, ind), BF), new((1, width), F32), new((1, HD), F32)],
            aliases={len(terms) + 8: 0} if chain else None,
            name="project_back",
        )
        order.step(s["d_raw"])
        s["normed_in"] = normed_in[index]
        return input_grad

    def to_columns(part):
        part = lax.all_to_all(part.reshape(seq, wrows, pad), "seq", 0, 0)
        [columns] = call(
            functools.partial(columns_kernel, dp),
            None,
            [plain(part)],
            [(shape((wrows, ff), F32), VMEM)],
            name="columns",
        )
        return columns

    input_grad = None
    scattered = lambda terms: lax.psum_scatter(terms, "dp", scatter_dimension=0, tiled=True)
    def meanwhile():
        for index in range(micro - 1):
            attend_back(index)
        nonlocal down_grad
        down_grad, states[-1]["terms"] = order.step(order.behind((down_grad, states[-1]["terms"])))

    gate_up_terms = weight_terms("tokens", ["d_gate", "d_up"], None, meanwhile)
    gate_sum = scattered(next(gate_up_terms))
    if not split:
        attend_back(micro - 1)
    core = lax.axis_index("seq") & 1
    out_terms = order.step(sum(dot(s["attended"], order.behind(s["d_attn"]), TN) for s in states).astype(BF))
    if split:
        view = out_terms.reshape(devices // 2, 2, qd // devices, width)
        mine, other = (
            lax.dynamic_index_in_dim(view, at.astype(jnp.uint32), 1, keepdims=False).reshape(-1, width)
            for at in (core, 1 - core)
        )
        got = xor_permute(other, 1, seq)
    input_grad = project_back(micro - 1, input_grad)
    if split:
        out_parts = fold_chips(mine, got, dp, seq, order)
    else:
        out_grad = lax.psum_scatter(out_terms, BOTH, scatter_dimension=0, tiled=True).astype(F32)
    for index in range(micro - 1):
        input_grad = project_back(index, input_grad)
    up_sum = scattered(next(gate_up_terms))
    if split:
        out_parts = fold_line(out_parts, dp, order)
    sums = [s[name] for name in ("t_in", "t_attn", "t_pre", "t_post", "t_query", "t_keys") for s in states]
    half_out = (shape((devices // 2 * wrows, ind + LANES), BF), VMEM)
    mine, other = call(
        functools.partial(weights_kernel, short, wrows, micro),
        None,
        [(order.behind((core if split else jnp.int32(0)).reshape(1)), smem), plain(normed_in)]
        + [plain(s["d_raw"]) for s in states]
        + [plain(term) for term in sums],
        [half_out, half_out],
        scratch=[pltpu.VMEM((width, ind + LANES), F32)],
        name="weights",
    )
    order.step(other)
    if split:
        got = xor_permute(other, 1, seq)
        in_parts = fold_chips(mine, got, dp, seq, order)
        out_grad = order.step(add_up_arrays(order.behind(out_parts)))
        gate_grad = order.step(to_columns(gate_sum))
        in_parts = fold_line(in_parts, dp, order)
        up_grad = to_columns(order.behind(up_sum))
    else:
        halves_of = [part.reshape(devices // 2, wrows, -1) for part in (mine, other)]
        whole_terms = jnp.stack(halves_of, axis=1).reshape(devices, wrows, -1)
        in_parts = [lax.psum_scatter(whole_terms, BOTH, scatter_dimension=0, tiled=True)[0]]
    q_grad, k_grad, v_grad, gain_sum = call(
        functools.partial(finish_kernel, len(in_parts)),
        None,
        [plain(part) for part in in_parts],
        [(shape((wrows, columns), F32), VMEM) for columns in (qd, HD, HD)] + [(shape((8, wrows), F32), VMEM)],
        name="finish",
    )

    if not split:
        gate_grad, up_grad = to_columns(gate_sum), to_columns(up_sum)
    down_grad = order.behind(down_grad).astype(F32)

    return (
        layer_out,
        input_grad,
        gain_sum[0],
        q_grad,
        k_grad,
        v_grad,
        gain_sum[4, :short],
        gain_sum[5, :short],
        out_grad,
        gain_sum[1],
        gain_sum[2],
        gate_grad,
        up_grad,
        down_grad,
        gain_sum[3],
    )


def solution(mesh):
    dp, seq = mesh.shape["dp"], mesh.shape["seq"]
    acts = P(None, "dp", "seq", None)
    vector = P(BOTH)
    matrix = P(BOTH, None)
    weights = (vector,) + (matrix,) * 3 + (vector,) * 2 + (matrix, vector, vector) + (matrix,) * 3 + (vector,)
    return jax.shard_map(
        functools.partial(shards, dp, seq),
        mesh=mesh,
        in_specs=(acts, acts, P(None, "dp", None)) + weights,
        out_specs=(acts, acts) + weights,
        check_vma=False,
    )
```

time: 924 us -> 681 us (0.74)
  Pallas kernels: 0 us -> 335 us
  waiting for transfers between devices: 444 us -> 173 us
  matrix products: 190 us -> 1.8 us
  other arithmetic: 88.4 us -> 6.2 us
  local copies, waits for them, and re-layouts: 109 us -> 38.1 us
  blocking collectives: 0 us -> 20.1 us
  starting transfers between devices: 64.2 us -> 83.6 us
    pallas_call x0 -> x31, Pallas kernels: none -> 335 us  [call(): pl.pallas_call(body, **{} if grid is None else {'grid': grid}, in_specs=[...]
    dot_general x37 -> x2, matrix products: 190 us -> 1.8 us  [dot(): lax.dot_general(left, right, (dims, ((), ())), preferred_element_type=F32)]
    unnamed x10 -> x5, waiting for transfers between devices: 141 us -> 0.75 us
    all_gather x3 -> x1, waiting for transfers between devices: 67.4 us -> 0.01 us  [shards(): w_gu = [lax.all_gather(gate_up, 'dp', axis=0, tiled=True)]]
    reduce_scatter x2, waiting for transfers between devices: 56.6 us -> 0.01 us  [shards(): lax.psum_scatter(terms, 'dp', scatter_dimension=0, tiled=True)]
    ppermute x32 -> x44, waiting for transfers between devices: 151 us -> 115 us  [xor_permute(): return lax.ppermute(value, 'seq', [(i, i ^ bit) for i in range(size)])]
    ppermute x0 -> x9, waiting for transfers between devices: none -> 27.1 us  [around(): return lax.ppermute(value, 'dp', [(i, (i + by) % dp) for i in range(dp)])]
    all_gather x1, waiting for transfers between devices: 21 us -> 0.01 us  [shards(): w_down = lax.all_gather(downproj, 'dp', axis=0, tiled=True)]
  transfers between devices with their start and end apart: 50 -> 66, of which waited for: 24 -> 26; matrix products, arithmetic and copies ran while one was open for 33% -> 3% of each run, Pallas kernels for 0% -> 34%
where the time goes in v2:
time: 681 us; the launch traced here: 673 us
  Pallas kernels  335 us (49%)
  waiting for transfers between devices  173 us (25%)
  starting transfers between devices  83.6 us (12%)
  local copies, waits for them, and re-layouts  38.1 us (6%)
  blocking collectives  20.1 us (3%)
  between operations  14.9 us (2%)
    pallas_call x31, Pallas kernels, call(): pl.pallas_call(body, **{} if grid is None else {'grid': grid}, in_specs=[...  335 us
    ppermute x44, waiting for transfers between devices, xor_permute(): return lax.ppermute(value, 'seq', [(i, i ^ bit) for i in range(size)])  115 us
    ppermute x44, starting transfers between devices, xor_permute(): return lax.ppermute(value, 'seq', [(i, i ^ bit) for i in range(size)])  45.1 us
    ppermute x9, waiting for transfers between devices, around(): return lax.ppermute(value, 'dp', [(i, (i + by) % dp) for i in range(dp)])  27.1 us
    unnamed x142, local copies, waits for them, and re-layouts  26.3 us
    ppermute x9, starting transfers between devices, around(): return lax.ppermute(value, 'dp', [(i, (i + by) % dp) for i in range(dp)])  20.5 us
    all_to_all x1, blocking collectives, shards(): gate_up = lax.all_to_all(gate_up, 'seq', 0, 0).reshape(seq * wrows, 2 * pad)  20.1 us
    ppermute x6, waiting for transfers between devices, from_behind(): return lax.ppermute(value, 'seq', pairs)  19.6 us
  transfers between devices with their start and end apart: 66, of which 26 were waited for; matrix products, arithmetic and copies ran while one was open for 3% of the time, Pallas kernels for 34%

profile of v2, /device:TPU:0, one launch (start us, length us, event | category | flops | bytes accessed | tf_op | source)
XLA Modules:
  0.0 672.8 jit_solution(18237279710974855552)
XLA Ops:
  23.5 20.1 %all_to_all.15 = bf16[8,36,1792]{2,1,0:T(8,128)(2,1)S(1)} all-to-all(bf16[8,36,1792]{2,1,0:T(8,128)(2,1)} %owner.1), channel_id=1, replica_groups=mesh['dp'=4,'seq'=8] {'seq'}, dimensions={0} | all-to-all | bytes 2064384 | tf_op jit(solution)/shard_map/all_to_all | solution.py:666
  46.8 18.9 %collective-permute-done.1.refs_2_ = bf16[1,36,2816]{2,1,0:T(8,128)(2,1)S(1)} collective-permute-done((bf16[1,36,2816]{2,1,0:T(8,128)(2,1)S(1)}, bf16[1,36,2816]{2,1,0:T(8,128)(2,1)S(1)}, u32[]{:S(2)}, u32[]{:S(2)}) %collective-permute-start.1) | collective-permute-done | bytes 202784 | tf_op jit(solution)/shard_map/ppermute | solution.py:556
  72.2 17.7 %collective-permute-done.3.refs_1_ = bf16[144,2816]{1,0:T(8,128)(2,1)S(1)} collective-permute-done((bf16[144,2816]{1,0:T(8,128)(2,1)}, bf16[144,2816]{1,0:T(8,128)(2,1)S(1)}, u32[]{:S(2)}, u32[]{:S(2)}) %collective-permute-start.3) | collective-permute-done | bytes 811040 | tf_op jit(solution)/shard_map/ppermute | solution.py:531
  89.9 17.6 %collective-permute-done.4.refs_2_ = bf16[144,2816]{1,0:T(8,128)(2,1)S(1)} collective-permute-done((bf16[144,2816]{1,0:T(8,128)(2,1)}, bf16[144,2816]{1,0:T(8,128)(2,1)S(1)}, u32[]{:S(2)}, u32[]{:S(2)}) %collective-permute-start.4) | collective-permute-done | bytes 811040 | tf_op jit(solution)/shard_map/ppermute | solution.py:531
  123.7 7.7 %project.1 = (bf16[2,256,1152]{2,1,0:T(8,128)(2,1)}, f32[2,256,1280]{2,1,0:T(8,128)}, bf16[2,256,1024]{2,1,0:T(8,128)(2,1)}, bf16[2,256,512]{2,1,0:T(8,128)(2,1)}, f32[8,1152]{1,0:T(8,128)}) custom-call(bf16[2,1,256,1152]{3,2,1,0:T(8,128)(2,1)} %refs_8_.3, bf16[1152,1664]{1,0:T(8,128)(2,1)} %get-tuple-element.213.w_ref.packed_ref.refs_7_, ...), custom_call_target="tpu_custom_call" | custom-call | bytes 1 | tf_op jit(solution)/shard_map/project/pallas_call | solution.py:42
  138.8 10.7 %collective-permute-done.12.rest_2_.refs_15_ = bf16[2,256,512]{2,1,0:T(8,128)(2,1)S(1)} collective-permute-done((bf16[2,256,512]{2,1,0:T(8,128)(2,1)}, bf16[2,256,512]{2,1,0:T(8,128)(2,1)S(1)}, u32[]{:S(2)}, u32[]{:S(2)}) %collective-permute-start.12) | collective-permute-done | bytes 524320 | tf_op jit(solution)/shard_map/ppermute | solution.py:536
  174.0 12.9 %collective-permute-done.15.refs_3_ = bf16[256,1152]{1,0:T(8,128)(2,1)S(1)} collective-permute-done((bf16[256,1152]{1,0:T(8,128)(2,1)}, bf16[256,1152]{1,0:T(8,128)(2,1)S(1)}, u32[]{:S(2)}, u32[]{:S(2)}) %collective-permute-start.15) | collective-permute-done | bytes 589856 | tf_op jit(solution)/shard_map/ppermute | solution.py:531
  198.0 22.7 %ffn.2 = (bf16[1024,1152]{1,0:T(8,128)(2,1)}, bf16[1024,896]{1,0:T(8,128)(2,1)}, bf16[1024,896]{1,0:T(8,128)(2,1)}, bf16[1024,896]{1,0:T(8,128)(2,1)}, bf16[1024...) custom-call(bf16[256,1152]{1,0:T(8,128)(2,1)} %get-tuple-element.231, ...), custom_call_target="tpu_custom_call" | custom-call | bytes 1 | tf_op jit(solution)/shard_map/ffn/pallas_call | solution.py:42
  224.3 22.4 %ffn.3 = (bf16[1024,1152]{1,0:T(8,128)(2,1)}, bf16[1024,896]{1,0:T(8,128)(2,1)}, bf16[1024,896]{1,0:T(8,128)(2,1)}, bf16[1024,896]{1,0:T(8,128)(2,1)}, bf16[1024...) custom-call(bf16[256,1152]{1,0:T(8,128)(2,1)} %get-tuple-element.236, ...), custom_call_target="tpu_custom_call" | custom-call | bytes 1 | tf_op jit(solution)/shard_map/ffn/pallas_call | solution.py:42
  265.3 11.2 %collective-permute-done.21.refs_2_ = bf16[256,1152]{1,0:T(8,128)(2,1)S(1)} collective-permute-done((bf16[256,1152]{1,0:T(8,128)(2,1)}, bf16[256,1152]{1,0:T(8,128)(2,1)S(1)}, u32[]{:S(2)}, u32[]{:S(2)}) %collective-permute-start.21) | collective-permute-done | bytes 589856 | tf_op jit(solution)/shard_map/ppermute | solution.py:531
  290.6 11.2 %collective-permute-done.27.refs_2_ = bf16[256,1152]{1,0:T(8,128)(2,1)S(1)} collective-permute-done((bf16[256,1152]{1,0:T(8,128)(2,1)}, bf16[256,1152]{1,0:T(8,128)(2,1)S(1)}, u32[]{:S(2)}, u32[]{:S(2)}) %collective-permute-start.27) | collective-permute-done | bytes 589856 | tf_op jit(solution)/shard_map/ppermute | solution.py:531
  302.8 30.2 %ffn_back.2 = (bf16[1024,1152]{1,0:T(8,128)(2,1)}, bf16[1024,896]{1,0:T(8,128)(2,1)}, bf16[1024,896]{1,0:T(8,128)(2,1)}, bf16[1024,896]{1,0:T(8,128)(2,1)}, bf16...) custom-call(bf16[256,1152]{1,0:T(8,128)(2,1)} %get-tuple-element.251, ...), custom_call_target="tpu_custom_call" | custom-call | bytes 1 | tf_op jit(solution)/shard_map/ffn_back/pallas_call | solution.py:42
  334.2 72.6 %join.1.refs_3_ = bf16[1024,1152]{1,0:T(8,128)(2,1)} custom-call(bf16[256,1152]{1,0:T(8,128)(2,1)} %get-tuple-element.272.refs_0_, bf16[256,1152]{1,0:T(8,128)(2,1)} %copy-done.4, bf16[256,1152]{1,0:T(8,128)(2,1)} %copy-done.5, bf16[256,1152]{1,0:T(8,128)(2,1)} %copy-done.6), custom_call_target="tpu_custom_call" | custom-call | bytes 1 | tf_op jit(solution)/shard_map/join/pallas_call | solution.py:42
  406.9 9.8 %terms.5 = bf16[864,1152]{1,0:T(8,128)(2,1)} custom-call(bf16[1024,896]{1,0:T(8,128)(2,1)} %get-tuple-element.267.refs_0_, bf16[1024,896]{1,0:T(8,128)(2,1)} %get-tuple-element.268.refs_1_, bf16[1024,1152]{1,0:T(8,128)(2,1)} %get-tuple-element.269.refs_2_, bf16[1024,1152]{1,0:T(8,128)(2,1)} %join.1.refs_3_), custom_call_target="tpu_custom_call" | custom-call | bytes 1 | tf_op jit(solution)/shard_map/terms/pallas_call | solution.py:42
  422.2 10.3 %terms.6 = bf16[864,1152]{1,0:T(8,128)(2,1)} custom-call(bf16[1024,896]{1,0:T(8,128)(2,1)} %get-tuple-element.270.refs_0_, bf16[1024,896]{1,0:T(8,128)(2,1)} %get-tuple-element.271.refs_1_, bf16[1024,1152]{1,0:T(8,128)(2,1)} %get-tuple-element.269.refs_2_, bf16[1024,1152]{1,0:T(8,128)(2,1)} %join.1.refs_3_, bf16[864,1152]{1,0:T(8,128)(2,1)} %copy-done.11), custom_call_target="tpu_custom_call" | custom-call | bytes 1 | tf_op jit(solution)/shard_map/terms/pallas_call | solution.py:42
  437.1 30.4 %ffn_back.3 = (bf16[1024,1152]{1,0:T(8,128)(2,1)}, bf16[1024,896]{1,0:T(8,128)(2,1)}, bf16[1024,896]{1,0:T(8,128)(2,1)}, bf16[1024,896]{1,0:T(8,128)(2,1)}, bf16...) custom-call(bf16[256,1152]{1,0:T(8,128)(2,1)} %get-tuple-element.272, ...), custom_call_target="tpu_custom_call" | custom-call | bytes 1 | tf_op jit(solution)/shard_map/ffn_back/pallas_call | solution.py:42
  471.0 15.5 %terms.7 = (bf16[1152,896]{1,0:T(8,128)(2,1)}, bf16[1152,896]{1,0:T(8,128)(2,1)}) custom-call(bf16[1024,1152]{1,0:T(8,128)(2,1)} %get-tuple-element.335.refs_0_, bf16[1024,1152]{1,0:T(8,128)(2,1)} %get-tuple-element.336.refs_1_, bf16[1024,896]{1,0:T(8,128)(2,1)} %get-tuple-element.287.refs_2_, bf16[1024,896]{1,0:T(8,128)(2,1)} %get-tuple-element.288.refs_3_, ...), custom_call_target="tpu_custom_call" | custom-call | bytes 1 | tf_op jit(solution)/shard_map/terms/pallas_call | solution.py:42
  486.6 11.2 %attend_back.2 = (f32[256,1152]{1,0:T(8,128)}, bf16[256,1152]{1,0:T(8,128)(2,1)}, bf16[256,1024]{1,0:T(8,128)(2,1)}, f32[1,1152]{1,0:T(1,128)}, f32[1,1152]{1,0:...) custom-call(s32[2]{0:T(128)} %pad_add_fusion.1.place, ...), custom_call_target="tpu_custom_call" | custom-call | bytes 1 | tf_op jit(solution)/shard_map/attend_back/pallas_call | solution.py:42
  499.0 11.4 %attend_back.3 = (f32[256,1152]{1,0:T(8,128)}, bf16[256,1152]{1,0:T(8,128)(2,1)}, bf16[256,1024]{1,0:T(8,128)(2,1)}, f32[1,1152]{1,0:T(1,128)}, f32[1,1152]{1,0:...) custom-call(s32[2]{0:T(128)} %pad_add_fusion.place, ...), custom_call_target="tpu_custom_call" | custom-call | bytes 1 | tf_op jit(solution)/shard_map/attend_back/pallas_call | solution.py:42
  511.7 9.4 %terms.8 = bf16[1152,896]{1,0:T(8,128)(2,1)} custom-call(bf16[1024,1152]{1,0:T(8,128)(2,1)} %get-tuple-element.335.refs_0_, bf16[1024,1152]{1,0:T(8,128)(2,1)} %get-tuple-element.336.refs_1_, bf16[1024,896]{1,0:T(8,128)(2,1)} %get-tuple-element.318.refs_2_, bf16[1024,896]{1,0:T(8,128)(2,1)} %get-tuple-element.319.refs_3_, bf16[1152,896]{1,0:T(8,128)(2,1)} %copy-done.10), custom_call_target="tpu_custom_call" | custom-call | bytes 1 | tf_op jit(solution)/shard_map/terms/pallas_call | solution.py:42
  530.9 8.9 %collective-permute-done.42.refs_2_ = bf16[256,512]{1,0:T(8,128)(2,1)} collective-permute-done((bf16[256,512]{1,0:T(8,128)(2,1)}, bf16[256,512]{1,0:T(8,128)(2,1)}, u32[]{:S(2)}, u32[]{:S(2)}) %collective-permute-start.42) | collective-permute-done | bytes 262176 | tf_op jit(solution)/shard_map/ppermute | solution.py:536
  556.3 9.4 %terms.9 = bf16[1152,896]{1,0:T(8,128)(2,1)} custom-call(bf16[1024,1152]{1,0:T(8,128)(2,1)} %get-tuple-element.335.refs_0_, bf16[1024,1152]{1,0:T(8,128)(2,1)} %get-tuple-element.336.refs_1_, bf16[1024,896]{1,0:T(8,128)(2,1)} %get-tuple-element.337.refs_2_, bf16[1024,896]{1,0:T(8,128)(2,1)} %get-tuple-element.338.refs_3_, bf16[1152,896]{1,0:T(8,128)(2,1)} %copy-done.9), custom_call_target="tpu_custom_call" | custom-call | bytes 1 | tf_op jit(solution)/shard_map/terms/pallas_call | solution.py:42
  585.9 7.1 %weights.1 = (bf16[576,1664]{1,0:T(8,128)(2,1)}, bf16[576,1664]{1,0:T(8,128)(2,1)}) custom-call(s32[1]{0:T(128)} %bitcast.16.core, bf16[2,256,1152]{2,1,0:T(8,128)(2,1)} %get-tuple-element.346.refs_0_, bf16[256,1536]{1,0:T(8,128)(2,1)} %get-tuple-element.334.refs_1_, bf16[256,1536]{1,0:T(8,128)(2,1)} %get-tuple-element.325.refs_2_, ...), custom_call_target="tpu_custom_call" | custom-call | bytes 1 | tf_op jit(solution)/shard_map/weights/pallas_call | solution.py:42
  624.9 7.6 %all-to-all-done.1.in_ref = bf16[8,36,896]{2,1,0:T(8,128)(2,1)S(1)} async-done(((bf16[8,36,896]{2,1,0:T(8,128)(2,1)}), bf16[8,36,896]{2,1,0:T(8,128)(2,1)S(1)}, u32[]{:S(2)}, u32[]{:S(2)}) %all-to-all-start.1) | async-done | bytes 516128 | tf_op jit(solution)/shard_map/all_to_all | solution.py:974
  (309 shorter events, 250.9 us)
Async XLA Ops:
  7.2 107.1 %all-gather.3.cloned.1.call-start = ((), (), s32[]{:S(2)}) async-start(), calls=%async_computation.6 | async-start | bytes 2488320 | tf_op jit(solution)/shard_map/all_gather | solution.py:663
  7.9 179.0 %all-gather.5.cloned.1.call-start = ((), (), s32[]{:S(2)}) async-start(), calls=%async_computation.7 | async-start | bytes 5160960 | tf_op jit(solution)/shard_map/all_gather | solution.py:689
  44.7 453.2 %reduce-scatter.10.cloned.1.call-start = ((), (), s32[]{:S(2)}) async-start(), calls=%async_computation.10 | async-start | bytes 2488320
  70.1 37.4 %collective-permute-start.4 = (bf16[144,2816]{1,0:T(8,128)(2,1)}, bf16[144,2816]{1,0:T(8,128)(2,1)S(1)}, u32[]{:S(2)}, u32[]{:S(2)}) collective-permute-start(bf16[144,2816]{1,0:T(8,128)(2,1)} %line.1.refs_0_), channel_id=1, source_target_pairs={{0,4},{1,5},{2,6},{3,7},{4,0},{5,1},{6,2},{7,3},{8,12},{9,13},{10,... | collective-permute-start | bytes 2433032 | tf_op jit(solution)/shard_map/ppermute | solution.py:531
  71.5 36.0 %collective-permute-start.5 = (bf16[144,2816]{1,0:T(8,128)(2,1)}, bf16[144,2816]{1,0:T(8,128)(2,1)S(1)}, u32[]{:S(2)}, u32[]{:S(2)}) collective-permute-start(bf16[144,2816]{1,0:T(8,128)(2,1)} %line.1.refs_0_), channel_id=1, source_target_pairs={{0,6},{1,7},{2,4},{3,5},{4,2},{5,3},{6,0},{7,1},{8,14},{9,15},{10,... | collective-permute-start | bytes 2433032 | tf_op jit(solution)/shard_map/ppermute | solution.py:531
  189.2 34.2 %collective-permute-start.17 = (bf16[256,1152]{1,0:T(8,128)(2,1)}, bf16[256,1152]{1,0:T(8,128)(2,1)S(1)}, u32[]{:S(2)}, u32[]{:S(2)}) collective-permute-start(bf16[256,1152]{1,0:T(8,128)(2,1)} %get-tuple-element.236.refs_0_), channel_id=1, source_target_pairs={{0,2},{1,3},{2,0},{3,1},{4,6},{5,7},{6,4},{7,5},{8,10},{9,11},{10,... | collective-permute-start | bytes 1769480 | tf_op jit(solution)/shard_map/ppermute | solution.py:531
  189.8 34.5 %collective-permute-start.18 = (bf16[256,1152]{1,0:T(8,128)(2,1)}, bf16[256,1152]{1,0:T(8,128)(2,1)}, u32[]{:S(2)}, u32[]{:S(2)}) collective-permute-start(bf16[256,1152]{1,0:T(8,128)(2,1)} %get-tuple-element.236.refs_0_), channel_id=1, source_target_pairs={{0,4},{1,5},{2,6},{3,7},{4,0},{5,1},{6,2},{7,3},{8,12},{9,13},{10,... | collective-permute-start | bytes 1769480 | tf_op jit(solution)/shard_map/ppermute | solution.py:531
  191.8 32.5 %collective-permute-start.19 = (bf16[256,1152]{1,0:T(8,128)(2,1)}, bf16[256,1152]{1,0:T(8,128)(2,1)}, u32[]{:S(2)}, u32[]{:S(2)}) collective-permute-start(bf16[256,1152]{1,0:T(8,128)(2,1)} %get-tuple-element.236.refs_0_), channel_id=1, source_target_pairs={{0,6},{1,7},{2,4},{3,5},{4,2},{5,3},{6,0},{7,1},{8,14},{9,15},{10,... | collective-permute-start | bytes 1769480 | tf_op jit(solution)/shard_map/ppermute | solution.py:531
  255.3 33.2 %collective-permute-start.26 = (bf16[256,1152]{1,0:T(8,128)(2,1)}, bf16[256,1152]{1,0:T(8,128)(2,1)S(1)}, u32[]{:S(2)}, u32[]{:S(2)}) collective-permute-start(bf16[256,1152]{1,0:T(8,128)(2,1)} %get-tuple-element.251.refs_0_), channel_id=1, source_target_pairs={{0,2},{1,3},{2,0},{3,1},{4,6},{5,7},{6,4},{7,5},{8,10},{9,11},{10,... | collective-permute-start | bytes 1769480 | tf_op jit(solution)/shard_map/ppermute | solution.py:531
  256.2 45.6 %collective-permute-start.27 = (bf16[256,1152]{1,0:T(8,128)(2,1)}, bf16[256,1152]{1,0:T(8,128)(2,1)S(1)}, u32[]{:S(2)}, u32[]{:S(2)}) collective-permute-start(bf16[256,1152]{1,0:T(8,128)(2,1)} %get-tuple-element.251.refs_0_), channel_id=1, source_target_pairs={{0,4},{1,5},{2,6},{3,7},{4,0},{5,1},{6,2},{7,3},{8,12},{9,13},{10,... | collective-permute-start | bytes 1769480 | tf_op jit(solution)/shard_map/ppermute | solution.py:531
  263.2 38.6 %collective-permute-start.28 = (bf16[256,1152]{1,0:T(8,128)(2,1)}, bf16[256,1152]{1,0:T(8,128)(2,1)S(1)}, u32[]{:S(2)}, u32[]{:S(2)}) collective-permute-start(bf16[256,1152]{1,0:T(8,128)(2,1)} %get-tuple-element.251.refs_0_), channel_id=1, source_target_pairs={{0,6},{1,7},{2,4},{3,5},{4,2},{5,3},{6,0},{7,1},{8,14},{9,15},{10,... | collective-permute-start | bytes 1769480 | tf_op jit(solution)/shard_map/ppermute | solution.py:531
  281.6 51.4 %collective-permute-start.32 = (bf16[256,1152]{1,0:T(8,128)(2,1)}, bf16[256,1152]{1,0:T(8,128)(2,1)S(1)}, u32[]{:S(2)}, u32[]{:S(2)}) collective-permute-start(bf16[256,1152]{1,0:T(8,128)(2,1)} %get-tuple-element.272.refs_0_), channel_id=1, source_target_pairs={{0,2},{1,3},{2,0},{3,1},{4,6},{5,7},{6,4},{7,5},{8,10},{9,11},{10,... | collective-permute-start | bytes 1769480 | tf_op jit(solution)/shard_map/ppermute | solution.py:531
  282.9 50.2 %collective-permute-start.33 = (bf16[256,1152]{1,0:T(8,128)(2,1)}, bf16[256,1152]{1,0:T(8,128)(2,1)S(1)}, u32[]{:S(2)}, u32[]{:S(2)}) collective-permute-start(bf16[256,1152]{1,0:T(8,128)(2,1)} %get-tuple-element.272.refs_0_), channel_id=1, source_target_pairs={{0,4},{1,5},{2,6},{3,7},{4,0},{5,1},{6,2},{7,3},{8,12},{9,13},{10,... | collective-permute-start | bytes 1769480 | tf_op jit(solution)/shard_map/ppermute | solution.py:531
  288.5 44.5 %collective-permute-start.34 = (bf16[256,1152]{1,0:T(8,128)(2,1)}, bf16[256,1152]{1,0:T(8,128)(2,1)S(1)}, u32[]{:S(2)}, u32[]{:S(2)}) collective-permute-start(bf16[256,1152]{1,0:T(8,128)(2,1)} %get-tuple-element.272.refs_0_), channel_id=1, source_target_pairs={{0,6},{1,7},{2,4},{3,5},{4,2},{5,3},{6,0},{7,1},{8,14},{9,15},{10,... | collective-permute-start | bytes 1769480 | tf_op jit(solution)/shard_map/ppermute | solution.py:531
  432.5 173.5 %reduce-scatter.6.cloned.1.call-start = ((), (), s32[]{:S(2)}) async-start(), calls=%async_computation.8 | async-start | bytes 2580480 | tf_op jit(solution)/shard_map/reduce_scatter | solution.py:985
  433.5 36.0 %collective-permute-start.29 = (bf16[256,1152]{1,0:T(8,128)(2,1)S(1)}, bf16[256,1152]{1,0:T(8,128)(2,1)S(1)}, u32[]{:S(2)}, u32[]{:S(2)}) collective-permute-start(bf16[256,1152]{1,0:T(8,128)(2,1)S(1)} %copy-done.61), channel_id=1, source_target_pairs={{0,2},{1,3},{2,0},{3,1},{4,6},{5,7},{6,4},{7,5},{8,10},{9,11},{10,... | collective-permute-start | bytes 1769480 | tf_op jit(solution)/shard_map/ppermute | solution.py:531
  434.8 36.2 %collective-permute-start.30 = (bf16[256,1152]{1,0:T(8,128)(2,1)S(1)}, bf16[256,1152]{1,0:T(8,128)(2,1)S(1)}, u32[]{:S(2)}, u32[]{:S(2)}) collective-permute-start(bf16[256,1152]{1,0:T(8,128)(2,1)S(1)} %copy-done.60), channel_id=1, source_target_pairs={{0,4},{1,5},{2,6},{3,7},{4,0},{5,1},{6,2},{7,3},{8,12},{9,13},{10,... | collective-permute-start | bytes 1769480 | tf_op jit(solution)/shard_map/ppermute | solution.py:531
  435.7 35.3 %collective-permute-start.31 = (bf16[256,1152]{1,0:T(8,128)(2,1)S(1)}, bf16[256,1152]{1,0:T(8,128)(2,1)S(1)}, u32[]{:S(2)}, u32[]{:S(2)}) collective-permute-start(bf16[256,1152]{1,0:T(8,128)(2,1)S(1)} %copy-done.59), channel_id=1, source_target_pairs={{0,6},{1,7},{2,4},{3,5},{4,2},{5,3},{6,0},{7,1},{8,14},{9,15},{10,... | collective-permute-start | bytes 1769480 | tf_op jit(solution)/shard_map/ppermute | solution.py:531
  467.5 30.3 %collective-permute-start.38 = (bf16[256,1152]{1,0:T(8,128)(2,1)}, bf16[256,1152]{1,0:T(8,128)(2,1)S(1)}, u32[]{:S(2)}, u32[]{:S(2)}) collective-permute-start(bf16[256,1152]{1,0:T(8,128)(2,1)} %get-tuple-element.278), channel_id=1, source_target_pairs={{0,2},{1,3},{2,0},{3,1},{4,6},{5,7},{6,4},{7,5},{8,10},{9,11},{10,... | collective-permute-start | bytes 1769480 | tf_op jit(solution)/shard_map/ppermute | solution.py:531
  521.1 125.8 %reduce-scatter.8.cloned.1.call-start = ((), (), s32[]{:S(2)}) async-start(), calls=%async_computation.9 | async-start | bytes 2580480 | tf_op jit(solution)/shard_map/reduce_scatter | solution.py:985
  521.2 33.8 %collective-permute-start.45 = (bf16[1152,896]{1,0:T(8,128)(2,1)}, bf16[1152,896]{1,0:T(8,128)(2,1)S(1)}, u32[]{:S(2)}, u32[]{:S(2)}) collective-permute-start(bf16[1152,896]{1,0:T(8,128)(2,1)} %get-tuple-element.339), channel_id=1, source_target_pairs={{0,1},{1,0},{2,3},{3,2},{4,5},{5,4},{6,7},{7,6},{8,9},{9,8},{10,11... | collective-permute-start | bytes 6193160 | tf_op jit(solution)/shard_map/ppermute | solution.py:531
  602.5 33.2 %collective-permute-start.50 = (bf16[144,1664]{1,0:T(8,128)(2,1)}, bf16[144,1664]{1,0:T(8,128)(2,1)S(1)}, u32[]{:S(2)}, u32[]{:S(2)}) collective-permute-start(bf16[144,1664]{1,0:T(8,128)(2,1)} %get-tuple-element.363), channel_id=1, source_target_pairs={{0,2},{1,3},{2,0},{3,1},{4,6},{5,7},{6,4},{7,5},{8,10},{9,11},{10,... | collective-permute-start | bytes 1437704 | tf_op jit(solution)/shard_map/ppermute | solution.py:531
  603.1 32.6 %collective-permute-start.51 = (bf16[144,1664]{1,0:T(8,128)(2,1)}, bf16[144,1664]{1,0:T(8,128)(2,1)S(1)}, u32[]{:S(2)}, u32[]{:S(2)}) collective-permute-start(bf16[144,1664]{1,0:T(8,128)(2,1)} %get-tuple-element.364), channel_id=1, source_target_pairs={{0,4},{1,5},{2,6},{3,7},{4,0},{5,1},{6,2},{7,3},{8,12},{9,13},{10,... | collective-permute-start | bytes 1437704 | tf_op jit(solution)/shard_map/ppermute | solution.py:531
  604.5 31.3 %collective-permute-start.52 = (bf16[144,1664]{1,0:T(8,128)(2,1)}, bf16[144,1664]{1,0:T(8,128)(2,1)S(1)}, u32[]{:S(2)}, u32[]{:S(2)}) collective-permute-start(bf16[144,1664]{1,0:T(8,128)(2,1)} %get-tuple-element.365), channel_id=1, source_target_pairs={{0,6},{1,7},{2,4},{3,5},{4,2},{5,3},{6,0},{7,1},{8,14},{9,15},{10,... | collective-permute-start | bytes 1437704 | tf_op jit(solution)/shard_map/ppermute | solution.py:531
  (111 other events, 1015.6 us)
Sparse Core Ops, SparseCore 0:
  9.6 55.5 all-gather.2
  67.3 83.7 all-gather.4
  432.6 44.5 reduce-scatter.9
  521.3 45.8 reduce-scatter.5
  569.4 42.4 reduce-scatter.7

commit v3 on v2

--- a/solution.py
+++ b/solution.py
@@ -21,6 +21,7 @@
 BF = jnp.bfloat16
 F32 = jnp.float32
 BOTH = ("dp", "seq")
+BITS = (6, 2, 4)
 NN = ((1,), (0,))
 NT = ((1,), (1,))
 TN = ((0,), (0,))
@@ -154,18 +155,15 @@
     nf_ref[...] = rms(hidden, gains[2:3]).astype(BF)
 
 
-def gelu_gate(gate, up):
-    return 0.5 * gate * (1.0 + jnp.tanh(GELU_C * (gate + 0.044715 * gate * gate * gate))) * up
-
-
 def ffn_rows(tokens, w_gu, w_down, store):
     total = None
     for half, (gu, down) in enumerate(zip(w_gu, w_down)):
         pad = down.shape[0]
         both = dot(tokens, gu[...])
         gate, up = both[:, :pad], both[:, pad:]
-        act = gelu_gate(gate, up).astype(BF)
-        store(half, gate.astype(BF), up.astype(BF), act)
+        gelu, slope = gelu_parts(gate)
+        act = (gelu * up).astype(BF)
+        store(half, gelu.astype(BF), (up * slope).astype(BF), act)
         part = dot(act, down[...])
         total = part if total is None else total + part
     return total.astype(BF)
@@ -174,11 +172,10 @@
 def ffn_back_rows(tokens, kept, w_gu, w_down, store):
     total = None
     for half, (gu, down) in enumerate(zip(w_gu, w_down)):
-        gate, up = kept(half)
+        gelu, rise = kept(half)
         d_act = dot(tokens, down[...], NT)
-        gelu, slope = gelu_parts(gate.astype(F32))
-        d_gate = (d_act * up.astype(F32) * slope).astype(BF)
-        d_up = (d_act * gelu).astype(BF)
+        d_gate = (d_act * rise.astype(F32)).astype(BF)
+        d_up = (d_act * gelu.astype(F32)).astype(BF)
         store(half, d_gate, d_up)
         pad = down.shape[0]
         part = dot(d_gate, gu[:, :pad], NT) + dot(d_up, gu[:, pad:], NT)
@@ -197,14 +194,14 @@
 
 
 def ffn_back_grid_kernel(halves, t_ref, *refs):
-    gates, ups, w_gu, w_down = (refs[i * halves : (i + 1) * halves] for i in range(4))
+    gelus, rises, w_gu, w_down = (refs[i * halves : (i + 1) * halves] for i in range(4))
     refs = refs[4 * halves :]
 
     def store(half, *values):
         for kind, value in enumerate(values):
             refs[kind * halves + half][...] = value
 
-    kept = lambda half: (gates[half][...], ups[half][...])
+    kept = lambda half: (gelus[half][...], rises[half][...])
     refs[-1][...] = ffn_back_rows(t_ref[...], kept, w_gu, w_down, store)
 
 
@@ -222,11 +219,51 @@
             copy.wait()
 
 
+class Weights:
+    def __init__(self, sources, buffers, sems):
+        self.buffers = buffers
+        self.copies = []
+        for index, (source, buffer) in enumerate(zip(sources, buffers)):
+            self.copies.append(pltpu.make_async_copy(source, buffer, sems.at[index]))
+        self.used = [False] * len(self.copies)
+
+    def start(self, index):
+        self.copies[index].start()
+
+    def __getitem__(self, index):
+        if not self.used[index]:
+            self.copies[index].wait()
+            self.used[index] = True
+        return self.buffers[index]
+
+
+class Lazy:
+    def __init__(self, weights, index):
+        self.weights, self.index = weights, index
+
+    @property
+    def shape(self):
+        return self.weights.buffers[self.index].shape
+
+    def __getitem__(self, at):
+        return self.weights[self.index][at]
+
+
+def lazy_weights(sources, buffers, sems, halves, first):
+    weights = Weights(sources, buffers, sems)
+    for half in range(halves):
+        for kind in first:
+            weights.start(kind * halves + half)
+    return [Lazy(weights, half) for half in range(halves)], [Lazy(weights, halves + half) for half in range(halves)]
+
+
 def ffn_kernel(count, halves, *refs):
     tokens, refs = refs[:count], refs[count:]
-    w_gu, w_down, refs = refs[:halves], refs[halves : 2 * halves], refs[2 * halves :]
+    sources, refs = refs[: 2 * halves], refs[2 * halves :]
     t_out, outs, parts = refs[0], refs[1 : 1 + 3 * halves], refs[1 + 3 * halves : 1 + 3 * halves + count]
-    buffers, sems = refs[1 + 3 * halves + count : -1], refs[-1]
+    refs = refs[1 + 3 * halves + count :]
+    buffers, w_buffers, sems, w_sems = refs[: 3 * halves], refs[3 * halves : -2], refs[-2], refs[-1]
+    w_gu, w_down = lazy_weights(sources, w_buffers, w_sems, halves, (0, 1))
     leaving = Leaving(sems)
     rows = tokens[0].shape[0]
     for index in range(count):
@@ -245,17 +282,20 @@
 
 def ffn_back_kernel(count, halves, *refs):
     tokens, refs = refs[:count], refs[count:]
-    gates, ups, w_gu, w_down = (refs[i * halves : (i + 1) * halves] for i in range(4))
+    gelus, rises, sources = refs[:halves], refs[halves : 2 * halves], refs[2 * halves : 4 * halves]
     t_out, refs = refs[4 * halves], refs[4 * halves + 1 :]
     outs, parts = refs[: 2 * halves], refs[2 * halves : 2 * halves + count]
-    kept_in, buffers, sems, in_sems = refs[2 * halves + count : -2 - 2 * halves], refs[-2 - 2 * halves : -2], refs[-2], refs[-1]
+    refs = refs[2 * halves + count :]
+    kept_in, buffers, w_buffers = (refs[i * 2 * halves : (i + 1) * 2 * halves] for i in range(3))
+    sems, in_sems, w_sems = refs[6 * halves :]
+    w_gu, w_down = lazy_weights(sources, w_buffers, w_sems, halves, (1, 0))
     leaving = Leaving(sems)
     rows = tokens[0].shape[0]
     arriving = {}
     for index in range(count):
         at = pl.ds(index * rows, rows)
         for half in range(halves):
-            for kind, source in enumerate((gates[half], ups[half])):
+            for kind, source in enumerate((gelus[half], rises[half])):
                 slot = kind * halves + half
                 copy = pltpu.make_async_copy(source.at[at], kept_in[slot].at[at], in_sems.at[index * 2 * halves + slot])
                 copy.start()
@@ -280,17 +320,15 @@
 
 
 def untangle_kernel(dp, seq, place, *refs):
-    lines, (in_ref, out_ref) = refs[:-2], refs[-2:]
-    columns = in_ref.shape[1]
-    in_rows, out_rows = in_ref.shape[0] // (dp * seq), out_ref.shape[0] // (dp * seq)
+    lines, out = refs[:-1], refs[-1]
+    rows = out.shape[0] // (dp * seq)
 
     def body(me):
         for index, ref in enumerate(lines):
             at = me ^ (index % 4 * 2) ^ (index // 4)
             for d in range(dp):
-                start, to = d * in_rows, d * seq + at
-                in_ref[to * in_rows : (to + 1) * in_rows] = ref[start : start + in_rows, :columns]
-                out_ref[to * out_rows : (to + 1) * out_rows] = ref[start : start + out_rows, columns:]
+                start, to = d * rows, (d * seq + at) * rows
+                out[to : to + rows] = ref[start : start + rows]
 
     on_value(place[0], seq, body)
 
@@ -302,14 +340,9 @@
 
 
 def join_kernel(*refs):
-    pieces, out, sems = refs[:-2], refs[-2], refs[-1]
-    rows = pieces[0].shape[0]
-    copies = []
-    for index, piece in enumerate(pieces):
-        copies.append(pltpu.make_async_copy(piece, out.at[pl.ds(index * rows, rows)], sems.at[index]))
-        copies[-1].start()
-    for copy in copies:
-        copy.wait()
+    rows = refs[0].shape[0]
+    for index, ref in enumerate(refs[:-1]):
+        refs[-1][index * rows : (index + 1) * rows] = ref[...]
 
 
 def owner_kernel(dp, gate_ref, up_ref, out_ref):
@@ -415,8 +448,15 @@
 
 
 def weights_kernel(short, wrows, micro, core, *refs):
+    attended, d_attn, refs = refs[:micro], refs[micro : 2 * micro], refs[2 * micro :]
     normed, d_raw, terms = refs[0], refs[1 : 1 + micro], refs[1 + micro : 1 + 7 * micro]
-    mine, other, total = refs[1 + 7 * micro :]
+    mine, other, total, out_total = refs[1 + 7 * micro :]
+    out_weights = None
+    for left, right in zip(attended, d_attn):
+        term = dot(left[...], right[...], TN)
+        out_weights = term if out_weights is None else out_weights + term
+    out_total[...] = out_weights
+    orows = out_total.shape[0] // (2 * (mine.shape[0] // wrows))
     width = normed.shape[-1]
     ind = d_raw[0].shape[-1]
     weights = None
@@ -439,8 +479,18 @@
         at = slice(index * wrows, (index + 1) * wrows)
         first = total[2 * index * wrows : (2 * index + 1) * wrows]
         second = total[(2 * index + 1) * wrows : (2 * index + 2) * wrows]
-        mine[at] = jnp.where(odd, second, first).astype(BF)
-        other[at] = jnp.where(odd, first, second).astype(BF)
+        columns = first.shape[1]
+        mine[at, :columns] = jnp.where(odd, second, first).astype(BF)
+        other[at, :columns] = jnp.where(odd, first, second).astype(BF)
+        first = out_total[2 * index * orows : (2 * index + 1) * orows]
+        second = out_total[(2 * index + 1) * orows : (2 * index + 2) * orows]
+        at = slice(index * wrows, index * wrows + orows)
+        mine[at, columns:] = jnp.where(odd, second, first).astype(BF)
+        other[at, columns:] = jnp.where(odd, first, second).astype(BF)
+        if orows < wrows:
+            rest = slice(index * wrows + orows, (index + 1) * wrows)
+            for ref in (mine, other):
+                ref[rest, columns:] = jnp.zeros((wrows - orows, ref.shape[1] - columns), BF)
 
 
 def on_value(scalar, count, body):
@@ -452,13 +502,15 @@
 
 
 def line_kernel(place, *refs):
-    blocks, out = refs[:-1], refs[-1]
-    count, rows = len(blocks), blocks[0].shape[1]
+    blocks, (in_ref, out_ref) = refs[:-2], refs[-2:]
+    count, columns = len(blocks), in_ref.shape[1]
+    in_rows, out_rows = in_ref.shape[0] // count, out_ref.shape[0] // count
 
     def body(d):
         for by, ref in enumerate(blocks):
             at = (d - by) % count
-            out[at * rows : (at + 1) * rows] = ref[0]
+            in_ref[at * in_rows : (at + 1) * in_rows] = ref[0, :in_rows, :columns]
+            out_ref[at * out_rows : (at + 1) * out_rows] = ref[0, :out_rows, columns:]
 
     on_value(place[0], count, body)
 
@@ -517,10 +569,11 @@
     parts, outs = refs[:count], refs[count:]
     total = add_up(parts)
     start = 0
-    for out in outs[:-1]:
+    for out in outs[:-2]:
         out[...] = total[:, start : start + out.shape[1]]
         start += out.shape[1]
-    outs[-1][...] = jnp.transpose(total[:, start:])[:8]
+    outs[-2][...] = jnp.transpose(total[:, start : start + LANES])[:8]
+    outs[-1][...] = total[: outs[-1].shape[0], start + LANES :]
 
 
 def after(value, *others):
@@ -536,8 +589,8 @@
     return lax.ppermute(value, "seq", pairs)
 
 
-def near_blocks(own, size):
-    return [xor_permute(own, bit, size) for bit in (2, 4, 6)]
+def near_blocks(own, size, bits=(2, 4, 6)):
+    return [xor_permute(own, bit, size) for bit in bits]
 
 
 class Order:
@@ -661,39 +714,38 @@
         name="owner",
     )
     w_down = lax.all_gather(downproj, "dp", axis=0, tiled=True)
-    if split:
-        gate_up, cosine, sine, line[0] = order.step(order.behind((gate_up, cosine, sine, line[0])))
     gate_up = lax.all_to_all(gate_up, "seq", 0, 0).reshape(seq * wrows, 2 * pad)
     if split:
-        [line] = call(
+        gate_up, cosine, sine = order.step(order.behind((gate_up, cosine, sine)))
+        in_line, out_line = call(
             line_kernel,
             None,
             [(along_dp, SMEM)] + [plain(block) for block in [both] + order.behind(line)],
-            [(shape((dp * wrows, both.shape[2]), BF), VMEM)],
+            [(shape((dp * wrows, ind + LANES), BF), VMEM), (shape((dp * orows, width), BF), VMEM)],
             name="line",
         )
-        lines = [line] + near_blocks(order.step(line), seq)
-        lines = order.step(order.behind(lines))
-        others = [xor_permute(line, 1, seq) for line in lines]
-        others, w_down = order.step(order.behind((others, w_down)))
-        w_in, w_out = call(
-            functools.partial(untangle_kernel, dp, seq),
-            None,
-            [(lax.axis_index("seq").reshape(1), SMEM)] + [plain(line) for line in lines + others],
-            [(shape((width, ind + LANES), BF), VMEM), (shape((qd, width), BF), VMEM)],
-            name="untangle",
-        )
+
+        def untangle(lines, name):
+            [array] = call(
+                functools.partial(untangle_kernel, dp, seq),
+                None,
+                [(lax.axis_index("seq").reshape(1), SMEM)] + [plain(line) for line in lines],
+                [(shape((lines[0].shape[0] * seq, lines[0].shape[1]), BF), VMEM)],
+                name=name,
+            )
+            return array
+
+        in_lines = [in_line] + near_blocks(order.step(in_line), seq)
+        in_lines = order.step(order.behind(in_lines))
+        out_lines = [out_line] + near_blocks(after(out_line, in_lines), seq)
+        in_lines = in_lines + [xor_permute(line, 1, seq) for line in in_lines]
+        in_lines = order.step(order.behind(in_lines))
+        w_in = untangle(in_lines, "untangle_in")
+        order.step(w_in)
     else:
         w_in = lax.all_gather(packed[None], BOTH, axis=0, tiled=True).reshape(width, -1)
         w_out = lax.all_gather(outproj, BOTH, axis=0, tiled=True)
     w_gu = [lax.all_gather(gate_up, "dp", axis=0, tiled=True)]
-    [w_down] = call(
-        pad_kernel, None, [plain(order.behind(w_down))], [(shape((pad, width), BF), VMEM)], name="pad"
-    )
-    w_down = [order.step(w_down)]
-    if split:
-        w_down = order.step(order.behind(w_down + [xor_permute(w_down[0], 1, seq)]))
-
     def of_micro(array, index):
         dims = array.shape[1:]
         return (array, pl.BlockSpec((1,) + dims, lambda *_: (index,) + (0,) * len(dims)))
@@ -727,6 +779,17 @@
 
     order.step(pair)
     behind = [from_behind(pair, by, seq) for by in range(1, reach + 1)]
+    if split:
+        out_lines = order.step(order.behind(out_lines))
+        out_lines = out_lines + [xor_permute(line, 1, seq) for line in out_lines]
+        out_lines, w_down = order.step(order.behind((out_lines, w_down)))
+        w_out = order.step(untangle(out_lines, "untangle_out"))
+    [w_down] = call(
+        pad_kernel, None, [plain(order.behind(w_down))], [(shape((pad, width), BF), VMEM)], name="pad"
+    )
+    w_down = [order.step(w_down)]
+    if split:
+        w_down = w_down + [xor_permute(w_down[0], 1, seq)]
     states = []
     for index in range(micro):
         place = order.behind(jnp.stack([lengths[index], base]))
@@ -742,7 +805,7 @@
         )
         order.step(normed_ffn)
         s = dict(place=place, pairs=pairs, attended=attended, attn_out=attn_out, hidden=hidden)
-        s["sent"] = near_blocks(normed_ffn, seq) if split else None
+        s["sent"] = near_blocks(normed_ffn, seq, BITS) if split else None
         s["nf"] = normed_ffn
         states.append(s)
 
@@ -764,6 +827,7 @@
         return pl.BlockSpec((rows, columns), index_of)
 
     any_spec = pl.BlockSpec(memory_space=pl.ANY)
+    w_scratch = [pltpu.VMEM((width, 2 * pad), BF)] * halves + [pltpu.VMEM((pad, width), BF)] * halves
 
     def ffn(pieces):
         if not split:
@@ -780,24 +844,25 @@
         results = call(
             functools.partial(ffn_kernel, count, halves),
             None,
-            [plain(array) for array in pieces + list(w_gu) + list(w_down)],
+            [plain(array) for array in order.behind(pieces)] + [(w, any_spec) for w in [*w_gu, *w_down]],
             [(shape((count * rows, width), BF), any_spec)]
             + [(shape((count * rows, pad), BF), any_spec)] * (3 * halves)
             + [(shape((rows, width), BF), VMEM)] * count,
             scratch=[pltpu.VMEM((count * rows, pad), BF)] * (3 * halves)
-            + [pltpu.SemaphoreType.DMA((count * (1 + 3 * halves),))],
+            + w_scratch
+            + [pltpu.SemaphoreType.DMA((count * (1 + 3 * halves),)), pltpu.SemaphoreType.DMA((2 * halves,))],
             name="ffn",
         )
         kinds = [results[1 + i * halves : 1 + (i + 1) * halves] for i in range(3)]
         return results[0], *kinds, results[1 + 3 * halves :]
 
-    def ffn_backward(pieces, gate, up):
+    def ffn_backward(pieces, gelu, rise):
         if not split:
             count = pieces[0].shape[0] // rows
             results = call(
                 functools.partial(ffn_back_grid_kernel, halves),
                 (count,),
-                [blocks(pieces[0]), *map(blocks, gate), *map(blocks, up)]
+                [blocks(pieces[0]), *map(blocks, gelu), *map(blocks, rise)]
                 + [fixed(w) for w in w_gu]
                 + [fixed(w) for w in w_down],
                 [made(count * rows, pad)] * 2 + [made(count * rows, width)],
@@ -809,13 +874,14 @@
             functools.partial(ffn_back_kernel, count, halves),
             None,
             [plain(piece) for piece in pieces]
-            + [(array, any_spec) for array in [*gate, *up]]
-            + [plain(array) for array in list(w_gu) + list(w_down)],
+            + [(array, any_spec) for array in [*gelu, *rise, *w_gu, *w_down]],
             [(shape((count * rows, width), BF), any_spec)]
             + [(shape((count * rows, pad), BF), any_spec)] * (2 * halves)
             + [(shape((rows, width), BF), VMEM)] * count,
             scratch=[pltpu.VMEM((count * rows, pad), BF)] * (4 * halves)
-            + [pltpu.SemaphoreType.DMA((count * (1 + 2 * halves),)), pltpu.SemaphoreType.DMA((count * 2 * halves,))],
+            + w_scratch
+            + [pltpu.SemaphoreType.DMA((count * (1 + 2 * halves),)), pltpu.SemaphoreType.DMA((count * 2 * halves,))]
+            + [pltpu.SemaphoreType.DMA((2 * halves,))],
             name="ffn_back",
         )
         return results[0], results[1 : 1 + halves], results[1 + halves : 1 + 2 * halves], results[1 + 2 * halves :]
@@ -823,16 +889,16 @@
     def pieces_of(own, near):
         if not split:
             return [lax.all_gather(order.behind(own), "seq", axis=0, tiled=True)]
-        return [order.behind(own)] + list(near)
+        return list(near) + [order.behind(own)]
 
     def scatter(parts):
         if not split:
             return [lax.psum_scatter(parts[0], "seq", scatter_dimension=0, tiled=True)]
-        return [parts[0]] + [xor_permute(part, bit, seq) for part, bit in zip(parts[1:], (2, 4, 6))]
+        return [parts[-1]] + [xor_permute(part, bit, seq) for part, bit in zip(parts, BITS)]
 
     for s in states:
         pieces = pieces_of(s["nf"], s["sent"])
-        s["tokens"], s["gate"], s["up"], s["act"], parts = ffn(pieces)
+        s["tokens"], s["gelu"], s["rise"], s["act"], parts = ffn(pieces)
         order.step(parts)
         s["terms"] = scatter(parts)
 
@@ -852,15 +918,14 @@
             name="middle",
         )
         order.step(s["d_ffn"])
-        s["sent"] = near_blocks(s["d_ffn"], seq) if split else None
+        s["sent"] = near_blocks(s["d_ffn"], seq, BITS) if split else None
 
     def join(pieces):
         [joined] = call(
             join_kernel,
             None,
-            [(piece, any_spec) for piece in pieces],
-            [(shape((len(pieces) * rows, width), BF), any_spec)],
-            scratch=[pltpu.SemaphoreType.DMA((len(pieces),))],
+            [plain(piece) for piece in pieces],
+            [(shape((len(pieces) * rows, width), BF), VMEM)],
             name="join",
         )
         return joined
@@ -888,25 +953,15 @@
         )
         return order.step(results)
 
-    def weight_terms(left, rights, high_out=None, meanwhile=None):
-        if not split:
-            if meanwhile is not None:
-                meanwhile()
-            yield from over_tokens(left, rights, 0, (), high_out)
-            return
-        others = over_tokens(left, rights, 1, (), high_out)
-        if meanwhile is not None:
-            meanwhile()
-            others = order.behind(others)
-        gots = [xor_permute(other, 1, seq) for other in others]
-        if meanwhile is not None:
-            attend_back(micro - 1)
-        for right, got in zip(rights, gots):
-            yield over_tokens(left, [right], 0, [got], high_out)[0]
+    def other_terms(left, right, high_out=None):
+        return over_tokens(left, [right], 1, (), high_out)[0] if split else None
+
+    def own_terms(left, right, other, high_out=None):
+        return over_tokens(left, [right], 0, [xor_permute(other, 1, seq)] if split else (), high_out)[0]
 
     def ffn_back(s):
         pieces = pieces_of(s["d_ffn"], s["sent"])
-        tokens, s["d_gate"], s["d_up"], parts = ffn_backward(pieces, s["gate"], s["up"])
+        tokens, s["d_gate"], s["d_up"], parts = ffn_backward(pieces, s["gelu"], s["rise"])
         s.setdefault("d_tokens", tokens)
         order.step(parts)
         s["terms"] = scatter(parts)
@@ -916,12 +971,12 @@
     late = states[-1]
     if split:
         late["sent"] = order.step(order.behind(late["sent"]))
-        late["d_tokens"] = order.step(join([late["d_ffn"]] + list(late["sent"])))
-        down_terms = next(weight_terms("act", ["d_tokens"], own_ff))
+        late["d_tokens"] = order.step(join(list(late["sent"]) + [late["d_ffn"]]))
+        down_terms = own_terms("act", "d_tokens", other_terms("act", "d_tokens", own_ff), own_ff)
         ffn_back(late)
     else:
         ffn_back(late)
-        down_terms = next(weight_terms("act", ["d_tokens"], own_ff))
+        down_terms = own_terms("act", "d_tokens", None, own_ff)
     down_grad = lax.psum_scatter(down_terms, "dp", scatter_dimension=0, tiled=True)
     for s in states[:-1]:
         s["terms"] = order.step(order.behind(s["terms"]))
@@ -970,77 +1025,71 @@
         s["normed_in"] = normed_in[index]
         return input_grad
 
-    def to_columns(part):
-        part = lax.all_to_all(part.reshape(seq, wrows, pad), "seq", 0, 0)
+    def columns_of(part, index):
         [columns] = call(
             functools.partial(columns_kernel, dp),
-            None,
-            [plain(part)],
-            [(shape((wrows, ff), F32), VMEM)],
+            (1,),
+            [(part, pl.BlockSpec((seq, wrows, pad), lambda *_: (0, 0, index)))],
+            [(shape((wrows, ff), F32), pl.BlockSpec((wrows, ff), lambda *_: (0, 0)))],
             name="columns",
         )
         return columns
 
+    def to_columns(part):
+        return columns_of(lax.all_to_all(part.reshape(seq, wrows, pad), "seq", 0, 0), 0)
+
     input_grad = None
     scattered = lambda terms: lax.psum_scatter(terms, "dp", scatter_dimension=0, tiled=True)
-    def meanwhile():
-        for index in range(micro - 1):
-            attend_back(index)
-        nonlocal down_grad
-        down_grad, states[-1]["terms"] = order.step(order.behind((down_grad, states[-1]["terms"])))
-
-    gate_up_terms = weight_terms("tokens", ["d_gate", "d_up"], None, meanwhile)
-    gate_sum = scattered(next(gate_up_terms))
-    if not split:
-        attend_back(micro - 1)
+    gate_other = other_terms("tokens", "d_gate")
+    for index in range(micro - 1):
+        attend_back(index)
+    down_grad = order.step(order.behind(down_grad))
+    gate_terms = own_terms("tokens", "d_gate", gate_other)
+    up_other = other_terms("tokens", "d_up")
+    for s in states[:-1]:
+        s["d_pairs"] = order.step(order.behind(s["d_pairs"]))
+    states[-1]["terms"] = order.step(order.behind(states[-1]["terms"]))
+    gate_sum = scattered(order.behind(gate_terms))
+    attend_back(micro - 1)
+    for index in range(micro):
+        input_grad = project_back(index, input_grad)
     core = lax.axis_index("seq") & 1
-    out_terms = order.step(sum(dot(s["attended"], order.behind(s["d_attn"]), TN) for s in states).astype(BF))
-    if split:
-        view = out_terms.reshape(devices // 2, 2, qd // devices, width)
-        mine, other = (
-            lax.dynamic_index_in_dim(view, at.astype(jnp.uint32), 1, keepdims=False).reshape(-1, width)
-            for at in (core, 1 - core)
-        )
-        got = xor_permute(other, 1, seq)
-    input_grad = project_back(micro - 1, input_grad)
-    if split:
-        out_parts = fold_chips(mine, got, dp, seq, order)
-    else:
-        out_grad = lax.psum_scatter(out_terms, BOTH, scatter_dimension=0, tiled=True).astype(F32)
-    for index in range(micro - 1):
-        input_grad = project_back(index, input_grad)
-    up_sum = scattered(next(gate_up_terms))
-    if split:
-        out_parts = fold_line(out_parts, dp, order)
     sums = [s[name] for name in ("t_in", "t_attn", "t_pre", "t_post", "t_query", "t_keys") for s in states]
-    half_out = (shape((devices // 2 * wrows, ind + LANES), BF), VMEM)
+    half_out = (shape((devices // 2 * wrows, ind + LANES + width), BF), VMEM)
     mine, other = call(
         functools.partial(weights_kernel, short, wrows, micro),
         None,
-        [(order.behind((core if split else jnp.int32(0)).reshape(1)), smem), plain(normed_in)]
+        [(order.behind((core if split else jnp.int32(0)).reshape(1)), smem)]
+        + [plain(s["attended"]) for s in states]
+        + [plain(s["d_attn"]) for s in states]
+        + [plain(normed_in)]
         + [plain(s["d_raw"]) for s in states]
         + [plain(term) for term in sums],
         [half_out, half_out],
-        scratch=[pltpu.VMEM((width, ind + LANES), F32)],
+        scratch=[pltpu.VMEM((width, ind + LANES), F32), pltpu.VMEM((qd, width), F32)],
         name="weights",
     )
     order.step(other)
     if split:
         got = xor_permute(other, 1, seq)
+        up_sum = scattered(own_terms("tokens", "d_up", up_other))
         in_parts = fold_chips(mine, got, dp, seq, order)
-        out_grad = order.step(add_up_arrays(order.behind(out_parts)))
-        gate_grad = order.step(to_columns(gate_sum))
+        both_sums = [part.reshape(seq, wrows, pad) for part in order.behind((gate_sum, up_sum))]
+        both_sums = order.step(jnp.concatenate(both_sums, axis=2))
         in_parts = fold_line(in_parts, dp, order)
-        up_grad = to_columns(order.behind(up_sum))
+        both_sums = lax.all_to_all(order.behind(both_sums), "seq", 0, 0)
+        gate_grad, up_grad = (columns_of(both_sums, index) for index in range(2))
     else:
+        up_sum = scattered(own_terms("tokens", "d_up", None))
         halves_of = [part.reshape(devices // 2, wrows, -1) for part in (mine, other)]
         whole_terms = jnp.stack(halves_of, axis=1).reshape(devices, wrows, -1)
         in_parts = [lax.psum_scatter(whole_terms, BOTH, scatter_dimension=0, tiled=True)[0]]
-    q_grad, k_grad, v_grad, gain_sum = call(
+    q_grad, k_grad, v_grad, gain_sum, out_grad = call(
         functools.partial(finish_kernel, len(in_parts)),
         None,
         [plain(part) for part in in_parts],
-        [(shape((wrows, columns), F32), VMEM) for columns in (qd, HD, HD)] + [(shape((8, wrows), F32), VMEM)],
+        [(shape((wrows, columns), F32), VMEM) for columns in (qd, HD, HD)] + [(shape((8, wrows), F32), VMEM)]
+        + [(shape((qd // devices, width), F32), VMEM)],
         name="finish",
     )
 

time: 681 us -> 593 us (0.87)
  Pallas kernels: 335 us -> 265 us
  blocking collectives: 20.1 us -> 0 us
  waiting for transfers between devices: 173 us -> 189 us
  local copies, waits for them, and re-layouts: 38.1 us -> 26.7 us
    pallas_call x31, Pallas kernels: 335 us -> 265 us  [call(): pl.pallas_call(body, **{} if grid is None else {'grid': grid}, in_specs=[...]
    reduce_scatter x2, waiting for transfers between devices: 0.01 us -> 36.5 us  [shards(): lax.psum_scatter(terms, 'dp', scatter_dimension=0, tiled=True)]
    ppermute x44 -> x47, waiting for transfers between devices: 115 us -> 89.5 us  [xor_permute(): return lax.ppermute(value, 'seq', [(i, i ^ bit) for i in range(size)])]
    all_to_all x1 -> x0, blocking collectives: 20.1 us -> none  [shards(): gate_up = lax.all_to_all(gate_up, 'seq', 0, 0).reshape(seq * wrows, 2 * pad)]
    ppermute x9 -> x6, waiting for transfers between devices: 27.1 us -> 38.3 us  [around(): return lax.ppermute(value, 'dp', [(i, (i + by) % dp) for i in range(dp)])]
    ppermute x6, waiting for transfers between devices: 19.6 us -> 9.76 us  [from_behind(): return lax.ppermute(value, 'seq', pairs)]
    unnamed x142 -> x149, local copies, waits for them, and re-layouts: 26.3 us -> 19.1 us
    ppermute x9 -> x6, starting transfers between devices: 20.5 us -> 15.3 us  [around(): return lax.ppermute(value, 'dp', [(i, (i + by) % dp) for i in range(dp)])]
  transfers between devices with their start and end apart: 66 -> 66, of which waited for: 26 -> 25; matrix products, arithmetic and copies ran while one was open for 3% -> 2% of each run, Pallas kernels for 34% -> 40%
where the time goes in v3:
time: 593 us; the launch traced here: 583 us
  Pallas kernels  265 us (45%)
  waiting for transfers between devices  189 us (32%)
  starting transfers between devices  81.6 us (14%)
  local copies, waits for them, and re-layouts  26.7 us (5%)
  between operations  15.1 us (3%)
    pallas_call x31, Pallas kernels, call(): pl.pallas_call(body, **{} if grid is None else {'grid': grid}, in_specs=[...  265 us
    ppermute x47, waiting for transfers between devices, xor_permute(): return lax.ppermute(value, 'seq', [(i, i ^ bit) for i in range(size)])  89.5 us
    ppermute x47, starting transfers between devices, xor_permute(): return lax.ppermute(value, 'seq', [(i, i ^ bit) for i in range(size)])  46.1 us
    ppermute x6, waiting for transfers between devices, around(): return lax.ppermute(value, 'dp', [(i, (i + by) % dp) for i in range(dp)])  38.3 us
    reduce_scatter x2, waiting for transfers between devices, shards(): lax.psum_scatter(terms, 'dp', scatter_dimension=0, tiled=True)  36.5 us
    unnamed x149, local copies, waits for them, and re-layouts  19.1 us
    ppermute x6, starting transfers between devices, around(): return lax.ppermute(value, 'dp', [(i, (i + by) % dp) for i in range(dp)])  15.3 us
    all_to_all x1, waiting for transfers between devices, shards(): gate_up = lax.all_to_all(gate_up, 'seq', 0, 0).reshape(seq * wrows, 2 * pad)  14 us
  transfers between devices with their start and end apart: 66, of which 25 were waited for; matrix products, arithmetic and copies ran while one was open for 2% of the time, Pallas kernels for 40%

profile of v3, /device:TPU:0, one launch (start us, length us, event | category | flops | bytes accessed | tf_op | source)
XLA Modules:
  0.0 582.6 jit_solution(704028963794295757)
XLA Ops:
  18.6 14.0 %all-to-all-done = bf16[8,36,1792]{2,1,0:T(8,128)(2,1)S(1)} async-done(((bf16[8,36,1792]{2,1,0:T(8,128)(2,1)}), bf16[8,36,1792]{2,1,0:T(8,128)(2,1)S(1)}, u32[]{:S(2)}, u32[]{:S(2)}) %all-to-all-start) | async-done | bytes 1032224 | tf_op jit(solution)/shard_map/all_to_all | solution.py:717
  39.3 9.5 %collective-permute-done.refs_1_ = bf16[1,36,2816]{2,1,0:T(8,128)(2,1)S(1)} collective-permute-done((bf16[1,36,2816]{2,1,0:T(8,128)(2,1)S(1)}, bf16[1,36,2816]{2,1,0:T(8,128)(2,1)S(1)}, u32[]{:S(2)}, u32[]{:S(2)}) %collective-permute-start) | collective-permute-done | bytes 202784 | tf_op jit(solution)/shard_map/ppermute | solution.py:609
  48.8 15.1 %collective-permute-done.1.refs_2_ = bf16[1,36,2816]{2,1,0:T(8,128)(2,1)S(1)} collective-permute-done((bf16[1,36,2816]{2,1,0:T(8,128)(2,1)S(1)}, bf16[1,36,2816]{2,1,0:T(8,128)(2,1)S(1)}, u32[]{:S(2)}, u32[]{:S(2)}) %collective-permute-start.1) | collective-permute-done | bytes 202784 | tf_op jit(solution)/shard_map/ppermute | solution.py:609
  70.5 10.6 %collective-permute-done.3.refs_1_ = bf16[144,1664]{1,0:T(8,128)(2,1)S(1)} collective-permute-done((bf16[144,1664]{1,0:T(8,128)(2,1)}, bf16[144,1664]{1,0:T(8,128)(2,1)S(1)}, u32[]{:S(2)}, u32[]{:S(2)}) %collective-permute-start.3) | collective-permute-done | bytes 479264 | tf_op jit(solution)/shard_map/ppermute | solution.py:584
  81.1 10.2 %collective-permute-done.4.refs_2_ = bf16[144,1664]{1,0:T(8,128)(2,1)S(1)} collective-permute-done((bf16[144,1664]{1,0:T(8,128)(2,1)}, bf16[144,1664]{1,0:T(8,128)(2,1)S(1)}, u32[]{:S(2)}, u32[]{:S(2)}) %collective-permute-start.4) | collective-permute-done | bytes 479264 | tf_op jit(solution)/shard_map/ppermute | solution.py:584
  149.4 14.1 %collective-permute-done.23.refs_1_ = bf16[256,1152]{1,0:T(8,128)(2,1)} collective-permute-done((bf16[256,1152]{1,0:T(8,128)(2,1)}, bf16[256,1152]{1,0:T(8,128)(2,1)}, u32[]{:S(2)}, u32[]{:S(2)}) %collective-permute-start.23) | collective-permute-done | bytes 589856 | tf_op jit(solution)/shard_map/ppermute | solution.py:584
  177.9 23.3 %ffn.2 = (bf16[1024,1152]{1,0:T(8,128)(2,1)}, bf16[1024,896]{1,0:T(8,128)(2,1)}, bf16[1024,896]{1,0:T(8,128)(2,1)}, bf16[1024,896]{1,0:T(8,128)(2,1)}, bf16[1024...) custom-call(bf16[256,1152]{1,0:T(8,128)(2,1)} %collective-permute-do, ...), custom_call_target="tpu_custom_call" | custom-call | bytes 1 | tf_op jit(solution)/shard_map/ffn/pallas_call | solution.py:43
  204.8 23.3 %ffn.3 = (bf16[1024,1152]{1,0:T(8,128)(2,1)}, bf16[1024,896]{1,0:T(8,128)(2,1)}, bf16[1024,896]{1,0:T(8,128)(2,1)}, bf16[1024,896]{1,0:T(8,128)(2,1)}, bf16[1024...) custom-call(bf16[256,1152]{1,0:T(8,128)(2,1)} %collective-permute-do, ...), custom_call_target="tpu_custom_call" | custom-call | bytes 1 | tf_op jit(solution)/shard_map/ffn/pallas_call | solution.py:43
  247.4 11.2 %collective-permute-done.28.refs_2_ = bf16[256,1152]{1,0:T(8,128)(2,1)S(1)} collective-permute-done((bf16[256,1152]{1,0:T(8,128)(2,1)}, bf16[256,1152]{1,0:T(8,128)(2,1)S(1)}, u32[]{:S(2)}, u32[]{:S(2)}) %collective-permute-start.28) | collective-permute-done | bytes 589856 | tf_op jit(solution)/shard_map/ppermute | solution.py:584
  272.7 11.2 %collective-permute-done.37.refs_1_ = bf16[256,1152]{1,0:T(8,128)(2,1)S(1)} collective-permute-done((bf16[256,1152]{1,0:T(8,128)(2,1)}, bf16[256,1152]{1,0:T(8,128)(2,1)S(1)}, u32[]{:S(2)}, u32[]{:S(2)}) %collective-permute-start.37) | collective-permute-done | bytes 589856 | tf_op jit(solution)/shard_map/ppermute | solution.py:584
  284.9 26.7 %ffn_back.2 = (bf16[1024,1152]{1,0:T(8,128)(2,1)}, bf16[1024,896]{1,0:T(8,128)(2,1)}, bf16[1024,896]{1,0:T(8,128)(2,1)}, bf16[1024,896]{1,0:T(8,128)(2,1)}, bf16...) custom-call(bf16[256,1152]{1,0:T(8,128)(2,1)} %copy-done.20, ...), custom_call_target="tpu_custom_call" | custom-call | bytes 1 | tf_op jit(solution)/shard_map/ffn_back/pallas_call | solution.py:43
  316.0 9.8 %terms.6 = bf16[864,1152]{1,0:T(8,128)(2,1)} custom-call(bf16[1024,896]{1,0:T(8,128)(2,1)} %get-tuple-element.298.refs_0_, bf16[1024,896]{1,0:T(8,128)(2,1)} %get-tuple-element.299.refs_1_, bf16[1024,1152]{1,0:T(8,128)(2,1)} %get-tuple-element.300.refs_2_, bf16[1024,1152]{1,0:T(8,128)(2,1)} %join.1.refs_3_), custom_call_target="tpu_custom_call" | custom-call | bytes 1 | tf_op jit(solution)/shard_map/terms/pallas_call | solution.py:43
  331.3 10.3 %terms.7 = bf16[864,1152]{1,0:T(8,128)(2,1)} custom-call(bf16[1024,896]{1,0:T(8,128)(2,1)} %get-tuple-element.301.refs_0_, bf16[1024,896]{1,0:T(8,128)(2,1)} %get-tuple-element.302.refs_1_, bf16[1024,1152]{1,0:T(8,128)(2,1)} %get-tuple-element.300.refs_2_, bf16[1024,1152]{1,0:T(8,128)(2,1)} %join.1.refs_3_, bf16[864,1152]{1,0:T(8,128)(2,1)} %copy-done.12), custom_call_target="tpu_custom_call" | custom-call | bytes 1 | tf_op jit(solution)/shard_map/terms/pallas_call | solution.py:43
  346.1 26.9 %ffn_back.3 = (bf16[1024,1152]{1,0:T(8,128)(2,1)}, bf16[1024,896]{1,0:T(8,128)(2,1)}, bf16[1024,896]{1,0:T(8,128)(2,1)}, bf16[1024,896]{1,0:T(8,128)(2,1)}, bf16...) custom-call(bf16[256,1152]{1,0:T(8,128)(2,1)} %copy-done.7, ...), custom_call_target="tpu_custom_call" | custom-call | bytes 1 | tf_op jit(solution)/shard_map/ffn_back/pallas_call | solution.py:43
  373.1 9.5 %terms.8 = bf16[1152,896]{1,0:T(8,128)(2,1)} custom-call(bf16[1024,1152]{1,0:T(8,128)(2,1)} %get-tuple-element.379.refs_0_, bf16[1024,1152]{1,0:T(8,128)(2,1)} %get-tuple-element.380.refs_1_, bf16[1024,896]{1,0:T(8,128)(2,1)} %get-tuple-element.320.refs_2_, bf16[1024,896]{1,0:T(8,128)(2,1)} %get-tuple-element.321.refs_3_), custom_call_target="tpu_custom_call" | custom-call | bytes 1 | tf_op jit(solution)/shard_map/terms/pallas_call | solution.py:43
  386.3 11.2 %attend_back.2 = (f32[256,1152]{1,0:T(8,128)}, bf16[256,1152]{1,0:T(8,128)(2,1)}, bf16[256,1024]{1,0:T(8,128)(2,1)}, f32[1,1152]{1,0:T(1,128)}, f32[1,1152]{1,0:...) custom-call(s32[2]{0:T(128)} %pad_add_fusion.1.place, ...), custom_call_target="tpu_custom_call" | custom-call | bytes 1 | tf_op jit(solution)/shard_map/attend_back/pallas_call | solution.py:43
  400.3 9.4 %terms.9 = bf16[1152,896]{1,0:T(8,128)(2,1)} custom-call(bf16[1024,1152]{1,0:T(8,128)(2,1)} %get-tuple-element.379.refs_0_, bf16[1024,1152]{1,0:T(8,128)(2,1)} %get-tuple-element.380.refs_1_, bf16[1024,896]{1,0:T(8,128)(2,1)} %get-tuple-element.332.refs_2_, bf16[1024,896]{1,0:T(8,128)(2,1)} %get-tuple-element.333.refs_3_, bf16[1152,896]{1,0:T(8,128)(2,1)} %copy-done.11), custom_call_target="tpu_custom_call" | custom-call | bytes 1 | tf_op jit(solution)/shard_map/terms/pallas_call | solution.py:43
  409.7 9.0 %terms.10 = bf16[1152,896]{1,0:T(8,128)(2,1)} custom-call(bf16[1024,1152]{1,0:T(8,128)(2,1)} %get-tuple-element.379.refs_0_, bf16[1024,1152]{1,0:T(8,128)(2,1)} %get-tuple-element.380.refs_1_, bf16[1024,896]{1,0:T(8,128)(2,1)} %get-tuple-element.336.refs_2_, bf16[1024,896]{1,0:T(8,128)(2,1)} %get-tuple-element.337.refs_3_), custom_call_target="tpu_custom_call" | custom-call | bytes 1 | tf_op jit(solution)/shard_map/terms/pallas_call | solution.py:43
  421.9 11.2 %attend_back.3 = (f32[256,1152]{1,0:T(8,128)}, bf16[256,1152]{1,0:T(8,128)(2,1)}, bf16[256,1024]{1,0:T(8,128)(2,1)}, f32[1,1152]{1,0:T(1,128)}, f32[1,1152]{1,0:...) custom-call(s32[2]{0:T(128)} %pad_add_fusion.place, ...), custom_call_target="tpu_custom_call" | custom-call | bytes 1 | tf_op jit(solution)/shard_map/attend_back/pallas_call | solution.py:43
  453.9 9.7 %weights.1 = (bf16[576,2816]{1,0:T(8,128)(2,1)}, bf16[576,2816]{1,0:T(8,128)(2,1)}) custom-call(s32[1]{0:T(128)} %bitcast.13.core, bf16[256,1024]{1,0:T(8,128)(2,1)} %get-tuple-element.363.refs_0_, bf16[256,1024]{1,0:T(8,128)(2,1)} %get-tuple-element.364.refs_1_, bf16[256,1152]{1,0:T(8,128)(2,1)} %get-tuple-element.328.refs_2_, ...), custom_call_target="tpu_custom_call" | custom-call | bytes 1 | tf_op jit(solution)/shard_map/weights/pallas_call | solution.py:43
  463.7 9.5 %terms.11 = bf16[1152,896]{1,0:T(8,128)(2,1)} custom-call(bf16[1024,1152]{1,0:T(8,128)(2,1)} %get-tuple-element.379.refs_0_, bf16[1024,1152]{1,0:T(8,128)(2,1)} %get-tuple-element.380.refs_1_, bf16[1024,896]{1,0:T(8,128)(2,1)} %get-tuple-element.381.refs_2_, bf16[1024,896]{1,0:T(8,128)(2,1)} %get-tuple-element.382.refs_3_, ...), custom_call_target="tpu_custom_call" | custom-call | bytes 1 | tf_op jit(solution)/shard_map/terms/pallas_call | solution.py:43
  491.1 36.5 %reduce-scatter.8.cloned.1.call-done = bf16[288,896]{1,0:T(8,128)(2,1)} async-done(((bf16[1152,896]{1,0:T(8,128)(2,1)}), bf16[288,896]{1,0:T(8,128)(2,1)}) %reduce-scatter.8.cloned.1.call-update) | async-done | bytes 516112 | tf_op jit(solution)/shard_map/reduce_scatter | solution.py:1042
  540.2 7.2 %collective-permute-start.56 = (bf16[36,2816]{1,0:T(8,128)(2,1)S(1)}, bf16[36,2816]{1,0:T(8,128)(2,1)S(1)}, u32[]{:S(2)}, u32[]{:S(2)}) collective-permute-start(bf16[36,2816]{1,0:T(8,128)(2,1)S(1)} %copy-done.71), channel_id=1, source_target_pairs={{0,8},{8,16},{16,24},{24,0},{1,9},{9,17},{17,25},{25,1},{2,10},{10... | collective-permute-start | bytes 608264 | tf_op jit(solution)/shard_map/ppermute | solution.py:609
  555.1 9.4 %collective-permute-done.57.refs_2_ = bf16[36,2816]{1,0:T(8,128)(2,1)S(1)} collective-permute-done((bf16[36,2816]{1,0:T(8,128)(2,1)S(1)}, bf16[36,2816]{1,0:T(8,128)(2,1)S(1)}, u32[]{:S(2)}, u32[]{:S(2)}) %collective-permute-start.57) | collective-permute-done | bytes 202784 | tf_op jit(solution)/shard_map/ppermute | solution.py:609
  (312 shorter events, 228.9 us)
Async XLA Ops:
  7.2 109.8 %all-gather.3.cloned.1.call-start = ((), (), s32[]{:S(2)}) async-start(), calls=%async_computation.5 | async-start | bytes 2488320 | tf_op jit(solution)/shard_map/all_gather | solution.py:716
  16.2 148.0 %all-gather.5.cloned.1.call-start = ((), (), s32[]{:S(2)}) async-start(), calls=%async_computation.6 | async-start | bytes 5160960 | tf_op jit(solution)/shard_map/all_gather | solution.py:748
  33.7 366.5 %reduce-scatter.10.cloned.1.call-start = ((), (), s32[]{:S(2)}) async-start(), calls=%async_computation.9 | async-start | bytes 2488320
  165.2 39.3 %collective-permute-start.19 = (bf16[256,1152]{1,0:T(8,128)(2,1)}, bf16[256,1152]{1,0:T(8,128)(2,1)}, u32[]{:S(2)}, u32[]{:S(2)}) collective-permute-start(bf16[256,1152]{1,0:T(8,128)(2,1)} %get-tuple-element.269.refs_3_), channel_id=1, source_target_pairs={{0,6},{1,7},{2,4},{3,5},{4,2},{5,3},{6,0},{7,1},{8,14},{9,15},{10,... | collective-permute-start | bytes 1769480 | tf_op jit(solution)/shard_map/ppermute | solution.py:584
  166.9 37.9 %collective-permute-start.20 = (bf16[256,1152]{1,0:T(8,128)(2,1)}, bf16[256,1152]{1,0:T(8,128)(2,1)}, u32[]{:S(2)}, u32[]{:S(2)}) collective-permute-start(bf16[256,1152]{1,0:T(8,128)(2,1)} %get-tuple-element.269.refs_3_), channel_id=1, source_target_pairs={{0,2},{1,3},{2,0},{3,1},{4,6},{5,7},{6,4},{7,5},{8,10},{9,11},{10,... | collective-permute-start | bytes 1769480 | tf_op jit(solution)/shard_map/ppermute | solution.py:584
  168.6 36.2 %collective-permute-start.21 = (bf16[256,1152]{1,0:T(8,128)(2,1)}, bf16[256,1152]{1,0:T(8,128)(2,1)}, u32[]{:S(2)}, u32[]{:S(2)}) collective-permute-start(bf16[256,1152]{1,0:T(8,128)(2,1)} %get-tuple-element.269.refs_3_), channel_id=1, source_target_pairs={{0,4},{1,5},{2,6},{3,7},{4,0},{5,1},{6,2},{7,3},{8,12},{9,13},{10,... | collective-permute-start | bytes 1769480 | tf_op jit(solution)/shard_map/ppermute | solution.py:584
  201.2 30.2 %collective-permute-start.30 = (bf16[256,1152]{1,0:T(8,128)(2,1)}, bf16[256,1152]{1,0:T(8,128)(2,1)S(1)}, u32[]{:S(2)}, u32[]{:S(2)}) collective-permute-start(bf16[256,1152]{1,0:T(8,128)(2,1)} %get-tuple-element.261), channel_id=1, source_target_pairs={{0,6},{1,7},{2,4},{3,5},{4,2},{5,3},{6,0},{7,1},{8,14},{9,15},{10,... | collective-permute-start | bytes 1769480 | tf_op jit(solution)/shard_map/ppermute | solution.py:584
  236.9 34.0 %collective-permute-start.36 = (bf16[256,1152]{1,0:T(8,128)(2,1)}, bf16[256,1152]{1,0:T(8,128)(2,1)S(1)}, u32[]{:S(2)}, u32[]{:S(2)}) collective-permute-start(bf16[256,1152]{1,0:T(8,128)(2,1)} %get-tuple-element.282.refs_3_), channel_id=1, source_target_pairs={{0,6},{1,7},{2,4},{3,5},{4,2},{5,3},{6,0},{7,1},{8,14},{9,15},{10,... | collective-permute-start | bytes 1769480 | tf_op jit(solution)/shard_map/ppermute | solution.py:584
  238.4 45.5 %collective-permute-start.37 = (bf16[256,1152]{1,0:T(8,128)(2,1)}, bf16[256,1152]{1,0:T(8,128)(2,1)S(1)}, u32[]{:S(2)}, u32[]{:S(2)}) collective-permute-start(bf16[256,1152]{1,0:T(8,128)(2,1)} %get-tuple-element.282.refs_3_), channel_id=1, source_target_pairs={{0,2},{1,3},{2,0},{3,1},{4,6},{5,7},{6,4},{7,5},{8,10},{9,11},{10,... | collective-permute-start | bytes 1769480 | tf_op jit(solution)/shard_map/ppermute | solution.py:584
  245.6 38.3 %collective-permute-start.38 = (bf16[256,1152]{1,0:T(8,128)(2,1)}, bf16[256,1152]{1,0:T(8,128)(2,1)S(1)}, u32[]{:S(2)}, u32[]{:S(2)}) collective-permute-start(bf16[256,1152]{1,0:T(8,128)(2,1)} %get-tuple-element.282.refs_3_), channel_id=1, source_target_pairs={{0,4},{1,5},{2,6},{3,7},{4,0},{5,1},{6,2},{7,3},{8,12},{9,13},{10,... | collective-permute-start | bytes 1769480 | tf_op jit(solution)/shard_map/ppermute | solution.py:584
  263.6 48.0 %collective-permute-start.33 = (bf16[256,1152]{1,0:T(8,128)(2,1)}, bf16[256,1152]{1,0:T(8,128)(2,1)S(1)}, u32[]{:S(2)}, u32[]{:S(2)}) collective-permute-start(bf16[256,1152]{1,0:T(8,128)(2,1)} %get-tuple-element.303.refs_3_), channel_id=1, source_target_pairs={{0,6},{1,7},{2,4},{3,5},{4,2},{5,3},{6,0},{7,1},{8,14},{9,15},{10,... | collective-permute-start | bytes 1769480 | tf_op jit(solution)/shard_map/ppermute | solution.py:584
  264.6 47.0 %collective-permute-start.34 = (bf16[256,1152]{1,0:T(8,128)(2,1)}, bf16[256,1152]{1,0:T(8,128)(2,1)S(1)}, u32[]{:S(2)}, u32[]{:S(2)}) collective-permute-start(bf16[256,1152]{1,0:T(8,128)(2,1)} %get-tuple-element.303.refs_3_), channel_id=1, source_target_pairs={{0,2},{1,3},{2,0},{3,1},{4,6},{5,7},{6,4},{7,5},{8,10},{9,11},{10,... | collective-permute-start | bytes 1769480 | tf_op jit(solution)/shard_map/ppermute | solution.py:584
  270.9 40.7 %collective-permute-start.35 = (bf16[256,1152]{1,0:T(8,128)(2,1)}, bf16[256,1152]{1,0:T(8,128)(2,1)S(1)}, u32[]{:S(2)}, u32[]{:S(2)}) collective-permute-start(bf16[256,1152]{1,0:T(8,128)(2,1)} %get-tuple-element.303.refs_3_), channel_id=1, source_target_pairs={{0,4},{1,5},{2,6},{3,7},{4,0},{5,1},{6,2},{7,3},{8,12},{9,13},{10,... | collective-permute-start | bytes 1769480 | tf_op jit(solution)/shard_map/ppermute | solution.py:584
  341.6 149.5 %reduce-scatter.6.cloned.1.call-start = ((), (), s32[]{:S(2)}) async-start(), calls=%async_computation.7 | async-start | bytes 2580480 | tf_op jit(solution)/shard_map/reduce_scatter | solution.py:1042
  342.6 30.4 %collective-permute-start.43 = (bf16[256,1152]{1,0:T(8,128)(2,1)S(1)}, bf16[256,1152]{1,0:T(8,128)(2,1)S(1)}, u32[]{:S(2)}, u32[]{:S(2)}) collective-permute-start(bf16[256,1152]{1,0:T(8,128)(2,1)S(1)} %copy-done.68), channel_id=1, source_target_pairs={{0,6},{1,7},{2,4},{3,5},{4,2},{5,3},{6,0},{7,1},{8,14},{9,15},{10,... | collective-permute-start | bytes 1769480 | tf_op jit(solution)/shard_map/ppermute | solution.py:584
  382.7 37.9 %collective-permute-start.40 = (bf16[256,1152]{1,0:T(8,128)(2,1)}, bf16[256,1152]{1,0:T(8,128)(2,1)S(1)}, u32[]{:S(2)}, u32[]{:S(2)}) collective-permute-start(bf16[256,1152]{1,0:T(8,128)(2,1)} %get-tuple-element.309), channel_id=1, source_target_pairs={{0,6},{1,7},{2,4},{3,5},{4,2},{5,3},{6,0},{7,1},{8,14},{9,15},{10,... | collective-permute-start | bytes 1769480 | tf_op jit(solution)/shard_map/ppermute | solution.py:584
  383.8 36.9 %collective-permute-start.41 = (bf16[256,1152]{1,0:T(8,128)(2,1)}, bf16[256,1152]{1,0:T(8,128)(2,1)S(1)}, u32[]{:S(2)}, u32[]{:S(2)}) collective-permute-start(bf16[256,1152]{1,0:T(8,128)(2,1)} %get-tuple-element.310), channel_id=1, source_target_pairs={{0,2},{1,3},{2,0},{3,1},{4,6},{5,7},{6,4},{7,5},{8,10},{9,11},{10,... | collective-permute-start | bytes 1769480 | tf_op jit(solution)/shard_map/ppermute | solution.py:584
  385.6 35.1 %collective-permute-start.42 = (bf16[256,1152]{1,0:T(8,128)(2,1)}, bf16[256,1152]{1,0:T(8,128)(2,1)}, u32[]{:S(2)}, u32[]{:S(2)}) collective-permute-start(bf16[256,1152]{1,0:T(8,128)(2,1)} %get-tuple-element.311), channel_id=1, source_target_pairs={{0,4},{1,5},{2,6},{3,7},{4,0},{5,1},{6,2},{7,3},{8,12},{9,13},{10,... | collective-permute-start | bytes 1769480 | tf_op jit(solution)/shard_map/ppermute | solution.py:584
  420.7 106.9 %reduce-scatter.8.cloned.1.call-start = ((), (), s32[]{:S(2)}) async-start(), calls=%async_computation.8 | async-start | bytes 2580480 | tf_op jit(solution)/shard_map/reduce_scatter | solution.py:1042
  420.8 42.9 %collective-permute-start.51 = (bf16[1152,896]{1,0:T(8,128)(2,1)S(1)}, bf16[1152,896]{1,0:T(8,128)(2,1)}, u32[]{:S(2)}, u32[]{:S(2)}) collective-permute-start(bf16[1152,896]{1,0:T(8,128)(2,1)S(1)} %copy-done.10), channel_id=1, source_target_pairs={{0,1},{1,0},{2,3},{3,2},{4,5},{5,4},{6,7},{7,6},{8,9},{9,8},{10,11... | collective-permute-start | bytes 6193160 | tf_op jit(solution)/shard_map/ppermute | solution.py:584
  487.1 44.6 %collective-permute-start.53 = (bf16[144,2816]{1,0:T(8,128)(2,1)}, bf16[144,2816]{1,0:T(8,128)(2,1)S(1)}, u32[]{:S(2)}, u32[]{:S(2)}) collective-permute-start(bf16[144,2816]{1,0:T(8,128)(2,1)} %get-tuple-element.385), channel_id=1, source_target_pairs={{0,2},{1,3},{2,0},{3,1},{4,6},{5,7},{6,4},{7,5},{8,10},{9,11},{10,... | collective-permute-start | bytes 2433032 | tf_op jit(solution)/shard_map/ppermute | solution.py:584
  489.7 42.0 %collective-permute-start.54 = (bf16[144,2816]{1,0:T(8,128)(2,1)}, bf16[144,2816]{1,0:T(8,128)(2,1)S(1)}, u32[]{:S(2)}, u32[]{:S(2)}) collective-permute-start(bf16[144,2816]{1,0:T(8,128)(2,1)} %get-tuple-element.386), channel_id=1, source_target_pairs={{0,4},{1,5},{2,6},{3,7},{4,0},{5,1},{6,2},{7,3},{8,12},{9,13},{10,... | collective-permute-start | bytes 2433032 | tf_op jit(solution)/shard_map/ppermute | solution.py:584
  489.7 42.0 %collective-permute-start.55 = (bf16[144,2816]{1,0:T(8,128)(2,1)}, bf16[144,2816]{1,0:T(8,128)(2,1)}, u32[]{:S(2)}, u32[]{:S(2)}) collective-permute-start(bf16[144,2816]{1,0:T(8,128)(2,1)} %get-tuple-element.387), channel_id=1, source_target_pairs={{0,6},{1,7},{2,4},{3,5},{4,2},{5,3},{6,0},{7,1},{8,14},{9,15},{10,... | collective-permute-start | bytes 2433032 | tf_op jit(solution)/shard_map/ppermute | solution.py:584
  536.4 33.5 %all-to-all-start.1 = ((bf16[8,36,1792]{2,1,0:T(8,128)(2,1)}), bf16[8,36,1792]{2,1,0:T(8,128)(2,1)S(1)}, u32[]{:S(2)}, u32[]{:S(2)}) async-start(bf16[8,36,1792]{2,1,0:T(8,128)(2,1)} %constant_dynamic-update-slice_fusion.4), calls=%async_computation.3 | async-start | bytes 2293760 | tf_op jit(solution)/shard_map/all_to_all | solution.py:1080
  (114 other events, 1048.8 us)
Sparse Core Ops, SparseCore 0:
  9.6 65.7 all-gather.2
  77.5 78.3 all-gather.4
  341.7 51.6 reduce-scatter.9
  420.8 54.4 reduce-scatter.5
  477.7 49.9 reduce-scatter.7

commit v4 on v3

--- a/solution.py
+++ b/solution.py
@@ -224,7 +224,7 @@
         self.buffers = buffers
         self.copies = []
         for index, (source, buffer) in enumerate(zip(sources, buffers)):
-            self.copies.append(pltpu.make_async_copy(source, buffer, sems.at[index]))
+            self.copies.append(pltpu.make_async_copy(source, buffer.at[pl.ds(0, source.shape[0])], sems.at[index]))
         self.used = [False] * len(self.copies)
 
     def start(self, index):
@@ -251,6 +251,10 @@
 
 def lazy_weights(sources, buffers, sems, halves, first):
     weights = Weights(sources, buffers, sems)
+    for source, buffer in zip(sources, buffers):
+        rows = source.shape[0]
+        if rows < buffer.shape[0]:
+            buffer[rows:] = jnp.zeros((buffer.shape[0] - rows, buffer.shape[1]), BF)
     for half in range(halves):
         for kind in first:
             weights.start(kind * halves + half)
@@ -280,10 +284,10 @@
     leaving.wait()
 
 
-def ffn_back_kernel(count, halves, *refs):
+def ffn_back_kernel(count, halves, begin, chained, *refs):
     tokens, refs = refs[:count], refs[count:]
     gelus, rises, sources = refs[:halves], refs[halves : 2 * halves], refs[2 * halves : 4 * halves]
-    t_out, refs = refs[4 * halves], refs[4 * halves + 1 :]
+    t_out, refs = refs[4 * halves + chained], refs[4 * halves + chained + 1 :]
     outs, parts = refs[: 2 * halves], refs[2 * halves : 2 * halves + count]
     refs = refs[2 * halves + count :]
     kept_in, buffers, w_buffers = (refs[i * 2 * halves : (i + 1) * 2 * halves] for i in range(3))
@@ -293,16 +297,16 @@
     rows = tokens[0].shape[0]
     arriving = {}
     for index in range(count):
-        at = pl.ds(index * rows, rows)
+        at, to = pl.ds(index * rows, rows), pl.ds((begin + index) * rows, rows)
         for half in range(halves):
             for kind, source in enumerate((gelus[half], rises[half])):
                 slot = kind * halves + half
-                copy = pltpu.make_async_copy(source.at[at], kept_in[slot].at[at], in_sems.at[index * 2 * halves + slot])
+                copy = pltpu.make_async_copy(source.at[to], kept_in[slot].at[at], in_sems.at[index * 2 * halves + slot])
                 copy.start()
                 arriving[index, slot] = copy
     for index in range(count):
-        at = pl.ds(index * rows, rows)
-        leaving.send(tokens[index], t_out.at[at])
+        at, to = pl.ds(index * rows, rows), pl.ds((begin + index) * rows, rows)
+        leaving.send(tokens[index], t_out.at[to])
 
         def kept(half):
             for slot in (half, halves + half):
@@ -313,7 +317,7 @@
             for kind, value in enumerate(values):
                 slot = kind * halves + half
                 buffers[slot][at] = value
-                leaving.send(buffers[slot].at[at], outs[slot].at[at])
+                leaving.send(buffers[slot].at[at], outs[slot].at[to])
 
         parts[index][...] = ffn_back_rows(tokens[index][...], kept, w_gu, w_down, store)
     leaving.wait()
@@ -331,12 +335,6 @@
                 out[to : to + rows] = ref[start : start + rows]
 
     on_value(place[0], seq, body)
-
-
-def pad_kernel(in_ref, out_ref):
-    rows = in_ref.shape[0]
-    out_ref[:rows] = in_ref[...]
-    out_ref[rows:] = jnp.zeros((out_ref.shape[0] - rows, out_ref.shape[1]), out_ref.dtype)
 
 
 def join_kernel(*refs):
@@ -501,18 +499,13 @@
             body(value)
 
 
-def line_kernel(place, *refs):
-    blocks, (in_ref, out_ref) = refs[:-2], refs[-2:]
-    count, columns = len(blocks), in_ref.shape[1]
+def line_kernel(both_ref, in_ref, out_ref):
+    count, columns = both_ref.shape[0], in_ref.shape[1]
     in_rows, out_rows = in_ref.shape[0] // count, out_ref.shape[0] // count
-
-    def body(d):
-        for by, ref in enumerate(blocks):
-            at = (d - by) % count
-            in_ref[at * in_rows : (at + 1) * in_rows] = ref[0, :in_rows, :columns]
-            out_ref[at * out_rows : (at + 1) * out_rows] = ref[0, :out_rows, columns:]
-
-    on_value(place[0], count, body)
+    end = columns + out_ref.shape[1]
+    for at in range(count):
+        in_ref[at * in_rows : (at + 1) * in_rows] = both_ref[at, :in_rows, :columns]
+        out_ref[at * out_rows : (at + 1) * out_rows] = both_ref[at, :out_rows, columns:end]
 
 
 def terms_kernel(count, kinds, has_got, *refs):
@@ -703,8 +696,10 @@
     if split:
         orows = outproj.shape[0]
         both = jnp.concatenate([packed, jnp.pad(outproj, ((0, wrows - orows), (0, 0)))], axis=1)
+        least = -(-(2**19) // (dp * wrows * LANES)) * LANES
+        both = jnp.pad(both, ((0, 0), (0, max(0, least - both.shape[1]))))
         both = order.step(lax.optimization_barrier(both[None]))
-        line = [around(both, by, dp) for by in range(1, dp)]
+        line = lax.all_gather(both, "dp", axis=0, tiled=True)
 
     [gate_up] = call(
         functools.partial(owner_kernel, dp),
@@ -713,14 +708,17 @@
         [(shape((seq, wrows, 2 * pad), BF), VMEM)],
         name="owner",
     )
+    gate_up = lax.all_to_all(gate_up, "seq", 0, 0).reshape(seq * wrows, 2 * pad)
+    w_gu = [lax.all_gather(gate_up, "dp", axis=0, tiled=True)]
+    if split:
+        cosine, sine, line = order.step(order.behind((cosine, sine, line)))
+        downproj = after(downproj, line)
     w_down = lax.all_gather(downproj, "dp", axis=0, tiled=True)
-    gate_up = lax.all_to_all(gate_up, "seq", 0, 0).reshape(seq * wrows, 2 * pad)
     if split:
-        gate_up, cosine, sine = order.step(order.behind((gate_up, cosine, sine)))
         in_line, out_line = call(
             line_kernel,
             None,
-            [(along_dp, SMEM)] + [plain(block) for block in [both] + order.behind(line)],
+            [plain(line)],
             [(shape((dp * wrows, ind + LANES), BF), VMEM), (shape((dp * orows, width), BF), VMEM)],
             name="line",
         )
@@ -745,7 +743,7 @@
     else:
         w_in = lax.all_gather(packed[None], BOTH, axis=0, tiled=True).reshape(width, -1)
         w_out = lax.all_gather(outproj, BOTH, axis=0, tiled=True)
-    w_gu = [lax.all_gather(gate_up, "dp", axis=0, tiled=True)]
+
     def of_micro(array, index):
         dims = array.shape[1:]
         return (array, pl.BlockSpec((1,) + dims, lambda *_: (index,) + (0,) * len(dims)))
@@ -782,14 +780,8 @@
     if split:
         out_lines = order.step(order.behind(out_lines))
         out_lines = out_lines + [xor_permute(line, 1, seq) for line in out_lines]
-        out_lines, w_down = order.step(order.behind((out_lines, w_down)))
+        out_lines = order.step(order.behind(out_lines))
         w_out = order.step(untangle(out_lines, "untangle_out"))
-    [w_down] = call(
-        pad_kernel, None, [plain(order.behind(w_down))], [(shape((pad, width), BF), VMEM)], name="pad"
-    )
-    w_down = [order.step(w_down)]
-    if split:
-        w_down = w_down + [xor_permute(w_down[0], 1, seq)]
     states = []
     for index in range(micro):
         place = order.behind(jnp.stack([lengths[index], base]))
@@ -812,6 +804,10 @@
     if split:
         states[0]["sent"] = order.step(order.behind(states[0]["sent"]))
         w_gu.append(xor_permute(order.step(order.behind(w_gu[0])), 1, seq))
+        w_down = [order.step(order.behind(w_down))]
+        w_down.append(xor_permute(w_down[0], 1, seq))
+    else:
+        w_down = [jnp.pad(w_down, ((0, pad - own_ff), (0, 0)))]
     halves = len(w_gu)
 
     def blocks(array):
@@ -856,7 +852,7 @@
         kinds = [results[1 + i * halves : 1 + (i + 1) * halves] for i in range(3)]
         return results[0], *kinds, results[1 + 3 * halves :]
 
-    def ffn_backward(pieces, gelu, rise):
+    def ffn_backward(pieces, gelu, rise, begin=0, total=0, kept=()):
         if not split:
             count = pieces[0].shape[0] // rows
             results = call(
@@ -870,18 +866,19 @@
             )
             return pieces[0], results[:1], results[1:2], results[2:]
         count = len(pieces)
+        arrays = [*gelu, *rise, *w_gu, *w_down, *kept]
         results = call(
-            functools.partial(ffn_back_kernel, count, halves),
+            functools.partial(ffn_back_kernel, count, halves, begin, len(kept)),
             None,
-            [plain(piece) for piece in pieces]
-            + [(array, any_spec) for array in [*gelu, *rise, *w_gu, *w_down]],
-            [(shape((count * rows, width), BF), any_spec)]
-            + [(shape((count * rows, pad), BF), any_spec)] * (2 * halves)
+            [plain(piece) for piece in pieces] + [(array, any_spec) for array in arrays],
+            [(shape((total * rows, width), BF), any_spec)]
+            + [(shape((total * rows, pad), BF), any_spec)] * (2 * halves)
             + [(shape((rows, width), BF), VMEM)] * count,
             scratch=[pltpu.VMEM((count * rows, pad), BF)] * (4 * halves)
             + w_scratch
             + [pltpu.SemaphoreType.DMA((count * (1 + 2 * halves),)), pltpu.SemaphoreType.DMA((count * 2 * halves,))]
             + [pltpu.SemaphoreType.DMA((2 * halves,))],
+            aliases={count + len(arrays) - len(kept) + index: index for index in range(len(kept))},
             name="ffn_back",
         )
         return results[0], results[1 : 1 + halves], results[1 + halves : 1 + 2 * halves], results[1 + 2 * halves :]
@@ -901,24 +898,6 @@
         s["tokens"], s["gelu"], s["rise"], s["act"], parts = ffn(pieces)
         order.step(parts)
         s["terms"] = scatter(parts)
-
-    layer_out = None
-    result = shape((micro, 1, rows, width), F32)
-    for index, s in enumerate(states):
-        parts = s["terms"]
-        chain = [] if layer_out is None else [(layer_out, pl.BlockSpec(memory_space=pl.ANY))]
-        layer_out, s["d_ffn"], s["t_post"] = call(
-            functools.partial(middle_kernel, len(parts), bool(chain)),
-            (1,),
-            [full(p) for p in parts]
-            + [of_micro(out_cotangent, index), full(s["hidden"]), full(order.behind(gains))]
-            + chain,
-            [(result, of_micro(result, index)[1]), new((rows, width), BF), new((1, width), F32)],
-            aliases={len(parts) + 3: 0} if chain else None,
-            name="middle",
-        )
-        order.step(s["d_ffn"])
-        s["sent"] = near_blocks(s["d_ffn"], seq, BITS) if split else None
 
     def join(pieces):
         [joined] = call(
@@ -959,27 +938,58 @@
     def own_terms(left, right, other, high_out=None):
         return over_tokens(left, [right], 0, [xor_permute(other, 1, seq)] if split else (), high_out)[0]
 
-    def ffn_back(s):
-        pieces = pieces_of(s["d_ffn"], s["sent"])
-        tokens, s["d_gate"], s["d_up"], parts = ffn_backward(pieces, s["gelu"], s["rise"])
+    def ffn_back(s, which):
+        if not split:
+            if which == "rest":
+                pieces = pieces_of(s["d_ffn"], s["sent"])
+                s["d_tokens"], s["d_gate"], s["d_up"], parts = ffn_backward(pieces, s["gelu"], s["rise"])
+                s["terms"] = scatter(order.step(parts))
+            return
+        own, others = [order.behind(s["d_ffn"])], list(s["sent"])
+        total = len(own) + len(others)
+        if which == "own":
+            s["kept"] = ffn_backward(own, s["gelu"], s["rise"], len(others), total)
+            order.step(s["kept"][-1])
+            return
+        tokens, d_gate, d_up, last = s["kept"]
+        others[0] = order.behind(others[0])
+        tokens, s["d_gate"], s["d_up"], parts = ffn_backward(
+            others, s["gelu"], s["rise"], 0, total, [tokens, *d_gate, *d_up]
+        )
         s.setdefault("d_tokens", tokens)
-        order.step(parts)
-        s["terms"] = scatter(parts)
+        s["terms"] = scatter(order.step(list(parts)) + list(last))
+
+    layer_out = None
+    result = shape((micro, 1, rows, width), F32)
+    for index, s in enumerate(states):
+        parts = s["terms"]
+        chain = [] if layer_out is None else [(layer_out, pl.BlockSpec(memory_space=pl.ANY))]
+        layer_out, s["d_ffn"], s["t_post"] = call(
+            functools.partial(middle_kernel, len(parts), bool(chain)),
+            (1,),
+            [full(p) for p in parts]
+            + [of_micro(out_cotangent, index), full(s["hidden"]), full(order.behind(gains))]
+            + chain,
+            [(result, of_micro(result, index)[1]), new((rows, width), BF), new((1, width), F32)],
+            aliases={len(parts) + 3: 0} if chain else None,
+            name="middle",
+        )
+        order.step(s["d_ffn"])
+        s["sent"] = near_blocks(s["d_ffn"], seq, BITS) if split else None
+        ffn_back(s, "own")
 
     for s in states[:-1]:
-        ffn_back(s)
+        ffn_back(s, "rest")
     late = states[-1]
     if split:
         late["sent"] = order.step(order.behind(late["sent"]))
         late["d_tokens"] = order.step(join(list(late["sent"]) + [late["d_ffn"]]))
-        down_terms = own_terms("act", "d_tokens", other_terms("act", "d_tokens", own_ff), own_ff)
-        ffn_back(late)
-    else:
-        ffn_back(late)
-        down_terms = own_terms("act", "d_tokens", None, own_ff)
-    down_grad = lax.psum_scatter(down_terms, "dp", scatter_dimension=0, tiled=True)
+        down_other = other_terms("act", "d_tokens", own_ff)
+    ffn_back(late, "rest")
+    down_terms = own_terms("act", "d_tokens", down_other if split else None, own_ff)
     for s in states[:-1]:
         s["terms"] = order.step(order.behind(s["terms"]))
+    down_grad = lax.psum_scatter(order.behind(down_terms), "dp", scatter_dimension=0, tiled=True)
 
     def attend_back(index):
         s = states[index]
@@ -1043,12 +1053,11 @@
     gate_other = other_terms("tokens", "d_gate")
     for index in range(micro - 1):
         attend_back(index)
-    down_grad = order.step(order.behind(down_grad))
     gate_terms = own_terms("tokens", "d_gate", gate_other)
     up_other = other_terms("tokens", "d_up")
     for s in states[:-1]:
         s["d_pairs"] = order.step(order.behind(s["d_pairs"]))
-    states[-1]["terms"] = order.step(order.behind(states[-1]["terms"]))
+    states[-1]["terms"], down_grad = order.step(order.behind((states[-1]["terms"], down_grad)))
     gate_sum = scattered(order.behind(gate_terms))
     attend_back(micro - 1)
     for index in range(micro):
@@ -1074,10 +1083,11 @@
         got = xor_permute(other, 1, seq)
         up_sum = scattered(own_terms("tokens", "d_up", up_other))
         in_parts = fold_chips(mine, got, dp, seq, order)
+        in_parts = order.step(order.behind(in_parts))
         both_sums = [part.reshape(seq, wrows, pad) for part in order.behind((gate_sum, up_sum))]
         both_sums = order.step(jnp.concatenate(both_sums, axis=2))
+        both_sums = lax.all_to_all(both_sums, "seq", 0, 0)
         in_parts = fold_line(in_parts, dp, order)
-        both_sums = lax.all_to_all(order.behind(both_sums), "seq", 0, 0)
         gate_grad, up_grad = (columns_of(both_sums, index) for index in range(2))
     else:
         up_sum = scattered(own_terms("tokens", "d_up", None))

time: 593 us -> 571 us (0.963)
  waiting for transfers between devices: 189 us -> 153 us
  blocking collectives: 0 us -> 21.6 us
  starting transfers between devices: 81.6 us -> 66.7 us
  Pallas kernels: 265 us -> 271 us
    reduce_scatter x2, waiting for transfers between devices: 36.5 us -> 0.01 us  [shards(): lax.psum_scatter(terms, 'dp', scatter_dimension=0, tiled=True)]
    ppermute x6 -> x3, waiting for transfers between devices: 38.3 us -> 14.3 us  [around(): return lax.ppermute(value, 'dp', [(i, (i + by) % dp) for i in range(dp)])]
    all_gather x1, waiting for transfers between devices: 0.02 us -> 23.8 us  [shards(): w_down = lax.all_gather(downproj, 'dp', axis=0, tiled=True)]
    all_to_all x0 -> x1, blocking collectives: none -> 21.6 us  [shards(): gate_up = lax.all_to_all(gate_up, 'seq', 0, 0).reshape(seq * wrows, 2 * pad)]
    all_to_all x2 -> x1, waiting for transfers between devices: 14 us -> 0.01 us  [shards(): both_sums = lax.all_to_all(both_sums, 'seq', 0, 0)]
    ppermute x6 -> x3, starting transfers between devices: 15.3 us -> 3.86 us  [around(): return lax.ppermute(value, 'dp', [(i, (i + by) % dp) for i in range(dp)])]
    ppermute x47, waiting for transfers between devices: 89.5 us -> 96.5 us  [xor_permute(): return lax.ppermute(value, 'seq', [(i, i ^ bit) for i in range(size)])]
    pallas_call x31 -> x32, Pallas kernels: 265 us -> 271 us  [call(): pl.pallas_call(body, **{} if grid is None else {'grid': grid}, in_specs=[...]
  transfers between devices with their start and end apart: 66 -> 63, of which waited for: 25 -> 21; matrix products, arithmetic and copies ran while one was open for 2% -> 2% of each run, Pallas kernels for 40% -> 45%
where the time goes in v4:
time: 571 us; the launch traced here: 561 us
  Pallas kernels  271 us (47%)
  waiting for transfers between devices  153 us (27%)
  starting transfers between devices  66.7 us (12%)
  local copies, waits for them, and re-layouts  28.7 us (5%)
  blocking collectives  21.6 us (4%)
  between operations  15.1 us (3%)
    pallas_call x32, Pallas kernels, call(): pl.pallas_call(body, **{} if grid is None else {'grid': grid}, in_specs=[...  271 us
    ppermute x47, waiting for transfers between devices, xor_permute(): return lax.ppermute(value, 'seq', [(i, i ^ bit) for i in range(size)])  96.5 us
    ppermute x47, starting transfers between devices, xor_permute(): return lax.ppermute(value, 'seq', [(i, i ^ bit) for i in range(size)])  47.7 us
    all_gather x1, waiting for transfers between devices, shards(): w_down = lax.all_gather(downproj, 'dp', axis=0, tiled=True)  23.8 us
    all_to_all x1, blocking collectives, shards(): gate_up = lax.all_to_all(gate_up, 'seq', 0, 0).reshape(seq * wrows, 2 * pad)  21.6 us
    unnamed x127, local copies, waits for them, and re-layouts  19.2 us
    ppermute x3, waiting for transfers between devices, around(): return lax.ppermute(value, 'dp', [(i, (i + by) % dp) for i in range(dp)])  14.3 us
    ppermute x6, waiting for transfers between devices, from_behind(): return lax.ppermute(value, 'seq', pairs)  12.3 us
  transfers between devices with their start and end apart: 63, of which 21 were waited for; matrix products, arithmetic and copies ran while one was open for 2% of the time, Pallas kernels for 45%

profile of v4, /device:TPU:0, one launch (start us, length us, event | category | flops | bytes accessed | tf_op | source)
XLA Modules:
  0.0 560.9 jit_solution(10575742683114445560)
XLA Ops:
  15.6 21.6 %all_to_all.10 = bf16[8,36,1792]{2,1,0:T(8,128)(2,1)S(1)} all-to-all(bf16[8,36,1792]{2,1,0:T(8,128)(2,1)} %owner.1), channel_id=1, replica_groups=mesh['dp'=4,'seq'=8] {'seq'}, dimensions={0} | all-to-all | bytes 2064384 | tf_op jit(solution)/shard_map/all_to_all | solution.py:711
  51.9 10.6 %collective-permute-done.refs_1_ = bf16[144,1664]{1,0:T(8,128)(2,1)S(1)} collective-permute-done((bf16[144,1664]{1,0:T(8,128)(2,1)}, bf16[144,1664]{1,0:T(8,128)(2,1)S(1)}, u32[]{:S(2)}, u32[]{:S(2)}) %collective-permute-start) | collective-permute-done | bytes 479264 | tf_op jit(solution)/shard_map/ppermute | solution.py:577
  62.5 9.7 %collective-permute-done.1.refs_2_ = bf16[144,1664]{1,0:T(8,128)(2,1)S(1)} collective-permute-done((bf16[144,1664]{1,0:T(8,128)(2,1)}, bf16[144,1664]{1,0:T(8,128)(2,1)S(1)}, u32[]{:S(2)}, u32[]{:S(2)}) %collective-permute-start.1) | collective-permute-done | bytes 479264 | tf_op jit(solution)/shard_map/ppermute | solution.py:577
  131.3 14.0 %collective-permute-done.20.refs_1_ = bf16[256,1152]{1,0:T(8,128)(2,1)S(1)} collective-permute-done((bf16[256,1152]{1,0:T(8,128)(2,1)}, bf16[256,1152]{1,0:T(8,128)(2,1)S(1)}, u32[]{:S(2)}, u32[]{:S(2)}) %collective-permute-start.20) | collective-permute-done | bytes 589856 | tf_op jit(solution)/shard_map/ppermute | solution.py:577
  147.5 23.8 %all-gather.6.cloned.1.call-done.refs_6_.refs_7_.refs_9_ = bf16[864,1152]{1,0:T(8,128)(2,1)} async-done(((bf16[216,1152]{1,0:T(8,128)(2,1)}), bf16[864,1152]{1,0:T(8,128)(2,1)}) %all-gather.6.cloned.1.call-update) | async-done | bytes 1990672 | tf_op jit(solution)/shard_map/all_gather | solution.py:716
  176.8 23.5 %ffn.2 = (bf16[1024,1152]{1,0:T(8,128)(2,1)}, bf16[1024,896]{1,0:T(8,128)(2,1)}, bf16[1024,896]{1,0:T(8,128)(2,1)}, bf16[1024,896]{1,0:T(8,128)(2,1)}, bf16[1024...) custom-call(bf16[256,1152]{1,0:T(8,128)(2,1)} %copy-done.18, ...), custom_call_target="tpu_custom_call" | custom-call | bytes 1 | tf_op jit(solution)/shard_map/ffn/pallas_call | solution.py:43
  205.6 23.4 %ffn.3 = (bf16[1024,1152]{1,0:T(8,128)(2,1)}, bf16[1024,896]{1,0:T(8,128)(2,1)}, bf16[1024,896]{1,0:T(8,128)(2,1)}, bf16[1024,896]{1,0:T(8,128)(2,1)}, bf16[1024...) custom-call(bf16[256,1152]{1,0:T(8,128)(2,1)} %copy-done.22, ...), custom_call_target="tpu_custom_call" | custom-call | bytes 1 | tf_op jit(solution)/shard_map/ffn/pallas_call | solution.py:43
  240.7 10.2 %ffn_back.4 = (bf16[1024,1152]{1,0:T(8,128)(2,1)}, bf16[1024,896]{1,0:T(8,128)(2,1)}, bf16[1024,896]{1,0:T(8,128)(2,1)}, bf16[1024,896]{1,0:T(8,128)(2,1)}, bf16...) custom-call(bf16[256,1152]{1,0:T(8,128)(2,1)} %get-tuple-element.288.refs_0_, ...), custom_call_target="tpu_custom_call" | custom-call | bytes 1 | tf_op jit(solution)/shard_map/ffn_back/pallas_call | solution.py:43
  251.5 7.7 %collective-permute-done.25.refs_2_ = bf16[256,1152]{1,0:T(8,128)(2,1)S(1)} collective-permute-done((bf16[256,1152]{1,0:T(8,128)(2,1)}, bf16[256,1152]{1,0:T(8,128)(2,1)S(1)}, u32[]{:S(2)}, u32[]{:S(2)}) %collective-permute-start.25) | collective-permute-done | bytes 589856 | tf_op jit(solution)/shard_map/ppermute | solution.py:577
  273.3 10.1 %ffn_back.5 = (bf16[1024,1152]{1,0:T(8,128)(2,1)}, bf16[1024,896]{1,0:T(8,128)(2,1)}, bf16[1024,896]{1,0:T(8,128)(2,1)}, bf16[1024,896]{1,0:T(8,128)(2,1)}, bf16...) custom-call(bf16[256,1152]{1,0:T(8,128)(2,1)} %get-tuple-element.298.refs_0_.refs_3_, ...), custom_call_target="tpu_custom_call" | custom-call | bytes 1 | tf_op jit(solution)/shard_map/ffn_back/pallas_call | solution.py:43
  285.6 21.1 %ffn_back.6 = (bf16[1024,1152]{1,0:T(8,128)(2,1)}, bf16[1024,896]{1,0:T(8,128)(2,1)}, bf16[1024,896]{1,0:T(8,128)(2,1)}, bf16[1024,896]{1,0:T(8,128)(2,1)}, bf16...) custom-call(bf16[256,1152]{1,0:T(8,128)(2,1)} %copy-done.31, ...), custom_call_target="tpu_custom_call", output_to_operand_aliasing={{0}: (11, {}), {1}: (12, {}), {2}: (13, {}), {3}: (14, {}),... | custom-call | bytes 1 | tf_op jit(solution)/shard_map/ffn_back/pallas_call | solution.py:43
  312.3 10.1 %terms.6 = bf16[864,1152]{1,0:T(8,128)(2,1)} custom-call(bf16[1024,896]{1,0:T(8,128)(2,1)} %get-tuple-element.318.refs_0_, bf16[1024,896]{1,0:T(8,128)(2,1)} %get-tuple-element.319.refs_1_, bf16[1024,1152]{1,0:T(8,128)(2,1)} %get-tuple-element.320.refs_2_, bf16[1024,1152]{1,0:T(8,128)(2,1)} %join.1.refs_3_), custom_call_target="tpu_custom_call" | custom-call | bytes 1 | tf_op jit(solution)/shard_map/terms/pallas_call | solution.py:43
  326.0 20.7 %ffn_back.7 = (bf16[1024,1152]{1,0:T(8,128)(2,1)}, bf16[1024,896]{1,0:T(8,128)(2,1)}, bf16[1024,896]{1,0:T(8,128)(2,1)}, bf16[1024,896]{1,0:T(8,128)(2,1)}, bf16...) custom-call(bf16[256,1152]{1,0:T(8,128)(2,1)} %copy-done.5, ...), custom_call_target="tpu_custom_call", output_to_operand_aliasing={{0}: (11, {}), {1}: (12, {}), {2}: (13, {}), {3}: (14, {}),... | custom-call | bytes 1 | tf_op jit(solution)/shard_map/ffn_back/pallas_call | solution.py:43
  348.1 10.5 %terms.7 = bf16[864,1152]{1,0:T(8,128)(2,1)} custom-call(bf16[1024,896]{1,0:T(8,128)(2,1)} %get-tuple-element.332.refs_0_, bf16[1024,896]{1,0:T(8,128)(2,1)} %get-tuple-element.333.refs_1_, bf16[1024,1152]{1,0:T(8,128)(2,1)} %get-tuple-element.320.refs_2_, bf16[1024,1152]{1,0:T(8,128)(2,1)} %join.1.refs_3_, bf16[864,1152]{1,0:T(8,128)(2,1)} %copy-done.10), custom_call_target="tpu_custom_call" | custom-call | bytes 1 | tf_op jit(solution)/shard_map/terms/pallas_call | solution.py:43
  358.7 9.4 %terms.8 = bf16[1152,896]{1,0:T(8,128)(2,1)} custom-call(bf16[1024,1152]{1,0:T(8,128)(2,1)} %get-tuple-element.402.refs_0_, bf16[1024,1152]{1,0:T(8,128)(2,1)} %get-tuple-element.403.refs_1_, bf16[1024,896]{1,0:T(8,128)(2,1)} %get-tuple-element.343.refs_2_, bf16[1024,896]{1,0:T(8,128)(2,1)} %get-tuple-element.344.refs_3_), custom_call_target="tpu_custom_call" | custom-call | bytes 1 | tf_op jit(solution)/shard_map/terms/pallas_call | solution.py:43
  371.8 11.2 %attend_back.2 = (f32[256,1152]{1,0:T(8,128)}, bf16[256,1152]{1,0:T(8,128)(2,1)}, bf16[256,1024]{1,0:T(8,128)(2,1)}, f32[1,1152]{1,0:T(1,128)}, f32[1,1152]{1,0:...) custom-call(s32[2]{0:T(128)} %pad_add_fusion.1.place, ...), custom_call_target="tpu_custom_call" | custom-call | bytes 1 | tf_op jit(solution)/shard_map/attend_back/pallas_call | solution.py:43
  385.6 9.9 %terms.9 = bf16[1152,896]{1,0:T(8,128)(2,1)} custom-call(bf16[1024,1152]{1,0:T(8,128)(2,1)} %get-tuple-element.402.refs_0_, bf16[1024,1152]{1,0:T(8,128)(2,1)} %get-tuple-element.403.refs_1_, bf16[1024,896]{1,0:T(8,128)(2,1)} %get-tuple-element.354.refs_2_, bf16[1024,896]{1,0:T(8,128)(2,1)} %get-tuple-element.355.refs_3_, bf16[1152,896]{1,0:T(8,128)(2,1)} %copy-done.9), custom_call_target="tpu_custom_call" | custom-call | bytes 1 | tf_op jit(solution)/shard_map/terms/pallas_call | solution.py:43
  395.5 8.9 %terms.10 = bf16[1152,896]{1,0:T(8,128)(2,1)} custom-call(bf16[1024,1152]{1,0:T(8,128)(2,1)} %get-tuple-element.402.refs_0_, bf16[1024,1152]{1,0:T(8,128)(2,1)} %get-tuple-element.403.refs_1_, bf16[1024,896]{1,0:T(8,128)(2,1)} %get-tuple-element.358.refs_2_, bf16[1024,896]{1,0:T(8,128)(2,1)} %get-tuple-element.359.refs_3_), custom_call_target="tpu_custom_call" | custom-call | bytes 1 | tf_op jit(solution)/shard_map/terms/pallas_call | solution.py:43
  407.7 11.1 %attend_back.3 = (f32[256,1152]{1,0:T(8,128)}, bf16[256,1152]{1,0:T(8,128)(2,1)}, bf16[256,1024]{1,0:T(8,128)(2,1)}, f32[1,1152]{1,0:T(1,128)}, f32[1,1152]{1,0:...) custom-call(s32[2]{0:T(128)} %pad_add_fusion.place, ...), custom_call_target="tpu_custom_call" | custom-call | bytes 1 | tf_op jit(solution)/shard_map/attend_back/pallas_call | solution.py:43
  439.7 9.7 %weights.1 = (bf16[576,2816]{1,0:T(8,128)(2,1)}, bf16[576,2816]{1,0:T(8,128)(2,1)}) custom-call(s32[1]{0:T(128)} %bitcast.13.core, bf16[256,1024]{1,0:T(8,128)(2,1)} %get-tuple-element.386.refs_0_, bf16[256,1024]{1,0:T(8,128)(2,1)} %get-tuple-element.387.refs_1_, bf16[256,1152]{1,0:T(8,128)(2,1)} %get-tuple-element.351.refs_2_, ...), custom_call_target="tpu_custom_call" | custom-call | bytes 1 | tf_op jit(solution)/shard_map/weights/pallas_call | solution.py:43
  449.5 9.5 %terms.11 = bf16[1152,896]{1,0:T(8,128)(2,1)} custom-call(bf16[1024,1152]{1,0:T(8,128)(2,1)} %get-tuple-element.402.refs_0_, bf16[1024,1152]{1,0:T(8,128)(2,1)} %get-tuple-element.403.refs_1_, bf16[1024,896]{1,0:T(8,128)(2,1)} %get-tuple-element.404.refs_2_, bf16[1024,896]{1,0:T(8,128)(2,1)} %get-tuple-element.405.refs_3_, ...), custom_call_target="tpu_custom_call" | custom-call | bytes 1 | tf_op jit(solution)/shard_map/terms/pallas_call | solution.py:43
  477.5 17.2 %collective-permute-done.50.refs_1_ = bf16[144,2816]{1,0:T(8,128)(2,1)S(1)} collective-permute-done((bf16[144,2816]{1,0:T(8,128)(2,1)}, bf16[144,2816]{1,0:T(8,128)(2,1)S(1)}, u32[]{:S(2)}, u32[]{:S(2)}) %collective-permute-start.50) | collective-permute-done | bytes 811040 | tf_op jit(solution)/shard_map/ppermute | solution.py:577
  494.6 16.7 %collective-permute-done.51.refs_2_ = bf16[144,2816]{1,0:T(8,128)(2,1)S(1)} collective-permute-done((bf16[144,2816]{1,0:T(8,128)(2,1)}, bf16[144,2816]{1,0:T(8,128)(2,1)S(1)}, u32[]{:S(2)}, u32[]{:S(2)}) %collective-permute-start.51) | collective-permute-done | bytes 811040 | tf_op jit(solution)/shard_map/ppermute | solution.py:577
  534.1 8.7 %collective-permute-done.54.refs_2_ = bf16[36,2816]{1,0:T(8,128)(2,1)S(1)} collective-permute-done((bf16[36,2816]{1,0:T(8,128)(2,1)}, bf16[36,2816]{1,0:T(8,128)(2,1)S(1)}, u32[]{:S(2)}, u32[]{:S(2)}) %collective-permute-start.54) | collective-permute-done | bytes 202784 | tf_op jit(solution)/shard_map/ppermute | solution.py:602
  (288 shorter events, 216.6 us)
Async XLA Ops:
  7.2 39.0 %all-gather.4.cloned.1.call-start = ((), (), s32[]{:S(2)}) async-start(), calls=%async_computation.5 | async-start | bytes 1484800 | tf_op jit(solution)/shard_map/all_gather | solution.py:702
  12.8 133.4 %all-gather.8.cloned.1.call-start = ((), (), s32[]{:S(2)}) async-start(), calls=%async_computation.7 | async-start | bytes 5160960 | tf_op jit(solution)/shard_map/all_gather | solution.py:712
  38.3 133.0 %all-gather.6.cloned.1.call-start = ((), (), s32[]{:S(2)}) async-start(), calls=%async_computation.6 | async-start | bytes 2488320 | tf_op jit(solution)/shard_map/all_gather | solution.py:716
  97.3 308.8 %reduce-scatter.10.cloned.1.call-start = ((), (), s32[]{:S(2)}) async-start(), calls=%async_computation.10 | async-start | bytes 2488320
  171.3 32.1 %collective-permute-start.16 = (bf16[256,1152]{1,0:T(8,128)(2,1)}, bf16[256,1152]{1,0:T(8,128)(2,1)S(1)}, u32[]{:S(2)}, u32[]{:S(2)}) collective-permute-start(bf16[256,1152]{1,0:T(8,128)(2,1)} %get-tuple-element.279.refs_3_), channel_id=1, source_target_pairs={{0,6},{1,7},{2,4},{3,5},{4,2},{5,3},{6,0},{7,1},{8,14},{9,15},{10,... | collective-permute-start | bytes 1769480 | tf_op jit(solution)/shard_map/ppermute | solution.py:577
  200.4 31.6 %collective-permute-start.27 = (bf16[256,1152]{1,0:T(8,128)(2,1)}, bf16[256,1152]{1,0:T(8,128)(2,1)S(1)}, u32[]{:S(2)}, u32[]{:S(2)}) collective-permute-start(bf16[256,1152]{1,0:T(8,128)(2,1)} %get-tuple-element.271), channel_id=1, source_target_pairs={{0,6},{1,7},{2,4},{3,5},{4,2},{5,3},{6,0},{7,1},{8,14},{9,15},{10,... | collective-permute-start | bytes 1769480 | tf_op jit(solution)/shard_map/ppermute | solution.py:577
  237.7 34.1 %collective-permute-start.33 = (bf16[256,1152]{1,0:T(8,128)(2,1)}, bf16[256,1152]{1,0:T(8,128)(2,1)S(1)}, u32[]{:S(2)}, u32[]{:S(2)}) collective-permute-start(bf16[256,1152]{1,0:T(8,128)(2,1)} %get-tuple-element.288.refs_0_), channel_id=1, source_target_pairs={{0,6},{1,7},{2,4},{3,5},{4,2},{5,3},{6,0},{7,1},{8,14},{9,15},{10,... | collective-permute-start | bytes 1769480 | tf_op jit(solution)/shard_map/ppermute | solution.py:577
  240.1 44.4 %collective-permute-start.34 = (bf16[256,1152]{1,0:T(8,128)(2,1)}, bf16[256,1152]{1,0:T(8,128)(2,1)S(1)}, u32[]{:S(2)}, u32[]{:S(2)}) collective-permute-start(bf16[256,1152]{1,0:T(8,128)(2,1)} %get-tuple-element.288.refs_0_), channel_id=1, source_target_pairs={{0,2},{1,3},{2,0},{3,1},{4,6},{5,7},{6,4},{7,5},{8,10},{9,11},{10,... | collective-permute-start | bytes 1769480 | tf_op jit(solution)/shard_map/ppermute | solution.py:577
  250.9 33.6 %collective-permute-start.35 = (bf16[256,1152]{1,0:T(8,128)(2,1)S(1)}, bf16[256,1152]{1,0:T(8,128)(2,1)S(1)}, u32[]{:S(2)}, u32[]{:S(2)}) collective-permute-start(bf16[256,1152]{1,0:T(8,128)(2,1)S(1)} %copy-done.19), channel_id=1, source_target_pairs={{0,4},{1,5},{2,6},{3,7},{4,0},{5,1},{6,2},{7,3},{8,12},{9,13},{10,... | collective-permute-start | bytes 1769480 | tf_op jit(solution)/shard_map/ppermute | solution.py:577
  264.2 42.5 %collective-permute-start.30 = (bf16[256,1152]{1,0:T(8,128)(2,1)}, bf16[256,1152]{1,0:T(8,128)(2,1)S(1)}, u32[]{:S(2)}, u32[]{:S(2)}) collective-permute-start(bf16[256,1152]{1,0:T(8,128)(2,1)} %get-tuple-element.298.refs_0_.refs_3_), channel_id=1, source_target_pairs={{0,6},{1,7},{2,4},{3,5},{4,2},{5,3},{6,0},{7,1},{8,14},{9,15},{10,... | collective-permute-start | bytes 1769480 | tf_op jit(solution)/shard_map/ppermute | solution.py:577
  266.4 41.6 %collective-permute-start.31 = (bf16[256,1152]{1,0:T(8,128)(2,1)}, bf16[256,1152]{1,0:T(8,128)(2,1)S(1)}, u32[]{:S(2)}, u32[]{:S(2)}) collective-permute-start(bf16[256,1152]{1,0:T(8,128)(2,1)} %get-tuple-element.298.refs_0_.refs_3_), channel_id=1, source_target_pairs={{0,2},{1,3},{2,0},{3,1},{4,6},{5,7},{6,4},{7,5},{8,10},{9,11},{10,... | collective-permute-start | bytes 1769480 | tf_op jit(solution)/shard_map/ppermute | solution.py:577
  271.8 36.2 %collective-permute-start.32 = (bf16[256,1152]{1,0:T(8,128)(2,1)}, bf16[256,1152]{1,0:T(8,128)(2,1)S(1)}, u32[]{:S(2)}, u32[]{:S(2)}) collective-permute-start(bf16[256,1152]{1,0:T(8,128)(2,1)} %get-tuple-element.298.refs_0_.refs_3_), channel_id=1, source_target_pairs={{0,4},{1,5},{2,6},{3,7},{4,0},{5,1},{6,2},{7,3},{8,12},{9,13},{10,... | collective-permute-start | bytes 1769480 | tf_op jit(solution)/shard_map/ppermute | solution.py:577
  322.5 36.1 %collective-permute-start.40 = (bf16[256,1152]{1,0:T(8,128)(2,1)S(1)}, bf16[256,1152]{1,0:T(8,128)(2,1)S(1)}, u32[]{:S(2)}, u32[]{:S(2)}) collective-permute-start(bf16[256,1152]{1,0:T(8,128)(2,1)S(1)} %copy-done.60), channel_id=1, source_target_pairs={{0,6},{1,7},{2,4},{3,5},{4,2},{5,3},{6,0},{7,1},{8,14},{9,15},{10,... | collective-permute-start | bytes 1769480 | tf_op jit(solution)/shard_map/ppermute | solution.py:577
  324.6 34.0 %collective-permute-start.41 = (bf16[256,1152]{1,0:T(8,128)(2,1)S(1)}, bf16[256,1152]{1,0:T(8,128)(2,1)S(1)}, u32[]{:S(2)}, u32[]{:S(2)}) collective-permute-start(bf16[256,1152]{1,0:T(8,128)(2,1)S(1)} %copy-done.59), channel_id=1, source_target_pairs={{0,2},{1,3},{2,0},{3,1},{4,6},{5,7},{6,4},{7,5},{8,10},{9,11},{10,... | collective-permute-start | bytes 1769480 | tf_op jit(solution)/shard_map/ppermute | solution.py:577
  325.2 33.5 %collective-permute-start.42 = (bf16[256,1152]{1,0:T(8,128)(2,1)S(1)}, bf16[256,1152]{1,0:T(8,128)(2,1)S(1)}, u32[]{:S(2)}, u32[]{:S(2)}) collective-permute-start(bf16[256,1152]{1,0:T(8,128)(2,1)S(1)} %copy-done.58), channel_id=1, source_target_pairs={{0,4},{1,5},{2,6},{3,7},{4,0},{5,1},{6,2},{7,3},{8,12},{9,13},{10,... | collective-permute-start | bytes 1769480 | tf_op jit(solution)/shard_map/ppermute | solution.py:577
  358.7 154.6 %reduce-scatter.6.cloned.1.call-start = ((), (), s32[]{:S(2)}) async-start(), calls=%async_computation.8 | async-start | bytes 2580480 | tf_op jit(solution)/shard_map/reduce_scatter | solution.py:1052
  368.2 37.7 %collective-permute-start.36 = (bf16[256,1152]{1,0:T(8,128)(2,1)}, bf16[256,1152]{1,0:T(8,128)(2,1)S(1)}, u32[]{:S(2)}, u32[]{:S(2)}) collective-permute-start(bf16[256,1152]{1,0:T(8,128)(2,1)} %get-tuple-element.327), channel_id=1, source_target_pairs={{0,6},{1,7},{2,4},{3,5},{4,2},{5,3},{6,0},{7,1},{8,14},{9,15},{10,... | collective-permute-start | bytes 1769480 | tf_op jit(solution)/shard_map/ppermute | solution.py:577
  370.3 35.6 %collective-permute-start.37 = (bf16[256,1152]{1,0:T(8,128)(2,1)}, bf16[256,1152]{1,0:T(8,128)(2,1)S(1)}, u32[]{:S(2)}, u32[]{:S(2)}) collective-permute-start(bf16[256,1152]{1,0:T(8,128)(2,1)} %get-tuple-element.328), channel_id=1, source_target_pairs={{0,2},{1,3},{2,0},{3,1},{4,6},{5,7},{6,4},{7,5},{8,10},{9,11},{10,... | collective-permute-start | bytes 1769480 | tf_op jit(solution)/shard_map/ppermute | solution.py:577
  370.9 35.1 %collective-permute-start.38 = (bf16[256,1152]{1,0:T(8,128)(2,1)}, bf16[256,1152]{1,0:T(8,128)(2,1)}, u32[]{:S(2)}, u32[]{:S(2)}) collective-permute-start(bf16[256,1152]{1,0:T(8,128)(2,1)} %get-tuple-element.329), channel_id=1, source_target_pairs={{0,4},{1,5},{2,6},{3,7},{4,0},{5,1},{6,2},{7,3},{8,12},{9,13},{10,... | collective-permute-start | bytes 1769480 | tf_op jit(solution)/shard_map/ppermute | solution.py:577
  406.0 107.2 %reduce-scatter.8.cloned.1.call-start = ((), (), s32[]{:S(2)}) async-start(), calls=%async_computation.9 | async-start | bytes 2580480 | tf_op jit(solution)/shard_map/reduce_scatter | solution.py:1052
  406.1 43.3 %collective-permute-start.48 = (bf16[1152,896]{1,0:T(8,128)(2,1)S(1)}, bf16[1152,896]{1,0:T(8,128)(2,1)}, u32[]{:S(2)}, u32[]{:S(2)}) collective-permute-start(bf16[1152,896]{1,0:T(8,128)(2,1)S(1)} %copy-done.8), channel_id=1, source_target_pairs={{0,1},{1,0},{2,3},{3,2},{4,5},{5,4},{6,7},{7,6},{8,9},{9,8},{10,11... | collective-permute-start | bytes 6193160 | tf_op jit(solution)/shard_map/ppermute | solution.py:577
  475.6 35.8 %collective-permute-start.51 = (bf16[144,2816]{1,0:T(8,128)(2,1)}, bf16[144,2816]{1,0:T(8,128)(2,1)S(1)}, u32[]{:S(2)}, u32[]{:S(2)}) collective-permute-start(bf16[144,2816]{1,0:T(8,128)(2,1)} %get-tuple-element.410), channel_id=1, source_target_pairs={{0,4},{1,5},{2,6},{3,7},{4,0},{5,1},{6,2},{7,3},{8,12},{9,13},{10,... | collective-permute-start | bytes 2433032 | tf_op jit(solution)/shard_map/ppermute | solution.py:577
  476.0 37.3 %collective-permute-start.52 = (bf16[144,2816]{1,0:T(8,128)(2,1)}, bf16[144,2816]{1,0:T(8,128)(2,1)}, u32[]{:S(2)}, u32[]{:S(2)}) collective-permute-start(bf16[144,2816]{1,0:T(8,128)(2,1)} %get-tuple-element.411), channel_id=1, source_target_pairs={{0,6},{1,7},{2,4},{3,5},{4,2},{5,3},{6,0},{7,1},{8,14},{9,15},{10,... | collective-permute-start | bytes 2433032 | tf_op jit(solution)/shard_map/ppermute | solution.py:577
  516.4 31.8 %all-to-all-start.1 = ((bf16[8,36,1792]{2,1,0:T(8,128)(2,1)}), bf16[8,36,1792]{2,1,0:T(8,128)(2,1)S(1)}, u32[]{:S(2)}, u32[]{:S(2)}) async-start(bf16[8,36,1792]{2,1,0:T(8,128)(2,1)} %constant_dynamic-update-slice_fusion.4), calls=%async_computation.3 | async-start | bytes 2293760 | tf_op jit(solution)/shard_map/all_to_all | solution.py:1089
  (100 other events, 1009.9 us)
Sparse Core Ops, SparseCore 0:
  12.9 33.2 all-gather.3
  48.4 78.7 all-gather.7
  128.8 42.4 all-gather.5
  358.8 40.2 reduce-scatter.9
  406.2 43.6 reduce-scatter.5
  459.1 42.4 reduce-scatter.7

commit v5 on v4

--- a/solution.py
+++ b/solution.py
@@ -510,16 +510,18 @@
 
 def terms_kernel(count, kinds, has_got, *refs):
     lefts, rights, refs = refs[:count], refs[count : count + count * kinds], refs[count + count * kinds :]
-    gots, outs = refs[: kinds if has_got else 0], refs[-kinds:]
+    out = refs[-1]
+    wide = out.shape[1] // kinds
     for kind in range(kinds):
         total = None
         for left, right in zip(lefts, rights[kind * count :]):
             term = dot(left[...], right[...], TN)
             total = term if total is None else total + term
-        total = total[: outs[kind].shape[0]]
+        total = total[: out.shape[0]]
+        at = slice(kind * wide, (kind + 1) * wide)
         if has_got:
-            total = total + gots[kind][...].astype(F32)
-        outs[kind][...] = total.astype(BF)
+            total = total + refs[0][:, at].astype(F32)
+        out[:, at] = total.astype(BF)
 
 
 def fold_chips_kernel(dp, place, mine, got, line, *sends):
@@ -562,10 +564,12 @@
     parts, outs = refs[:count], refs[count:]
     total = add_up(parts)
     start = 0
-    for out in outs[:-2]:
+    for out in outs[:3]:
         out[...] = total[:, start : start + out.shape[1]]
         start += out.shape[1]
-    outs[-2][...] = jnp.transpose(total[:, start : start + LANES])[:8]
+    rows = jnp.transpose(total[:, start : start + LANES])
+    for kind, out in enumerate(outs[3:9]):
+        out[...] = rows[kind : kind + 1, : out.shape[1]]
     outs[-1][...] = total[: outs[-1].shape[0], start + LANES :]
 
 
@@ -909,7 +913,7 @@
         )
         return joined
 
-    def over_tokens(left, rights, half, gots=(), high_out=None):
+    def over_tokens(left, rights, half, got=None, high_out=None):
         of = lambda s, name: s[name] if name in ("tokens", "d_tokens") else s[name][half]
         lefts = order.behind([of(s, left) for s in states])
         others = [of(s, right) for right in rights for s in states]
@@ -919,24 +923,26 @@
         staying = lambda columns: pl.BlockSpec((count, columns), lambda i: (0, 0), pipeline_mode=pl.Buffered(1))
         if by_rows:
             steps, left_spec, right_spec = high // 384, moving(384), staying(wide)
-            out_spec = pl.BlockSpec((384, wide), lambda i: (i, 0))
+            out_spec = pl.BlockSpec((384, wide * len(rights)), lambda i: (i, 0))
         else:
             steps, left_spec, right_spec = wide // 384, staying(high), moving(384)
             out_spec = pl.BlockSpec((high_out or high, 384), lambda i: (0, i))
-        results = call(
-            functools.partial(terms_kernel, micro, len(rights), bool(gots)),
+        [made_terms] = call(
+            functools.partial(terms_kernel, micro, len(rights), got is not None),
             (steps,),
-            [(a, left_spec) for a in lefts] + [(b, right_spec) for b in others] + [(got, out_spec) for got in gots],
-            [(shape((high_out or high, wide), BF), out_spec)] * len(rights),
+            [(a, left_spec) for a in lefts]
+            + [(b, right_spec) for b in others]
+            + ([] if got is None else [(got, out_spec)]),
+            [(shape((high_out or high, wide * len(rights)), BF), out_spec)],
             name="terms",
         )
-        return order.step(results)
-
-    def other_terms(left, right, high_out=None):
-        return over_tokens(left, [right], 1, (), high_out)[0] if split else None
-
-    def own_terms(left, right, other, high_out=None):
-        return over_tokens(left, [right], 0, [xor_permute(other, 1, seq)] if split else (), high_out)[0]
+        return order.step(made_terms)
+
+    def other_terms(left, rights, high_out=None):
+        return over_tokens(left, rights, 1, None, high_out) if split else None
+
+    def own_terms(left, rights, other, high_out=None):
+        return over_tokens(left, rights, 0, xor_permute(other, 1, seq) if split else None, high_out)
 
     def ffn_back(s, which):
         if not split:
@@ -984,9 +990,9 @@
     if split:
         late["sent"] = order.step(order.behind(late["sent"]))
         late["d_tokens"] = order.step(join(list(late["sent"]) + [late["d_ffn"]]))
-        down_other = other_terms("act", "d_tokens", own_ff)
+        down_other = other_terms("act", ["d_tokens"], own_ff)
     ffn_back(late, "rest")
-    down_terms = own_terms("act", "d_tokens", down_other if split else None, own_ff)
+    down_terms = own_terms("act", ["d_tokens"], down_other if split else None, own_ff)
     for s in states[:-1]:
         s["terms"] = order.step(order.behind(s["terms"]))
     down_grad = lax.psum_scatter(order.behind(down_terms), "dp", scatter_dimension=0, tiled=True)
@@ -1045,20 +1051,15 @@
         )
         return columns
 
-    def to_columns(part):
-        return columns_of(lax.all_to_all(part.reshape(seq, wrows, pad), "seq", 0, 0), 0)
-
     input_grad = None
-    scattered = lambda terms: lax.psum_scatter(terms, "dp", scatter_dimension=0, tiled=True)
-    gate_other = other_terms("tokens", "d_gate")
+    gu_other = other_terms("tokens", ["d_gate", "d_up"])
     for index in range(micro - 1):
         attend_back(index)
-    gate_terms = own_terms("tokens", "d_gate", gate_other)
-    up_other = other_terms("tokens", "d_up")
+    gu_terms = own_terms("tokens", ["d_gate", "d_up"], gu_other)
     for s in states[:-1]:
         s["d_pairs"] = order.step(order.behind(s["d_pairs"]))
     states[-1]["terms"], down_grad = order.step(order.behind((states[-1]["terms"], down_grad)))
-    gate_sum = scattered(order.behind(gate_terms))
+    gu_sum = lax.psum_scatter(order.behind(gu_terms), "dp", scatter_dimension=0, tiled=True)
     attend_back(micro - 1)
     for index in range(micro):
         input_grad = project_back(index, input_grad)
@@ -1081,48 +1082,48 @@
     order.step(other)
     if split:
         got = xor_permute(other, 1, seq)
-        up_sum = scattered(own_terms("tokens", "d_up", up_other))
         in_parts = fold_chips(mine, got, dp, seq, order)
         in_parts = order.step(order.behind(in_parts))
-        both_sums = [part.reshape(seq, wrows, pad) for part in order.behind((gate_sum, up_sum))]
-        both_sums = order.step(jnp.concatenate(both_sums, axis=2))
-        both_sums = lax.all_to_all(both_sums, "seq", 0, 0)
+        gu_sum = order.step(order.behind(gu_sum).reshape(seq, wrows, 2 * pad))
+        gu_sum = lax.all_to_all(gu_sum, "seq", 0, 0)
         in_parts = fold_line(in_parts, dp, order)
-        gate_grad, up_grad = (columns_of(both_sums, index) for index in range(2))
+        gu_sum = order.behind(gu_sum)
+        gate_grad, up_grad = order.step([columns_of(gu_sum, index) for index in range(2)])
     else:
-        up_sum = scattered(own_terms("tokens", "d_up", None))
         halves_of = [part.reshape(devices // 2, wrows, -1) for part in (mine, other)]
         whole_terms = jnp.stack(halves_of, axis=1).reshape(devices, wrows, -1)
         in_parts = [lax.psum_scatter(whole_terms, BOTH, scatter_dimension=0, tiled=True)[0]]
-    q_grad, k_grad, v_grad, gain_sum, out_grad = call(
+    q_grad, k_grad, v_grad, *gain_sum, out_grad = call(
         functools.partial(finish_kernel, len(in_parts)),
         None,
-        [plain(part) for part in in_parts],
-        [(shape((wrows, columns), F32), VMEM) for columns in (qd, HD, HD)] + [(shape((8, wrows), F32), VMEM)]
+        [plain(part) for part in order.behind(list(in_parts))],
+        [(shape((wrows, columns), F32), VMEM) for columns in (qd, HD, HD)]
+        + [(shape((1, size), F32), VMEM) for size in [wrows] * 4 + [short] * 2]
         + [(shape((qd // devices, width), F32), VMEM)],
         name="finish",
     )
 
     if not split:
-        gate_grad, up_grad = to_columns(gate_sum), to_columns(up_sum)
+        gu_sum = lax.all_to_all(gu_sum.reshape(seq, wrows, 2 * pad), "seq", 0, 0)
+        gate_grad, up_grad = (columns_of(gu_sum, index) for index in range(2))
     down_grad = order.behind(down_grad).astype(F32)
 
     return (
         layer_out,
         input_grad,
-        gain_sum[0],
+        gain_sum[0].reshape(wrows),
         q_grad,
         k_grad,
         v_grad,
-        gain_sum[4, :short],
-        gain_sum[5, :short],
+        gain_sum[4].reshape(short),
+        gain_sum[5].reshape(short),
         out_grad,
-        gain_sum[1],
-        gain_sum[2],
+        gain_sum[1].reshape(wrows),
+        gain_sum[2].reshape(wrows),
         gate_grad,
         up_grad,
         down_grad,
-        gain_sum[3],
+        gain_sum[3].reshape(wrows),
     )
 
 

time: 571 us -> 559 us (0.979)
  Pallas kernels: 271 us -> 265 us
    ppermute x3, waiting for transfers between devices: 14.3 us -> 0.15 us  [around(): return lax.ppermute(value, 'dp', [(i, (i + by) % dp) for i in range(dp)])]
    all_to_all x1, waiting for transfers between devices: 0.01 us -> 7.53 us  [shards(): gu_sum = lax.all_to_all(gu_sum, 'seq', 0, 0)]
    pallas_call x32 -> x30, Pallas kernels: 271 us -> 265 us  [call(): pl.pallas_call(body, **{} if grid is None else {'grid': grid}, in_specs=[...]
    ppermute x47 -> x46, starting transfers between devices: 47.7 us -> 45.2 us  [xor_permute(): return lax.ppermute(value, 'seq', [(i, i ^ bit) for i in range(size)])]
    unnamed x127 -> x128, local copies, waits for them, and re-layouts: 19.2 us -> 18.4 us
    ppermute x47 -> x46, waiting for transfers between devices: 96.5 us -> 96.7 us  [xor_permute(): return lax.ppermute(value, 'seq', [(i, i ^ bit) for i in range(size)])]
  transfers between devices with their start and end apart: 63 -> 61, of which waited for: 21 -> 21; matrix products, arithmetic and copies ran while one was open for 2% -> 1% of each run, Pallas kernels for 45% -> 43%
where the time goes in v5:
time: 559 us; the launch traced here: 548 us
  Pallas kernels  265 us (47%)
  waiting for transfers between devices  150 us (27%)
  starting transfers between devices  65.5 us (12%)
  local copies, waits for them, and re-layouts  25.6 us (5%)
  blocking collectives  21.6 us (4%)
  between operations  14.7 us (3%)
    pallas_call x30, Pallas kernels, call(): pl.pallas_call(body, **{} if grid is None else {'grid': grid}, in_specs=[...  265 us
    ppermute x46, waiting for transfers between devices, xor_permute(): return lax.ppermute(value, 'seq', [(i, i ^ bit) for i in range(size)])  96.7 us
    ppermute x46, starting transfers between devices, xor_permute(): return lax.ppermute(value, 'seq', [(i, i ^ bit) for i in range(size)])  45.2 us
    all_gather x1, waiting for transfers between devices, shards(): w_down = lax.all_gather(downproj, 'dp', axis=0, tiled=True)  23.7 us
    all_to_all x1, blocking collectives, shards(): gate_up = lax.all_to_all(gate_up, 'seq', 0, 0).reshape(seq * wrows, 2 * pad)  21.6 us
    unnamed x128, local copies, waits for them, and re-layouts  18.4 us
    ppermute x6, waiting for transfers between devices, from_behind(): return lax.ppermute(value, 'seq', pairs)  13.5 us
    ppermute x6, starting transfers between devices, from_behind(): return lax.ppermute(value, 'seq', pairs)  11.3 us
  transfers between devices with their start and end apart: 61, of which 21 were waited for; matrix products, arithmetic and copies ran while one was open for 1% of the time, Pallas kernels for 43%

profile of v5, /device:TPU:0, one launch (start us, length us, event | category | flops | bytes accessed | tf_op | source)
XLA Modules:
  0.0 548.1 jit_solution(6394120159089017136)
XLA Ops:
  15.6 21.6 %all_to_all.10 = bf16[8,36,1792]{2,1,0:T(8,128)(2,1)S(1)} all-to-all(bf16[8,36,1792]{2,1,0:T(8,128)(2,1)} %owner.1), channel_id=1, replica_groups=mesh['dp'=4,'seq'=8] {'seq'}, dimensions={0} | all-to-all | bytes 2064384 | tf_op jit(solution)/shard_map/all_to_all | solution.py:715
  51.9 10.6 %collective-permute-done.refs_1_ = bf16[144,1664]{1,0:T(8,128)(2,1)S(1)} collective-permute-done((bf16[144,1664]{1,0:T(8,128)(2,1)}, bf16[144,1664]{1,0:T(8,128)(2,1)S(1)}, u32[]{:S(2)}, u32[]{:S(2)}) %collective-permute-start) | collective-permute-done | bytes 479264 | tf_op jit(solution)/shard_map/ppermute | solution.py:581
  62.5 9.7 %collective-permute-done.1.refs_2_ = bf16[144,1664]{1,0:T(8,128)(2,1)S(1)} collective-permute-done((bf16[144,1664]{1,0:T(8,128)(2,1)}, bf16[144,1664]{1,0:T(8,128)(2,1)S(1)}, u32[]{:S(2)}, u32[]{:S(2)}) %collective-permute-start.1) | collective-permute-done | bytes 479264 | tf_op jit(solution)/shard_map/ppermute | solution.py:581
  83.0 7.0 %project.1 = (bf16[2,256,1152]{2,1,0:T(8,128)(2,1)}, f32[2,256,1280]{2,1,0:T(8,128)}, bf16[2,256,1024]{2,1,0:T(8,128)(2,1)}, bf16[2,256,512]{2,1,0:T(8,128)(2,1)}, f32[8,1152]{1,0:T(8,128)}) custom-call(bf16[2,1,256,1152]{3,2,1,0:T(8,128)(2,1)} %refs_8_.3, bf16[1152,1664]{1,0:T(8,128)(2,1)} %untangle_in.1.w_ref.packed_ref.refs_7_, ...), custom_call_target="tpu_custom_call" | custom-call | bytes 1 | tf_op jit(solution)/shard_map/project/pallas_call | solution.py:43
  109.6 6.1 %attend.2 = (bf16[256,1024]{1,0:T(8,128)(2,1)}, f32[256,1152]{1,0:T(8,128)}, f32[256,1152]{1,0:T(8,128)}, bf16[256,1152]{1,0:T(8,128)(2,1)}) custom-call(s32[2]{0:T(128)} %pad_add_fusion.1.place, bf16[2,1,256,1152]{3,2,1,0:T(8,128)(2,1)} %refs_8_.3, bf16[2,256,1024]{2,1,0:T(8,128)(2,1)} %get-tuple-element.260.q_ref.refs_7_, ...), custom_call_target="tpu_custom_call" | custom-call | bytes 1 | tf_op jit(solution)/shard_map/attend/pallas_call | solution.py:43
  131.3 14.0 %collective-permute-done.20.refs_1_ = bf16[256,1152]{1,0:T(8,128)(2,1)S(1)} collective-permute-done((bf16[256,1152]{1,0:T(8,128)(2,1)}, bf16[256,1152]{1,0:T(8,128)(2,1)S(1)}, u32[]{:S(2)}, u32[]{:S(2)}) %collective-permute-start.20) | collective-permute-done | bytes 589856 | tf_op jit(solution)/shard_map/ppermute | solution.py:581
  147.6 23.7 %all-gather.6.cloned.1.call-done.refs_6_.refs_7_.refs_9_ = bf16[864,1152]{1,0:T(8,128)(2,1)} async-done(((bf16[216,1152]{1,0:T(8,128)(2,1)}), bf16[864,1152]{1,0:T(8,128)(2,1)}) %all-gather.6.cloned.1.call-update) | async-done | bytes 1990672 | tf_op jit(solution)/shard_map/all_gather | solution.py:720
  176.9 23.5 %ffn.2 = (bf16[1024,1152]{1,0:T(8,128)(2,1)}, bf16[1024,896]{1,0:T(8,128)(2,1)}, bf16[1024,896]{1,0:T(8,128)(2,1)}, bf16[1024,896]{1,0:T(8,128)(2,1)}, bf16[1024...) custom-call(bf16[256,1152]{1,0:T(8,128)(2,1)} %copy-done.17, ...), custom_call_target="tpu_custom_call" | custom-call | bytes 1 | tf_op jit(solution)/shard_map/ffn/pallas_call | solution.py:43
  205.6 23.3 %ffn.3 = (bf16[1024,1152]{1,0:T(8,128)(2,1)}, bf16[1024,896]{1,0:T(8,128)(2,1)}, bf16[1024,896]{1,0:T(8,128)(2,1)}, bf16[1024,896]{1,0:T(8,128)(2,1)}, bf16[1024...) custom-call(bf16[256,1152]{1,0:T(8,128)(2,1)} %copy-done.21, ...), custom_call_target="tpu_custom_call" | custom-call | bytes 1 | tf_op jit(solution)/shard_map/ffn/pallas_call | solution.py:43
  240.5 10.2 %ffn_back.4 = (bf16[1024,1152]{1,0:T(8,128)(2,1)}, bf16[1024,896]{1,0:T(8,128)(2,1)}, bf16[1024,896]{1,0:T(8,128)(2,1)}, bf16[1024,896]{1,0:T(8,128)(2,1)}, bf16...) custom-call(bf16[256,1152]{1,0:T(8,128)(2,1)} %get-tuple-element.293.refs_0_, ...), custom_call_target="tpu_custom_call" | custom-call | bytes 1 | tf_op jit(solution)/shard_map/ffn_back/pallas_call | solution.py:43
  251.3 7.7 %collective-permute-done.25.refs_2_ = bf16[256,1152]{1,0:T(8,128)(2,1)S(1)} collective-permute-done((bf16[256,1152]{1,0:T(8,128)(2,1)}, bf16[256,1152]{1,0:T(8,128)(2,1)S(1)}, u32[]{:S(2)}, u32[]{:S(2)}) %collective-permute-start.25) | collective-permute-done | bytes 589856 | tf_op jit(solution)/shard_map/ppermute | solution.py:581
  273.2 10.1 %ffn_back.5 = (bf16[1024,1152]{1,0:T(8,128)(2,1)}, bf16[1024,896]{1,0:T(8,128)(2,1)}, bf16[1024,896]{1,0:T(8,128)(2,1)}, bf16[1024,896]{1,0:T(8,128)(2,1)}, bf16...) custom-call(bf16[256,1152]{1,0:T(8,128)(2,1)} %get-tuple-element.303.refs_0_.refs_3_, ...), custom_call_target="tpu_custom_call" | custom-call | bytes 1 | tf_op jit(solution)/shard_map/ffn_back/pallas_call | solution.py:43
  285.5 21.1 %ffn_back.6 = (bf16[1024,1152]{1,0:T(8,128)(2,1)}, bf16[1024,896]{1,0:T(8,128)(2,1)}, bf16[1024,896]{1,0:T(8,128)(2,1)}, bf16[1024,896]{1,0:T(8,128)(2,1)}, bf16...) custom-call(bf16[256,1152]{1,0:T(8,128)(2,1)} %copy-done.30, ...), custom_call_target="tpu_custom_call", output_to_operand_aliasing={{0}: (11, {}), {1}: (12, {}), {2}: (13, {}), {3}: (14, {}),... | custom-call | bytes 1 | tf_op jit(solution)/shard_map/ffn_back/pallas_call | solution.py:43
  312.2 10.0 %terms.4 = bf16[864,1152]{1,0:T(8,128)(2,1)} custom-call(bf16[1024,896]{1,0:T(8,128)(2,1)} %get-tuple-element.323.refs_0_, bf16[1024,896]{1,0:T(8,128)(2,1)} %get-tuple-element.324.refs_1_, bf16[1024,1152]{1,0:T(8,128)(2,1)} %get-tuple-element.325.refs_2_, bf16[1024,1152]{1,0:T(8,128)(2,1)} %join.1.refs_3_), custom_call_target="tpu_custom_call" | custom-call | bytes 1 | tf_op jit(solution)/shard_map/terms/pallas_call | solution.py:43
  325.9 20.7 %ffn_back.7 = (bf16[1024,1152]{1,0:T(8,128)(2,1)}, bf16[1024,896]{1,0:T(8,128)(2,1)}, bf16[1024,896]{1,0:T(8,128)(2,1)}, bf16[1024,896]{1,0:T(8,128)(2,1)}, bf16...) custom-call(bf16[256,1152]{1,0:T(8,128)(2,1)} %copy-done.5, ...), custom_call_target="tpu_custom_call", output_to_operand_aliasing={{0}: (11, {}), {1}: (12, {}), {2}: (13, {}), {3}: (14, {}),... | custom-call | bytes 1 | tf_op jit(solution)/shard_map/ffn_back/pallas_call | solution.py:43
  347.9 10.5 %terms.5 = bf16[864,1152]{1,0:T(8,128)(2,1)} custom-call(bf16[1024,896]{1,0:T(8,128)(2,1)} %get-tuple-element.337.refs_0_, bf16[1024,896]{1,0:T(8,128)(2,1)} %get-tuple-element.338.refs_1_, bf16[1024,1152]{1,0:T(8,128)(2,1)} %get-tuple-element.325.refs_2_, bf16[1024,1152]{1,0:T(8,128)(2,1)} %join.1.refs_3_, bf16[864,1152]{1,0:T(8,128)(2,1)} %copy-done.8), custom_call_target="tpu_custom_call" | custom-call | bytes 1 | tf_op jit(solution)/shard_map/terms/pallas_call | solution.py:43
  358.5 15.7 %terms.6 = bf16[1152,1792]{1,0:T(8,128)(2,1)} custom-call(bf16[1024,1152]{1,0:T(8,128)(2,1)} %get-tuple-element.359.refs_0_, bf16[1024,1152]{1,0:T(8,128)(2,1)} %get-tuple-element.360.refs_1_, bf16[1024,896]{1,0:T(8,128)(2,1)} %get-tuple-element.348.refs_2_, bf16[1024,896]{1,0:T(8,128)(2,1)} %get-tuple-element.349.refs_3_, ...), custom_call_target="tpu_custom_call" | custom-call | bytes 1 | tf_op jit(solution)/shard_map/terms/pallas_call | solution.py:43
  377.9 11.6 %attend_back.2 = (f32[256,1152]{1,0:T(8,128)}, bf16[256,1152]{1,0:T(8,128)(2,1)}, bf16[256,1024]{1,0:T(8,128)(2,1)}, f32[1,1152]{1,0:T(1,128)}, f32[1,1152]{1,0:...) custom-call(s32[2]{0:T(128)} %pad_add_fusion.1.place, ...), custom_call_target="tpu_custom_call" | custom-call | bytes 1 | tf_op jit(solution)/shard_map/attend_back/pallas_call | solution.py:43
  392.1 16.3 %terms.7 = bf16[1152,1792]{1,0:T(8,128)(2,1)} custom-call(bf16[1024,1152]{1,0:T(8,128)(2,1)} %get-tuple-element.359.refs_0_, bf16[1024,1152]{1,0:T(8,128)(2,1)} %get-tuple-element.360.refs_1_, bf16[1024,896]{1,0:T(8,128)(2,1)} %get-tuple-element.361.refs_2_, bf16[1024,896]{1,0:T(8,128)(2,1)} %get-tuple-element.362.refs_3_, ...), custom_call_target="tpu_custom_call" | custom-call | bytes 1 | tf_op jit(solution)/shard_map/terms/pallas_call | solution.py:43
  415.0 11.1 %attend_back.3 = (f32[256,1152]{1,0:T(8,128)}, bf16[256,1152]{1,0:T(8,128)(2,1)}, bf16[256,1024]{1,0:T(8,128)(2,1)}, f32[1,1152]{1,0:T(1,128)}, f32[1,1152]{1,0:...) custom-call(s32[2]{0:T(128)} %pad_add_fusion.place, ...), custom_call_target="tpu_custom_call" | custom-call | bytes 1 | tf_op jit(solution)/shard_map/attend_back/pallas_call | solution.py:43
  446.1 9.7 %weights.1 = (bf16[576,2816]{1,0:T(8,128)(2,1)}, bf16[576,2816]{1,0:T(8,128)(2,1)}) custom-call(s32[1]{0:T(128)} %bitcast.14.core, bf16[256,1024]{1,0:T(8,128)(2,1)} %get-tuple-element.391.refs_0_, bf16[256,1024]{1,0:T(8,128)(2,1)} %get-tuple-element.392.refs_1_, bf16[256,1152]{1,0:T(8,128)(2,1)} %get-tuple-element.358.refs_2_, ...), custom_call_target="tpu_custom_call" | custom-call | bytes 1 | tf_op jit(solution)/shard_map/weights/pallas_call | solution.py:43
  473.3 17.6 %collective-permute-done.49.refs_1_ = bf16[144,2816]{1,0:T(8,128)(2,1)S(1)} collective-permute-done((bf16[144,2816]{1,0:T(8,128)(2,1)}, bf16[144,2816]{1,0:T(8,128)(2,1)S(1)}, u32[]{:S(2)}, u32[]{:S(2)}) %collective-permute-start.49) | collective-permute-done | bytes 811040 | tf_op jit(solution)/shard_map/ppermute | solution.py:581
  490.9 18.4 %collective-permute-done.50.refs_2_ = bf16[144,2816]{1,0:T(8,128)(2,1)S(1)} collective-permute-done((bf16[144,2816]{1,0:T(8,128)(2,1)}, bf16[144,2816]{1,0:T(8,128)(2,1)S(1)}, u32[]{:S(2)}, u32[]{:S(2)}) %collective-permute-start.50) | collective-permute-done | bytes 811040 | tf_op jit(solution)/shard_map/ppermute | solution.py:581
  524.1 7.5 %all-to-all-done.1.in_ref = bf16[8,36,1792]{2,1,0:T(8,128)(2,1)S(1)} async-done(((bf16[8,36,1792]{2,1,0:T(8,128)(2,1)}), bf16[8,36,1792]{2,1,0:T(8,128)(2,1)S(1)}, u32[]{:S(2)}, u32[]{:S(2)}) %all-to-all-start.1) | async-done | bytes 1032224 | tf_op jit(solution)/shard_map/all_to_all | solution.py:1088
  (278 shorter events, 195.7 us)
Async XLA Ops:
  7.2 39.0 %all-gather.4.cloned.1.call-start = ((), (), s32[]{:S(2)}) async-start(), calls=%async_computation.4 | async-start | bytes 1484800 | tf_op jit(solution)/shard_map/all_gather | solution.py:706
  12.8 133.4 %all-gather.8.cloned.1.call-start = ((), (), s32[]{:S(2)}) async-start(), calls=%async_computation.6 | async-start | bytes 5160960 | tf_op jit(solution)/shard_map/all_gather | solution.py:716
  38.3 133.0 %all-gather.6.cloned.1.call-start = ((), (), s32[]{:S(2)}) async-start(), calls=%async_computation.5 | async-start | bytes 2488320 | tf_op jit(solution)/shard_map/all_gather | solution.py:720
  97.3 317.7 %reduce-scatter.7.cloned.1.call-start = ((), (), s32[]{:S(2)}) async-start(), calls=%async_computation.8 | async-start | bytes 2488320
  171.3 32.1 %collective-permute-start.16 = (bf16[256,1152]{1,0:T(8,128)(2,1)}, bf16[256,1152]{1,0:T(8,128)(2,1)S(1)}, u32[]{:S(2)}, u32[]{:S(2)}) collective-permute-start(bf16[256,1152]{1,0:T(8,128)(2,1)} %get-tuple-element.284.refs_3_), channel_id=1, source_target_pairs={{0,6},{1,7},{2,4},{3,5},{4,2},{5,3},{6,0},{7,1},{8,14},{9,15},{10,... | collective-permute-start | bytes 1769480 | tf_op jit(solution)/shard_map/ppermute | solution.py:581
  173.7 30.3 %collective-permute-start.17 = (bf16[256,1152]{1,0:T(8,128)(2,1)}, bf16[256,1152]{1,0:T(8,128)(2,1)S(1)}, u32[]{:S(2)}, u32[]{:S(2)}) collective-permute-start(bf16[256,1152]{1,0:T(8,128)(2,1)} %get-tuple-element.284.refs_3_), channel_id=1, source_target_pairs={{0,2},{1,3},{2,0},{3,1},{4,6},{5,7},{6,4},{7,5},{8,10},{9,11},{10,... | collective-permute-start | bytes 1769480 | tf_op jit(solution)/shard_map/ppermute | solution.py:581
  174.2 29.7 %collective-permute-start.18 = (bf16[256,1152]{1,0:T(8,128)(2,1)}, bf16[256,1152]{1,0:T(8,128)(2,1)S(1)}, u32[]{:S(2)}, u32[]{:S(2)}) collective-permute-start(bf16[256,1152]{1,0:T(8,128)(2,1)} %get-tuple-element.284.refs_3_), channel_id=1, source_target_pairs={{0,4},{1,5},{2,6},{3,7},{4,0},{5,1},{6,2},{7,3},{8,12},{9,13},{10,... | collective-permute-start | bytes 1769480 | tf_op jit(solution)/shard_map/ppermute | solution.py:581
  200.4 31.5 %collective-permute-start.27 = (bf16[256,1152]{1,0:T(8,128)(2,1)}, bf16[256,1152]{1,0:T(8,128)(2,1)S(1)}, u32[]{:S(2)}, u32[]{:S(2)}) collective-permute-start(bf16[256,1152]{1,0:T(8,128)(2,1)} %get-tuple-element.276), channel_id=1, source_target_pairs={{0,6},{1,7},{2,4},{3,5},{4,2},{5,3},{6,0},{7,1},{8,14},{9,15},{10,... | collective-permute-start | bytes 1769480 | tf_op jit(solution)/shard_map/ppermute | solution.py:581
  202.8 29.6 %collective-permute-start.28 = (bf16[256,1152]{1,0:T(8,128)(2,1)}, bf16[256,1152]{1,0:T(8,128)(2,1)S(1)}, u32[]{:S(2)}, u32[]{:S(2)}) collective-permute-start(bf16[256,1152]{1,0:T(8,128)(2,1)} %get-tuple-element.277), channel_id=1, source_target_pairs={{0,2},{1,3},{2,0},{3,1},{4,6},{5,7},{6,4},{7,5},{8,10},{9,11},{10,... | collective-permute-start | bytes 1769480 | tf_op jit(solution)/shard_map/ppermute | solution.py:581
  237.6 34.1 %collective-permute-start.33 = (bf16[256,1152]{1,0:T(8,128)(2,1)}, bf16[256,1152]{1,0:T(8,128)(2,1)S(1)}, u32[]{:S(2)}, u32[]{:S(2)}) collective-permute-start(bf16[256,1152]{1,0:T(8,128)(2,1)} %get-tuple-element.293.refs_0_), channel_id=1, source_target_pairs={{0,6},{1,7},{2,4},{3,5},{4,2},{5,3},{6,0},{7,1},{8,14},{9,15},{10,... | collective-permute-start | bytes 1769480 | tf_op jit(solution)/shard_map/ppermute | solution.py:581
  240.0 44.4 %collective-permute-start.34 = (bf16[256,1152]{1,0:T(8,128)(2,1)}, bf16[256,1152]{1,0:T(8,128)(2,1)S(1)}, u32[]{:S(2)}, u32[]{:S(2)}) collective-permute-start(bf16[256,1152]{1,0:T(8,128)(2,1)} %get-tuple-element.293.refs_0_), channel_id=1, source_target_pairs={{0,2},{1,3},{2,0},{3,1},{4,6},{5,7},{6,4},{7,5},{8,10},{9,11},{10,... | collective-permute-start | bytes 1769480 | tf_op jit(solution)/shard_map/ppermute | solution.py:581
  250.7 33.7 %collective-permute-start.35 = (bf16[256,1152]{1,0:T(8,128)(2,1)S(1)}, bf16[256,1152]{1,0:T(8,128)(2,1)S(1)}, u32[]{:S(2)}, u32[]{:S(2)}) collective-permute-start(bf16[256,1152]{1,0:T(8,128)(2,1)S(1)} %copy-done.18), channel_id=1, source_target_pairs={{0,4},{1,5},{2,6},{3,7},{4,0},{5,1},{6,2},{7,3},{8,12},{9,13},{10,... | collective-permute-start | bytes 1769480 | tf_op jit(solution)/shard_map/ppermute | solution.py:581
  264.1 42.4 %collective-permute-start.30 = (bf16[256,1152]{1,0:T(8,128)(2,1)}, bf16[256,1152]{1,0:T(8,128)(2,1)S(1)}, u32[]{:S(2)}, u32[]{:S(2)}) collective-permute-start(bf16[256,1152]{1,0:T(8,128)(2,1)} %get-tuple-element.303.refs_0_.refs_3_), channel_id=1, source_target_pairs={{0,6},{1,7},{2,4},{3,5},{4,2},{5,3},{6,0},{7,1},{8,14},{9,15},{10,... | collective-permute-start | bytes 1769480 | tf_op jit(solution)/shard_map/ppermute | solution.py:581
  266.4 41.6 %collective-permute-start.31 = (bf16[256,1152]{1,0:T(8,128)(2,1)}, bf16[256,1152]{1,0:T(8,128)(2,1)S(1)}, u32[]{:S(2)}, u32[]{:S(2)}) collective-permute-start(bf16[256,1152]{1,0:T(8,128)(2,1)} %get-tuple-element.303.refs_0_.refs_3_), channel_id=1, source_target_pairs={{0,2},{1,3},{2,0},{3,1},{4,6},{5,7},{6,4},{7,5},{8,10},{9,11},{10,... | collective-permute-start | bytes 1769480 | tf_op jit(solution)/shard_map/ppermute | solution.py:581
  271.7 36.2 %collective-permute-start.32 = (bf16[256,1152]{1,0:T(8,128)(2,1)}, bf16[256,1152]{1,0:T(8,128)(2,1)S(1)}, u32[]{:S(2)}, u32[]{:S(2)}) collective-permute-start(bf16[256,1152]{1,0:T(8,128)(2,1)} %get-tuple-element.303.refs_0_.refs_3_), channel_id=1, source_target_pairs={{0,4},{1,5},{2,6},{3,7},{4,0},{5,1},{6,2},{7,3},{8,12},{9,13},{10,... | collective-permute-start | bytes 1769480 | tf_op jit(solution)/shard_map/ppermute | solution.py:581
  322.3 36.1 %collective-permute-start.40 = (bf16[256,1152]{1,0:T(8,128)(2,1)S(1)}, bf16[256,1152]{1,0:T(8,128)(2,1)S(1)}, u32[]{:S(2)}, u32[]{:S(2)}) collective-permute-start(bf16[256,1152]{1,0:T(8,128)(2,1)S(1)} %copy-done.61), channel_id=1, source_target_pairs={{0,6},{1,7},{2,4},{3,5},{4,2},{5,3},{6,0},{7,1},{8,14},{9,15},{10,... | collective-permute-start | bytes 1769480 | tf_op jit(solution)/shard_map/ppermute | solution.py:581
  324.5 33.9 %collective-permute-start.41 = (bf16[256,1152]{1,0:T(8,128)(2,1)S(1)}, bf16[256,1152]{1,0:T(8,128)(2,1)S(1)}, u32[]{:S(2)}, u32[]{:S(2)}) collective-permute-start(bf16[256,1152]{1,0:T(8,128)(2,1)S(1)} %copy-done.60), channel_id=1, source_target_pairs={{0,2},{1,3},{2,0},{3,1},{4,6},{5,7},{6,4},{7,5},{8,10},{9,11},{10,... | collective-permute-start | bytes 1769480 | tf_op jit(solution)/shard_map/ppermute | solution.py:581
  325.0 33.4 %collective-permute-start.42 = (bf16[256,1152]{1,0:T(8,128)(2,1)S(1)}, bf16[256,1152]{1,0:T(8,128)(2,1)S(1)}, u32[]{:S(2)}, u32[]{:S(2)}) collective-permute-start(bf16[256,1152]{1,0:T(8,128)(2,1)S(1)} %copy-done.59), channel_id=1, source_target_pairs={{0,4},{1,5},{2,6},{3,7},{4,0},{5,1},{6,2},{7,3},{8,12},{9,13},{10,... | collective-permute-start | bytes 1769480 | tf_op jit(solution)/shard_map/ppermute | solution.py:581
  374.3 134.9 %reduce-scatter.5.cloned.1.call-start = ((), (), s32[]{:S(2)}) async-start(), calls=%async_computation.7 | async-start | bytes 5160960 | tf_op jit(solution)/shard_map/reduce_scatter | solution.py:1062
  374.4 37.7 %collective-permute-start.36 = (bf16[256,1152]{1,0:T(8,128)(2,1)}, bf16[256,1152]{1,0:T(8,128)(2,1)S(1)}, u32[]{:S(2)}, u32[]{:S(2)}) collective-permute-start(bf16[256,1152]{1,0:T(8,128)(2,1)} %get-tuple-element.332), channel_id=1, source_target_pairs={{0,6},{1,7},{2,4},{3,5},{4,2},{5,3},{6,0},{7,1},{8,14},{9,15},{10,... | collective-permute-start | bytes 1769480 | tf_op jit(solution)/shard_map/ppermute | solution.py:581
  376.5 35.6 %collective-permute-start.37 = (bf16[256,1152]{1,0:T(8,128)(2,1)S(1)}, bf16[256,1152]{1,0:T(8,128)(2,1)S(1)}, u32[]{:S(2)}, u32[]{:S(2)}) collective-permute-start(bf16[256,1152]{1,0:T(8,128)(2,1)S(1)} %copy-done.58), channel_id=1, source_target_pairs={{0,2},{1,3},{2,0},{3,1},{4,6},{5,7},{6,4},{7,5},{8,10},{9,11},{10,... | collective-permute-start | bytes 1769480 | tf_op jit(solution)/shard_map/ppermute | solution.py:581
  377.0 35.0 %collective-permute-start.38 = (bf16[256,1152]{1,0:T(8,128)(2,1)S(1)}, bf16[256,1152]{1,0:T(8,128)(2,1)S(1)}, u32[]{:S(2)}, u32[]{:S(2)}) collective-permute-start(bf16[256,1152]{1,0:T(8,128)(2,1)S(1)} %copy-done.57), channel_id=1, source_target_pairs={{0,4},{1,5},{2,6},{3,7},{4,0},{5,1},{6,2},{7,3},{8,12},{9,13},{10,... | collective-permute-start | bytes 1769480 | tf_op jit(solution)/shard_map/ppermute | solution.py:581
  471.8 37.4 %collective-permute-start.50 = (bf16[144,2816]{1,0:T(8,128)(2,1)}, bf16[144,2816]{1,0:T(8,128)(2,1)S(1)}, u32[]{:S(2)}, u32[]{:S(2)}) collective-permute-start(bf16[144,2816]{1,0:T(8,128)(2,1)} %get-tuple-element.411), channel_id=1, source_target_pairs={{0,4},{1,5},{2,6},{3,7},{4,0},{5,1},{6,2},{7,3},{8,12},{9,13},{10,... | collective-permute-start | bytes 2433032 | tf_op jit(solution)/shard_map/ppermute | solution.py:581
  471.8 37.4 %collective-permute-start.51 = (bf16[144,2816]{1,0:T(8,128)(2,1)}, bf16[144,2816]{1,0:T(8,128)(2,1)}, u32[]{:S(2)}, u32[]{:S(2)}) collective-permute-start(bf16[144,2816]{1,0:T(8,128)(2,1)} %get-tuple-element.412), channel_id=1, source_target_pairs={{0,6},{1,7},{2,4},{3,5},{4,2},{5,3},{6,0},{7,1},{8,14},{9,15},{10,... | collective-permute-start | bytes 2433032 | tf_op jit(solution)/shard_map/ppermute | solution.py:581
  (99 other events, 958.3 us)
Sparse Core Ops, SparseCore 0:
  12.9 33.2 all-gather.3
  48.4 78.7 all-gather.7
  128.8 42.4 all-gather.5
  374.4 40.4 reduce-scatter.6
  417.1 75.4 reduce-scatter.4

commit v6 on v5

--- a/solution.py
+++ b/solution.py
@@ -1058,9 +1058,10 @@
     gu_terms = own_terms("tokens", ["d_gate", "d_up"], gu_other)
     for s in states[:-1]:
         s["d_pairs"] = order.step(order.behind(s["d_pairs"]))
-    states[-1]["terms"], down_grad = order.step(order.behind((states[-1]["terms"], down_grad)))
+    states[-1]["terms"] = order.step(order.behind(states[-1]["terms"]))
+    attend_back(micro - 1)
+    down_grad = order.step(order.behind(down_grad))
     gu_sum = lax.psum_scatter(order.behind(gu_terms), "dp", scatter_dimension=0, tiled=True)
-    attend_back(micro - 1)
     for index in range(micro):
         input_grad = project_back(index, input_grad)
     core = lax.axis_index("seq") & 1
@@ -1082,10 +1083,11 @@
     order.step(other)
     if split:
         got = xor_permute(other, 1, seq)
+        down_grad = order.step(order.behind(down_grad).astype(F32))
         in_parts = fold_chips(mine, got, dp, seq, order)
+        gu_sum = order.step(order.behind(gu_sum).reshape(seq, wrows, 2 * pad))
         in_parts = order.step(order.behind(in_parts))
-        gu_sum = order.step(order.behind(gu_sum).reshape(seq, wrows, 2 * pad))
-        gu_sum = lax.all_to_all(gu_sum, "seq", 0, 0)
+        gu_sum = lax.all_to_all(order.behind(gu_sum), "seq", 0, 0)
         in_parts = fold_line(in_parts, dp, order)
         gu_sum = order.behind(gu_sum)
         gate_grad, up_grad = order.step([columns_of(gu_sum, index) for index in range(2)])
@@ -1106,7 +1108,7 @@
     if not split:
         gu_sum = lax.all_to_all(gu_sum.reshape(seq, wrows, 2 * pad), "seq", 0, 0)
         gate_grad, up_grad = (columns_of(gu_sum, index) for index in range(2))
-    down_grad = order.behind(down_grad).astype(F32)
+        down_grad = down_grad.astype(F32)
 
     return (
         layer_out,

time: 559 us -> 555 us (level)
  waiting for transfers between devices: 150 us -> 144 us
    ppermute x46, waiting for transfers between devices: 96.7 us -> 65.9 us  [xor_permute(): return lax.ppermute(value, 'seq', [(i, i ^ bit) for i in range(size)])]
    reduce_scatter x1, waiting for transfers between devices: 0.01 us -> 26 us  [shards(): lax.psum_scatter(order.behind(gu_terms), 'dp', scatter_dimension=0, tiled...]
    unnamed x128 -> x132, local copies, waits for them, and re-layouts: 18.4 us -> 21.5 us
  transfers between devices with their start and end apart: 61 -> 61, of which waited for: 21 -> 21; matrix products, arithmetic and copies ran while one was open for 1% -> 2% of each run, Pallas kernels for 43% -> 43%
where the time goes in v6:
time: 555 us; the launch traced here: 545 us
  Pallas kernels  266 us (48%)
  waiting for transfers between devices  144 us (26%)
  starting transfers between devices  64.3 us (12%)
  local copies, waits for them, and re-layouts  28.4 us (5%)
  blocking collectives  21.6 us (4%)
  between operations  14.7 us (3%)
  other arithmetic  6.53 us (1%)
    pallas_call x30, Pallas kernels, call(): pl.pallas_call(body, **{} if grid is None else {'grid': grid}, in_specs=[...  266 us
    ppermute x46, waiting for transfers between devices, xor_permute(): return lax.ppermute(value, 'seq', [(i, i ^ bit) for i in range(size)])  65.9 us
    ppermute x46, starting transfers between devices, xor_permute(): return lax.ppermute(value, 'seq', [(i, i ^ bit) for i in range(size)])  45 us
    reduce_scatter x1, waiting for transfers between devices, shards(): lax.psum_scatter(order.behind(gu_terms), 'dp', scatter_dimension=0, tiled...  26 us
    all_gather x1, waiting for transfers between devices, shards(): w_down = lax.all_gather(downproj, 'dp', axis=0, tiled=True)  23.7 us
    all_to_all x1, blocking collectives, shards(): gate_up = lax.all_to_all(gate_up, 'seq', 0, 0).reshape(seq * wrows, 2 * pad)  21.6 us
    unnamed x132, local copies, waits for them, and re-layouts  21.5 us
    ppermute x6, waiting for transfers between devices, from_behind(): return lax.ppermute(value, 'seq', pairs)  13 us
  transfers between devices with their start and end apart: 61, of which 21 were waited for; matrix products, arithmetic and copies ran while one was open for 2% of the time, Pallas kernels for 43%

profile of v6, /device:TPU:0, one launch (start us, length us, event | category | flops | bytes accessed | tf_op | source)
XLA Modules:
  0.0 545.3 jit_solution(15992702818910365792)
XLA Ops:
  15.6 21.6 %all_to_all.10 = bf16[8,36,1792]{2,1,0:T(8,128)(2,1)S(1)} all-to-all(bf16[8,36,1792]{2,1,0:T(8,128)(2,1)} %owner.1), channel_id=1, replica_groups=mesh['dp'=4,'seq'=8] {'seq'}, dimensions={0} | all-to-all | bytes 2064384 | tf_op jit(solution)/shard_map/all_to_all | solution.py:715
  51.9 10.6 %collective-permute-done.refs_1_ = bf16[144,1664]{1,0:T(8,128)(2,1)S(1)} collective-permute-done((bf16[144,1664]{1,0:T(8,128)(2,1)}, bf16[144,1664]{1,0:T(8,128)(2,1)S(1)}, u32[]{:S(2)}, u32[]{:S(2)}) %collective-permute-start) | collective-permute-done | bytes 479264 | tf_op jit(solution)/shard_map/ppermute | solution.py:581
  62.5 9.7 %collective-permute-done.1.refs_2_ = bf16[144,1664]{1,0:T(8,128)(2,1)S(1)} collective-permute-done((bf16[144,1664]{1,0:T(8,128)(2,1)}, bf16[144,1664]{1,0:T(8,128)(2,1)S(1)}, u32[]{:S(2)}, u32[]{:S(2)}) %collective-permute-start.1) | collective-permute-done | bytes 479264 | tf_op jit(solution)/shard_map/ppermute | solution.py:581
  82.9 7.0 %project.1 = (bf16[2,256,1152]{2,1,0:T(8,128)(2,1)}, f32[2,256,1280]{2,1,0:T(8,128)}, bf16[2,256,1024]{2,1,0:T(8,128)(2,1)}, bf16[2,256,512]{2,1,0:T(8,128)(2,1)}, f32[8,1152]{1,0:T(8,128)}) custom-call(bf16[2,1,256,1152]{3,2,1,0:T(8,128)(2,1)} %refs_8_.3, bf16[1152,1664]{1,0:T(8,128)(2,1)} %untangle_in.1.w_ref.packed_ref.refs_7_, ...), custom_call_target="tpu_custom_call" | custom-call | bytes 1 | tf_op jit(solution)/shard_map/project/pallas_call | solution.py:43
  131.4 14.0 %collective-permute-done.20.refs_1_ = bf16[256,1152]{1,0:T(8,128)(2,1)S(1)} collective-permute-done((bf16[256,1152]{1,0:T(8,128)(2,1)}, bf16[256,1152]{1,0:T(8,128)(2,1)S(1)}, u32[]{:S(2)}, u32[]{:S(2)}) %collective-permute-start.20) | collective-permute-done | bytes 589856 | tf_op jit(solution)/shard_map/ppermute | solution.py:581
  147.6 23.7 %all-gather.6.cloned.1.call-done.refs_6_.refs_7_.refs_9_ = bf16[864,1152]{1,0:T(8,128)(2,1)} async-done(((bf16[216,1152]{1,0:T(8,128)(2,1)}), bf16[864,1152]{1,0:T(8,128)(2,1)}) %all-gather.6.cloned.1.call-update) | async-done | bytes 1990672 | tf_op jit(solution)/shard_map/all_gather | solution.py:720
  176.9 23.5 %ffn.2 = (bf16[1024,1152]{1,0:T(8,128)(2,1)}, bf16[1024,896]{1,0:T(8,128)(2,1)}, bf16[1024,896]{1,0:T(8,128)(2,1)}, bf16[1024,896]{1,0:T(8,128)(2,1)}, bf16[1024...) custom-call(bf16[256,1152]{1,0:T(8,128)(2,1)} %copy-done.18, ...), custom_call_target="tpu_custom_call" | custom-call | bytes 1 | tf_op jit(solution)/shard_map/ffn/pallas_call | solution.py:43
  205.6 23.3 %ffn.3 = (bf16[1024,1152]{1,0:T(8,128)(2,1)}, bf16[1024,896]{1,0:T(8,128)(2,1)}, bf16[1024,896]{1,0:T(8,128)(2,1)}, bf16[1024,896]{1,0:T(8,128)(2,1)}, bf16[1024...) custom-call(bf16[256,1152]{1,0:T(8,128)(2,1)} %copy-done.22, ...), custom_call_target="tpu_custom_call" | custom-call | bytes 1 | tf_op jit(solution)/shard_map/ffn/pallas_call | solution.py:43
  240.5 10.2 %ffn_back.4 = (bf16[1024,1152]{1,0:T(8,128)(2,1)}, bf16[1024,896]{1,0:T(8,128)(2,1)}, bf16[1024,896]{1,0:T(8,128)(2,1)}, bf16[1024,896]{1,0:T(8,128)(2,1)}, bf16...) custom-call(bf16[256,1152]{1,0:T(8,128)(2,1)} %get-tuple-element.294.refs_0_, ...), custom_call_target="tpu_custom_call" | custom-call | bytes 1 | tf_op jit(solution)/shard_map/ffn_back/pallas_call | solution.py:43
  251.3 7.7 %collective-permute-done.25.refs_2_ = bf16[256,1152]{1,0:T(8,128)(2,1)S(1)} collective-permute-done((bf16[256,1152]{1,0:T(8,128)(2,1)}, bf16[256,1152]{1,0:T(8,128)(2,1)S(1)}, u32[]{:S(2)}, u32[]{:S(2)}) %collective-permute-start.25) | collective-permute-done | bytes 589856 | tf_op jit(solution)/shard_map/ppermute | solution.py:581
  273.2 10.1 %ffn_back.5 = (bf16[1024,1152]{1,0:T(8,128)(2,1)}, bf16[1024,896]{1,0:T(8,128)(2,1)}, bf16[1024,896]{1,0:T(8,128)(2,1)}, bf16[1024,896]{1,0:T(8,128)(2,1)}, bf16...) custom-call(bf16[256,1152]{1,0:T(8,128)(2,1)} %get-tuple-element.304.refs_0_.refs_3_, ...), custom_call_target="tpu_custom_call" | custom-call | bytes 1 | tf_op jit(solution)/shard_map/ffn_back/pallas_call | solution.py:43
  285.5 21.1 %ffn_back.6 = (bf16[1024,1152]{1,0:T(8,128)(2,1)}, bf16[1024,896]{1,0:T(8,128)(2,1)}, bf16[1024,896]{1,0:T(8,128)(2,1)}, bf16[1024,896]{1,0:T(8,128)(2,1)}, bf16...) custom-call(bf16[256,1152]{1,0:T(8,128)(2,1)} %copy-done.31, ...), custom_call_target="tpu_custom_call", output_to_operand_aliasing={{0}: (11, {}), {1}: (12, {}), {2}: (13, {}), {3}: (14, {}),... | custom-call | bytes 1 | tf_op jit(solution)/shard_map/ffn_back/pallas_call | solution.py:43
  312.2 10.1 %terms.4 = bf16[864,1152]{1,0:T(8,128)(2,1)} custom-call(bf16[1024,896]{1,0:T(8,128)(2,1)} %get-tuple-element.324.refs_0_, bf16[1024,896]{1,0:T(8,128)(2,1)} %get-tuple-element.325.refs_1_, bf16[1024,1152]{1,0:T(8,128)(2,1)} %get-tuple-element.326.refs_2_, bf16[1024,1152]{1,0:T(8,128)(2,1)} %join.1.refs_3_), custom_call_target="tpu_custom_call" | custom-call | bytes 1 | tf_op jit(solution)/shard_map/terms/pallas_call | solution.py:43
  326.0 20.7 %ffn_back.7 = (bf16[1024,1152]{1,0:T(8,128)(2,1)}, bf16[1024,896]{1,0:T(8,128)(2,1)}, bf16[1024,896]{1,0:T(8,128)(2,1)}, bf16[1024,896]{1,0:T(8,128)(2,1)}, bf16...) custom-call(bf16[256,1152]{1,0:T(8,128)(2,1)} %copy-done.5, ...), custom_call_target="tpu_custom_call", output_to_operand_aliasing={{0}: (11, {}), {1}: (12, {}), {2}: (13, {}), {3}: (14, {}),... | custom-call | bytes 1 | tf_op jit(solution)/shard_map/ffn_back/pallas_call | solution.py:43
  348.0 10.5 %terms.5 = bf16[864,1152]{1,0:T(8,128)(2,1)} custom-call(bf16[1024,896]{1,0:T(8,128)(2,1)} %get-tuple-element.340.refs_0_, bf16[1024,896]{1,0:T(8,128)(2,1)} %get-tuple-element.341.refs_1_, bf16[1024,1152]{1,0:T(8,128)(2,1)} %get-tuple-element.326.refs_2_, bf16[1024,1152]{1,0:T(8,128)(2,1)} %join.1.refs_3_, bf16[864,1152]{1,0:T(8,128)(2,1)} %copy-done.8), custom_call_target="tpu_custom_call" | custom-call | bytes 1 | tf_op jit(solution)/shard_map/terms/pallas_call | solution.py:43
  358.5 15.7 %terms.6 = bf16[1152,1792]{1,0:T(8,128)(2,1)} custom-call(bf16[1024,1152]{1,0:T(8,128)(2,1)} %get-tuple-element.359.refs_0_, bf16[1024,1152]{1,0:T(8,128)(2,1)} %get-tuple-element.360.refs_1_, bf16[1024,896]{1,0:T(8,128)(2,1)} %get-tuple-element.348.refs_2_, bf16[1024,896]{1,0:T(8,128)(2,1)} %get-tuple-element.349.refs_3_, ...), custom_call_target="tpu_custom_call" | custom-call | bytes 1 | tf_op jit(solution)/shard_map/terms/pallas_call | solution.py:43
  378.0 11.5 %attend_back.2 = (f32[256,1152]{1,0:T(8,128)}, bf16[256,1152]{1,0:T(8,128)(2,1)}, bf16[256,1024]{1,0:T(8,128)(2,1)}, f32[1,1152]{1,0:T(1,128)}, f32[1,1152]{1,0:...) custom-call(s32[2]{0:T(128)} %pad_add_fusion.1.place, ...), custom_call_target="tpu_custom_call" | custom-call | bytes 1 | tf_op jit(solution)/shard_map/attend_back/pallas_call | solution.py:43
  392.1 16.3 %terms.7 = bf16[1152,1792]{1,0:T(8,128)(2,1)} custom-call(bf16[1024,1152]{1,0:T(8,128)(2,1)} %get-tuple-element.359.refs_0_, bf16[1024,1152]{1,0:T(8,128)(2,1)} %get-tuple-element.360.refs_1_, bf16[1024,896]{1,0:T(8,128)(2,1)} %get-tuple-element.361.refs_2_, bf16[1024,896]{1,0:T(8,128)(2,1)} %get-tuple-element.362.refs_3_, ...), custom_call_target="tpu_custom_call" | custom-call | bytes 1 | tf_op jit(solution)/shard_map/terms/pallas_call | solution.py:43
  413.4 11.2 %attend_back.3 = (f32[256,1152]{1,0:T(8,128)}, bf16[256,1152]{1,0:T(8,128)(2,1)}, bf16[256,1024]{1,0:T(8,128)(2,1)}, f32[1,1152]{1,0:T(1,128)}, f32[1,1152]{1,0:...) custom-call(s32[2]{0:T(128)} %pad_add_fusion.place, ...), custom_call_target="tpu_custom_call" | custom-call | bytes 1 | tf_op jit(solution)/shard_map/attend_back/pallas_call | solution.py:43
  428.4 6.3 %project_back.2 = (f32[2,1,256,1152]{3,2,1,0:T(8,128)}, bf16[256,1536]{1,0:T(8,128)(2,1)}, f32[1,1152]{1,0:T(1,128)}, f32[1,256]{1,0:T(1,128)}) custom-call(f32[256,512]{1,0:T(8,128)} %get-tuple-element.365.refs_0_, bf16[256,512]{1,0:T(8,128)(2,1)} %copy-done.49, bf16[256,512]{1,0:T(8,128)(2,1)} %copy-done.50, ...), custom_call_target="tpu_custom_call" | custom-call | bytes 1 | tf_op jit(solution)/shard_map/project_back/pallas_call | solution.py:43
  445.7 9.8 %weights.1 = (bf16[576,2816]{1,0:T(8,128)(2,1)}, bf16[576,2816]{1,0:T(8,128)(2,1)}) custom-call(s32[1]{0:T(128)} %bitcast.14.core, bf16[256,1024]{1,0:T(8,128)(2,1)} %get-tuple-element.391.refs_0_, bf16[256,1024]{1,0:T(8,128)(2,1)} %get-tuple-element.392.refs_1_, bf16[256,1152]{1,0:T(8,128)(2,1)} %get-tuple-element.358.refs_2_, ...), custom_call_target="tpu_custom_call" | custom-call | bytes 1 | tf_op jit(solution)/shard_map/weights/pallas_call | solution.py:43
  472.8 26.0 %reduce-scatter.5.cloned.1.call-done = bf16[288,1792]{1,0:T(8,128)(2,1)} async-done(((bf16[1152,1792]{1,0:T(8,128)(2,1)}), bf16[288,1792]{1,0:T(8,128)(2,1)}) %reduce-scatter.5.cloned.1.call-update) | async-done | bytes 1032208 | tf_op jit(solution)/shard_map/reduce_scatter | solution.py:1064
  501.1 7.2 %collective-permute-done.50.refs_2_ = bf16[144,2816]{1,0:T(8,128)(2,1)S(1)} collective-permute-done((bf16[144,2816]{1,0:T(8,128)(2,1)}, bf16[144,2816]{1,0:T(8,128)(2,1)S(1)}, u32[]{:S(2)}, u32[]{:S(2)}) %collective-permute-start.50) | collective-permute-done | bytes 811040 | tf_op jit(solution)/shard_map/ppermute | solution.py:581
  520.6 8.6 %all-to-all-done.1.in_ref = bf16[8,36,1792]{2,1,0:T(8,128)(2,1)S(1)} async-done(((bf16[8,36,1792]{2,1,0:T(8,128)(2,1)}), bf16[8,36,1792]{2,1,0:T(8,128)(2,1)S(1)}, u32[]{:S(2)}, u32[]{:S(2)}) %all-to-all-start.1) | async-done | bytes 1032224 | tf_op jit(solution)/shard_map/all_to_all | solution.py:1090
  (282 shorter events, 194.1 us)
Async XLA Ops:
  7.2 39.0 %all-gather.4.cloned.1.call-start = ((), (), s32[]{:S(2)}) async-start(), calls=%async_computation.4 | async-start | bytes 1484800 | tf_op jit(solution)/shard_map/all_gather | solution.py:706
  12.8 133.4 %all-gather.8.cloned.1.call-start = ((), (), s32[]{:S(2)}) async-start(), calls=%async_computation.6 | async-start | bytes 5160960 | tf_op jit(solution)/shard_map/all_gather | solution.py:716
  38.3 133.0 %all-gather.6.cloned.1.call-start = ((), (), s32[]{:S(2)}) async-start(), calls=%async_computation.5 | async-start | bytes 2488320 | tf_op jit(solution)/shard_map/all_gather | solution.py:720
  97.3 327.4 %reduce-scatter.7.cloned.1.call-start = ((), (), s32[]{:S(2)}) async-start(), calls=%async_computation.8 | async-start | bytes 2488320
  171.3 32.1 %collective-permute-start.16 = (bf16[256,1152]{1,0:T(8,128)(2,1)}, bf16[256,1152]{1,0:T(8,128)(2,1)S(1)}, u32[]{:S(2)}, u32[]{:S(2)}) collective-permute-start(bf16[256,1152]{1,0:T(8,128)(2,1)} %get-tuple-element.285.refs_3_), channel_id=1, source_target_pairs={{0,6},{1,7},{2,4},{3,5},{4,2},{5,3},{6,0},{7,1},{8,14},{9,15},{10,... | collective-permute-start | bytes 1769480 | tf_op jit(solution)/shard_map/ppermute | solution.py:581
  173.7 30.3 %collective-permute-start.17 = (bf16[256,1152]{1,0:T(8,128)(2,1)}, bf16[256,1152]{1,0:T(8,128)(2,1)S(1)}, u32[]{:S(2)}, u32[]{:S(2)}) collective-permute-start(bf16[256,1152]{1,0:T(8,128)(2,1)} %get-tuple-element.285.refs_3_), channel_id=1, source_target_pairs={{0,2},{1,3},{2,0},{3,1},{4,6},{5,7},{6,4},{7,5},{8,10},{9,11},{10,... | collective-permute-start | bytes 1769480 | tf_op jit(solution)/shard_map/ppermute | solution.py:581
  174.2 29.7 %collective-permute-start.18 = (bf16[256,1152]{1,0:T(8,128)(2,1)}, bf16[256,1152]{1,0:T(8,128)(2,1)S(1)}, u32[]{:S(2)}, u32[]{:S(2)}) collective-permute-start(bf16[256,1152]{1,0:T(8,128)(2,1)} %get-tuple-element.285.refs_3_), channel_id=1, source_target_pairs={{0,4},{1,5},{2,6},{3,7},{4,0},{5,1},{6,2},{7,3},{8,12},{9,13},{10,... | collective-permute-start | bytes 1769480 | tf_op jit(solution)/shard_map/ppermute | solution.py:581
  200.4 31.5 %collective-permute-start.27 = (bf16[256,1152]{1,0:T(8,128)(2,1)}, bf16[256,1152]{1,0:T(8,128)(2,1)S(1)}, u32[]{:S(2)}, u32[]{:S(2)}) collective-permute-start(bf16[256,1152]{1,0:T(8,128)(2,1)} %get-tuple-element.277), channel_id=1, source_target_pairs={{0,6},{1,7},{2,4},{3,5},{4,2},{5,3},{6,0},{7,1},{8,14},{9,15},{10,... | collective-permute-start | bytes 1769480 | tf_op jit(solution)/shard_map/ppermute | solution.py:581
  237.6 34.1 %collective-permute-start.33 = (bf16[256,1152]{1,0:T(8,128)(2,1)}, bf16[256,1152]{1,0:T(8,128)(2,1)S(1)}, u32[]{:S(2)}, u32[]{:S(2)}) collective-permute-start(bf16[256,1152]{1,0:T(8,128)(2,1)} %get-tuple-element.294.refs_0_), channel_id=1, source_target_pairs={{0,6},{1,7},{2,4},{3,5},{4,2},{5,3},{6,0},{7,1},{8,14},{9,15},{10,... | collective-permute-start | bytes 1769480 | tf_op jit(solution)/shard_map/ppermute | solution.py:581
  240.0 44.4 %collective-permute-start.34 = (bf16[256,1152]{1,0:T(8,128)(2,1)}, bf16[256,1152]{1,0:T(8,128)(2,1)S(1)}, u32[]{:S(2)}, u32[]{:S(2)}) collective-permute-start(bf16[256,1152]{1,0:T(8,128)(2,1)} %get-tuple-element.294.refs_0_), channel_id=1, source_target_pairs={{0,2},{1,3},{2,0},{3,1},{4,6},{5,7},{6,4},{7,5},{8,10},{9,11},{10,... | collective-permute-start | bytes 1769480 | tf_op jit(solution)/shard_map/ppermute | solution.py:581
  250.7 33.7 %collective-permute-start.35 = (bf16[256,1152]{1,0:T(8,128)(2,1)S(1)}, bf16[256,1152]{1,0:T(8,128)(2,1)S(1)}, u32[]{:S(2)}, u32[]{:S(2)}) collective-permute-start(bf16[256,1152]{1,0:T(8,128)(2,1)S(1)} %copy-done.19), channel_id=1, source_target_pairs={{0,4},{1,5},{2,6},{3,7},{4,0},{5,1},{6,2},{7,3},{8,12},{9,13},{10,... | collective-permute-start | bytes 1769480 | tf_op jit(solution)/shard_map/ppermute | solution.py:581
  264.2 42.4 %collective-permute-start.30 = (bf16[256,1152]{1,0:T(8,128)(2,1)}, bf16[256,1152]{1,0:T(8,128)(2,1)S(1)}, u32[]{:S(2)}, u32[]{:S(2)}) collective-permute-start(bf16[256,1152]{1,0:T(8,128)(2,1)} %get-tuple-element.304.refs_0_.refs_3_), channel_id=1, source_target_pairs={{0,6},{1,7},{2,4},{3,5},{4,2},{5,3},{6,0},{7,1},{8,14},{9,15},{10,... | collective-permute-start | bytes 1769480 | tf_op jit(solution)/shard_map/ppermute | solution.py:581
  266.4 41.6 %collective-permute-start.31 = (bf16[256,1152]{1,0:T(8,128)(2,1)}, bf16[256,1152]{1,0:T(8,128)(2,1)S(1)}, u32[]{:S(2)}, u32[]{:S(2)}) collective-permute-start(bf16[256,1152]{1,0:T(8,128)(2,1)} %get-tuple-element.304.refs_0_.refs_3_), channel_id=1, source_target_pairs={{0,2},{1,3},{2,0},{3,1},{4,6},{5,7},{6,4},{7,5},{8,10},{9,11},{10,... | collective-permute-start | bytes 1769480 | tf_op jit(solution)/shard_map/ppermute | solution.py:581
  271.7 36.2 %collective-permute-start.32 = (bf16[256,1152]{1,0:T(8,128)(2,1)}, bf16[256,1152]{1,0:T(8,128)(2,1)S(1)}, u32[]{:S(2)}, u32[]{:S(2)}) collective-permute-start(bf16[256,1152]{1,0:T(8,128)(2,1)} %get-tuple-element.304.refs_0_.refs_3_), channel_id=1, source_target_pairs={{0,4},{1,5},{2,6},{3,7},{4,0},{5,1},{6,2},{7,3},{8,12},{9,13},{10,... | collective-permute-start | bytes 1769480 | tf_op jit(solution)/shard_map/ppermute | solution.py:581
  322.4 36.1 %collective-permute-start.39 = (bf16[256,1152]{1,0:T(8,128)(2,1)S(1)}, bf16[256,1152]{1,0:T(8,128)(2,1)S(1)}, u32[]{:S(2)}, u32[]{:S(2)}) collective-permute-start(bf16[256,1152]{1,0:T(8,128)(2,1)S(1)} %copy-done.61), channel_id=1, source_target_pairs={{0,6},{1,7},{2,4},{3,5},{4,2},{5,3},{6,0},{7,1},{8,14},{9,15},{10,... | collective-permute-start | bytes 1769480 | tf_op jit(solution)/shard_map/ppermute | solution.py:581
  324.5 34.0 %collective-permute-start.40 = (bf16[256,1152]{1,0:T(8,128)(2,1)S(1)}, bf16[256,1152]{1,0:T(8,128)(2,1)S(1)}, u32[]{:S(2)}, u32[]{:S(2)}) collective-permute-start(bf16[256,1152]{1,0:T(8,128)(2,1)S(1)} %copy-done.60), channel_id=1, source_target_pairs={{0,2},{1,3},{2,0},{3,1},{4,6},{5,7},{6,4},{7,5},{8,10},{9,11},{10,... | collective-permute-start | bytes 1769480 | tf_op jit(solution)/shard_map/ppermute | solution.py:581
  325.1 33.4 %collective-permute-start.41 = (bf16[256,1152]{1,0:T(8,128)(2,1)S(1)}, bf16[256,1152]{1,0:T(8,128)(2,1)S(1)}, u32[]{:S(2)}, u32[]{:S(2)}) collective-permute-start(bf16[256,1152]{1,0:T(8,128)(2,1)S(1)} %copy-done.59), channel_id=1, source_target_pairs={{0,4},{1,5},{2,6},{3,7},{4,0},{5,1},{6,2},{7,3},{8,12},{9,13},{10,... | collective-permute-start | bytes 1769480 | tf_op jit(solution)/shard_map/ppermute | solution.py:581
  374.4 124.5 %reduce-scatter.5.cloned.1.call-start = ((), (), s32[]{:S(2)}) async-start(), calls=%async_computation.7 | async-start | bytes 5160960 | tf_op jit(solution)/shard_map/reduce_scatter | solution.py:1064
  374.4 37.7 %collective-permute-start.36 = (bf16[256,1152]{1,0:T(8,128)(2,1)}, bf16[256,1152]{1,0:T(8,128)(2,1)S(1)}, u32[]{:S(2)}, u32[]{:S(2)}) collective-permute-start(bf16[256,1152]{1,0:T(8,128)(2,1)} %get-tuple-element.333), channel_id=1, source_target_pairs={{0,6},{1,7},{2,4},{3,5},{4,2},{5,3},{6,0},{7,1},{8,14},{9,15},{10,... | collective-permute-start | bytes 1769480 | tf_op jit(solution)/shard_map/ppermute | solution.py:581
  376.5 35.6 %collective-permute-start.37 = (bf16[256,1152]{1,0:T(8,128)(2,1)S(1)}, bf16[256,1152]{1,0:T(8,128)(2,1)S(1)}, u32[]{:S(2)}, u32[]{:S(2)}) collective-permute-start(bf16[256,1152]{1,0:T(8,128)(2,1)S(1)} %copy-done.58), channel_id=1, source_target_pairs={{0,2},{1,3},{2,0},{3,1},{4,6},{5,7},{6,4},{7,5},{8,10},{9,11},{10,... | collective-permute-start | bytes 1769480 | tf_op jit(solution)/shard_map/ppermute | solution.py:581
  377.1 35.0 %collective-permute-start.38 = (bf16[256,1152]{1,0:T(8,128)(2,1)S(1)}, bf16[256,1152]{1,0:T(8,128)(2,1)S(1)}, u32[]{:S(2)}, u32[]{:S(2)}) collective-permute-start(bf16[256,1152]{1,0:T(8,128)(2,1)S(1)} %copy-done.57), channel_id=1, source_target_pairs={{0,4},{1,5},{2,6},{3,7},{4,0},{5,1},{6,2},{7,3},{8,12},{9,13},{10,... | collective-permute-start | bytes 1769480 | tf_op jit(solution)/shard_map/ppermute | solution.py:581
  469.3 31.7 %collective-permute-start.49 = (bf16[144,2816]{1,0:T(8,128)(2,1)}, bf16[144,2816]{1,0:T(8,128)(2,1)S(1)}, u32[]{:S(2)}, u32[]{:S(2)}) collective-permute-start(bf16[144,2816]{1,0:T(8,128)(2,1)} %get-tuple-element.411), channel_id=1, source_target_pairs={{0,2},{1,3},{2,0},{3,1},{4,6},{5,7},{6,4},{7,5},{8,10},{9,11},{10,... | collective-permute-start | bytes 2433032 | tf_op jit(solution)/shard_map/ppermute | solution.py:581
  470.9 37.4 %collective-permute-start.50 = (bf16[144,2816]{1,0:T(8,128)(2,1)}, bf16[144,2816]{1,0:T(8,128)(2,1)S(1)}, u32[]{:S(2)}, u32[]{:S(2)}) collective-permute-start(bf16[144,2816]{1,0:T(8,128)(2,1)} %get-tuple-element.412), channel_id=1, source_target_pairs={{0,4},{1,5},{2,6},{3,7},{4,0},{5,1},{6,2},{7,3},{8,12},{9,13},{10,... | collective-permute-start | bytes 2433032 | tf_op jit(solution)/shard_map/ppermute | solution.py:581
  470.9 37.4 %collective-permute-start.51 = (bf16[144,2816]{1,0:T(8,128)(2,1)}, bf16[144,2816]{1,0:T(8,128)(2,1)S(1)}, u32[]{:S(2)}, u32[]{:S(2)}) collective-permute-start(bf16[144,2816]{1,0:T(8,128)(2,1)} %get-tuple-element.413), channel_id=1, source_target_pairs={{0,6},{1,7},{2,4},{3,5},{4,2},{5,3},{6,0},{7,1},{8,14},{9,15},{10,... | collective-permute-start | bytes 2433032 | tf_op jit(solution)/shard_map/ppermute | solution.py:581
  (101 other events, 962.5 us)
Sparse Core Ops, SparseCore 0:
  12.9 33.2 all-gather.3
  48.4 78.7 all-gather.7
  128.8 42.4 all-gather.5
  374.5 40.4 reduce-scatter.6
  424.8 73.9 reduce-scatter.4
